TPU v7x, 32 devices: a whole 2x2x4 slice. The times are simulated.
32 devices in a mesh: row: 4 (over y, x), col: 8 (over z, core).
Axes of the slice: x: 2, y: 2, z: 4, core: 2. Of those that a mesh axis runs over, the one named last changes fastest.
Arguments:
- block_in: bfloat16 [8, 2048, 1024], P('col', 'row'), may hold values from -6 to 6
- cotangent: bfloat16 [8, 2048, 1024], P('col', 'row'), may hold values from -6 to 6
- seq_lengths: int32 [8, 12], P('col'), may hold values from 1 to 256, as said below
- seq_order: int32 [8, 12], P('col'), may hold values from 0 to 11, as said below
- expert_ids: int32 [8, 2048, 8], P('col'), may hold values from 0 to 31, as said below
- places: int32 [8, 2048, 8], P('col'), may hold values from 0 to 2047, as said below
- attn_gain: float32 [1024], replicated, may hold values from 0.5 to 1.5
- w_qkv: bfloat16 [1024, 2048], P('col', 'row'), may hold values from -0.59765625 to 0.59765625
- w_out: bfloat16 [1024, 1024], P('col', 'row'), may hold values from -1.796875 to 1.796875
- moe_gain: float32 [1024], replicated, may hold values from 0.5 to 1.5
- w_router: bfloat16 [1024, 32], P('col'), may hold values from -0.099609375 to 0.099609375
- w_gate: bfloat16 [1024, 32, 512], P('col', 'row'), may hold values from -0.1875 to 0.1875
- w_up: bfloat16 [1024, 32, 512], P('col', 'row'), may hold values from -0.1875 to 0.1875
- w_down: bfloat16 [1024, 32, 512], P('col', 'row'), may hold values from -3.59375 to 3.59375
Outputs:
- block_out: bfloat16 [8, 2048, 1024], P('col', 'row')
- input_grad: float32 [8, 2048, 1024], P('col', 'row')
- attn_gain_grad: float32 [1024], replicated
- qkv_grad: float32 [1024, 2048], P('col', 'row')
- out_grad: float32 [1024, 1024], P('col', 'row')
- moe_gain_grad: float32 [1024], replicated
- router_grad: float32 [1024, 32], P('col')
- gate_grad: float32 [1024, 32, 512], P('col', 'row')
- up_grad: float32 [1024, 32, 512], P('col', 'row')
- down_grad: float32 [1024, 32, 512], P('col', 'row')
Inputs may be any that keep to these rules, and one draw needn't show every extreme that they name: `seq_lengths`: the sequences of dealt slots r*3 to (r+1)*3 - 1 of a group add up to 512 tokens, and one of them has 256. `seq_order`: each row is a permutation of the group's 12 sequences. `expert_ids`: each token names 8 different experts; in each group one expert is named by every token. `places`: a pair's place is the number of earlier pairs of its group, tokens in dealt order and a token's 8 choices in order, that name the same expert.
All inputs are finite; a program needn't handle non-finite values.
Results may differ from a plain program's by a relative error of at most 0.012.
The roundings to bfloat16 on the way count: a program that leaves them out, or rounds other values in their place, can miss the bound.
Values may be sent and summed in bfloat16 or wider, within the bound.
A program may use at most 256 MiB of HBM per device.

v0:
```python
import jax
import jax.numpy as jnp
from jax import lax
from jax.sharding import PartitionSpec as P

HEAD_WIDTH = 64
QUERY_HEADS = 16
KEY_VALUE_HEADS = 8
EXPERT_COUNT = 32
TOPK = 8


EPSILON = 1e-06
RESIDUAL_SCALE = 0.22
SCORE_SCALE = 0.015625
ROPE_BASE = 10000.0
MASKED = -1e30


def norm_rows(values, gain_vec):
    scale_rows = lax.rsqrt(jnp.mean(values * values, axis=-1, keepdims=True) + EPSILON)
    return (values * scale_rows * gain_vec, scale_rows)


def norm_back(values, scale_rows, gain_vec, grad_rows):
    scaled = grad_rows * gain_vec
    inner_sum = jnp.mean(scaled * values, axis=-1, keepdims=True)
    cubed = scale_rows * scale_rows * scale_rows
    return (
        scale_rows * scaled - values * cubed * inner_sum,
        jnp.sum(grad_rows * values * scale_rows, axis=0),
    )


def dealt_tables(lengths, seq_perm, group_tokens):
    seq_ids = jnp.arange(lengths.shape[0], dtype=jnp.int32)
    picked = seq_perm[:, None] == seq_ids[None, :]
    dealt_len = jnp.sum(jnp.where(picked, lengths[None, :], 0), axis=1)
    before = seq_ids[None, :] < seq_perm[:, None]
    source_base = jnp.sum(jnp.where(before, lengths[None, :], 0), axis=1)
    seq_ends = jnp.cumsum(dealt_len)
    positions = jnp.arange(group_tokens, dtype=jnp.int32)
    past_end = positions[:, None] >= seq_ends[None, :]
    seq_starts = jnp.sum(jnp.where(past_end, dealt_len[None, :], 0), axis=1)
    slot_of = jnp.sum(past_end.astype(jnp.int32), axis=1)
    offset = positions - seq_starts
    source_rows = (
        jnp.sum(jnp.where(slot_of[:, None] == seq_ids[None, :], source_base[None, :], 0), axis=1)
        + offset
    )
    return (offset, seq_starts, source_rows, positions)


def angles(offset):
    frequency = ROPE_BASE ** (-jnp.arange(HEAD_WIDTH // 2, dtype=jnp.float32) * 2.0 / HEAD_WIDTH)
    turned = offset.astype(jnp.float32)[:, None] * frequency[None, :]
    return (jnp.cos(turned), jnp.sin(turned))


def rotate(values, cosine, sine_table):
    half_size = values.shape[-1] // 2
    first_half = values[..., :half_size]
    second_half = values[..., half_size:]
    return jnp.concatenate(
        [
            first_half * cosine - second_half * sine_table,
            second_half * cosine + first_half * sine_table,
        ],
        axis=-1,
    )


def rotate_back(grad_vals, cosine, sine_table):
    half_size = grad_vals.shape[-1] // 2
    first_half = grad_vals[..., :half_size]
    second_half = grad_vals[..., half_size:]
    return jnp.concatenate(
        [
            first_half * cosine + second_half * sine_table,
            second_half * cosine - first_half * sine_table,
        ],
        axis=-1,
    )


def body(
    block_in,
    cotangent,
    seq_lengths,
    seq_order,
    expert_ids,
    places,
    attn_gain,
    w_qkv,
    w_out,
    moe_gain,
    w_router,
    w_gate,
    w_up,
    w_down,
):
    device_tokens = block_in.shape[1]
    model_width = block_in.shape[2]
    row_count = lax.axis_size("row")
    tok_grp = device_tokens * row_count
    row_rank = lax.axis_index("row")
    row_base = row_rank * device_tokens
    head_repeat_count = QUERY_HEADS // KEY_VALUE_HEADS
    exp_dev = w_gate.shape[1]
    capacity = tok_grp * TOPK // EXPERT_COUNT
    block_rows = min(512, device_tokens)
    block_total_count = device_tokens // block_rows
    given_in, given_grad = (
        lax.all_gather(block_in[0], "row", axis=0, tiled=True),
        lax.all_gather(cotangent[0], "row", axis=0, tiled=True),
    )
    offset, seq_starts, source_rows, positions = dealt_tables(seq_lengths[0], seq_order[0], tok_grp)
    own_source = lax.dynamic_slice_in_dim(source_rows, row_base, device_tokens, 0)
    own_rows = given_in[own_source].astype(jnp.float32)
    dealt_grad = given_grad[source_rows]
    grad_out = lax.dynamic_slice_in_dim(dealt_grad, row_base, device_tokens, 0).astype(jnp.float32)
    attn_normed, attn_scale = norm_rows(own_rows, attn_gain)
    attn_rows = attn_normed.astype(jnp.bfloat16)
    qkv_cols, out_cols = (
        lax.all_gather(w_qkv, "col", axis=0, tiled=True),
        lax.all_gather(w_out, "col", axis=0, tiled=True),
    )
    qkv_full, out_full = (
        lax.all_gather(qkv_cols, "row", axis=1, tiled=True),
        lax.all_gather(out_cols, "row", axis=1, tiled=True),
    )
    own_offset = lax.dynamic_slice_in_dim(offset, row_base, device_tokens, 0)
    own_starts = lax.dynamic_slice_in_dim(seq_starts, row_base, device_tokens, 0) - row_base
    local_pos = jnp.arange(device_tokens, dtype=jnp.int32)
    cosine, sine_table = angles(own_offset)
    cos_four = cosine[:, None, None, :]
    sin_four = sine_table[:, None, None, :]
    cos_three = cosine[:, None, :]
    sin_three = sine_table[:, None, :]
    projected_rows = jnp.dot(attn_rows, qkv_full, preferred_element_type=jnp.float32).reshape(
        device_tokens, KEY_VALUE_HEADS, head_repeat_count + 2, HEAD_WIDTH
    )
    query_rows = rotate(projected_rows[:, :, :head_repeat_count], cos_four, sin_four).astype(
        jnp.bfloat16
    )
    head_keys = rotate(projected_rows[:, :, head_repeat_count], cos_three, sin_three).astype(
        jnp.bfloat16
    )
    head_values = projected_rows[:, :, head_repeat_count + 1].astype(jnp.bfloat16)

    def block_scores():
        raw_scores = (
            jnp.einsum("qgjd,kgd->gjqk", query_rows, head_keys, preferred_element_type=jnp.float32)
            * SCORE_SCALE
        )
        allowed = (local_pos[None, :] <= local_pos[:, None]) & (
            local_pos[None, :] >= own_starts[:, None]
        )
        return (query_rows, jnp.where(allowed, raw_scores, MASKED))

    def attend(block_start):
        query_block, attention_logits = block_scores()
        row_max = jnp.max(attention_logits, axis=-1, keepdims=True)
        exponent = jnp.exp(attention_logits - row_max)
        row_total = jnp.sum(exponent, axis=-1, keepdims=True)
        prob_rows = (exponent / row_total).astype(jnp.bfloat16)
        mixed_block = jnp.einsum(
            "gjqk,kgd->qgjd", prob_rows, head_values, preferred_element_type=jnp.float32
        )
        return (
            mixed_block.astype(jnp.bfloat16).reshape(block_rows, -1),
            (row_max + jnp.log(row_total))[..., 0],
        )

    block_starts = jnp.arange(block_total_count, dtype=jnp.int32) * block_rows
    mixed_blocks, logsum_blocks = lax.map(attend, block_starts)
    blended_rows = mixed_blocks.reshape(device_tokens, -1)
    attn_out = lax.dot_general(
        blended_rows, out_full, (((1,), (1,)), ((), ())), preferred_element_type=jnp.float32
    )
    middle = own_rows + RESIDUAL_SCALE * attn_out
    moe_normed, moe_scale = norm_rows(middle, moe_gain)
    moe_rows = lax.all_gather(moe_normed.astype(jnp.bfloat16), "row", axis=0, tiled=True)
    gate_full, up_full, down_full, router_full = (
        lax.all_gather(w_gate, "col", axis=0, tiled=True),
        lax.all_gather(w_up, "col", axis=0, tiled=True),
        lax.all_gather(w_down, "col", axis=0, tiled=True),
        lax.all_gather(w_router, "col", axis=0, tiled=True),
    )
    chosen_ids = expert_ids[0]
    pair_places = places[0]
    logits = jnp.dot(moe_rows, router_full, preferred_element_type=jnp.float32)
    chosen = jnp.take_along_axis(logits, chosen_ids, axis=1)
    pair_gates = jax.nn.softmax(chosen, axis=-1)
    local_ids = chosen_ids - row_rank * exp_dev
    is_mine = (local_ids >= 0) & (local_ids < exp_dev) & (pair_places < capacity)
    slot_index = jnp.where(is_mine, local_ids * capacity + pair_places, exp_dev * capacity).reshape(
        -1
    )
    pair_token = (positions[:, None] + jnp.zeros_like(chosen_ids)).reshape(-1)
    slot_token = (
        jnp.full((exp_dev * capacity,), tok_grp, jnp.int32)
        .at[slot_index]
        .set(pair_token, mode="drop")
    )
    slot_pair = (
        jnp.full((exp_dev * capacity,), tok_grp * TOPK, jnp.int32)
        .at[slot_index]
        .set(jnp.arange(tok_grp * TOPK, dtype=jnp.int32), mode="drop")
    )
    padded_rows = jnp.concatenate([moe_rows, jnp.zeros((1, model_width), jnp.bfloat16)], axis=0)
    routed = padded_rows[slot_token].reshape(exp_dev, capacity, model_width)
    gate_in = jnp.einsum("ecd,def->ecf", routed, gate_full, preferred_element_type=jnp.float32)
    up_in = jnp.einsum("ecd,def->ecf", routed, up_full, preferred_element_type=jnp.float32)
    sigmoid_gate = jax.nn.sigmoid(gate_in)
    silu_gate = gate_in * sigmoid_gate
    hidden = (silu_gate * up_in).astype(jnp.bfloat16)
    expert_out = jnp.einsum(
        "ecf,def->ecd", hidden, down_full, preferred_element_type=jnp.float32
    ).reshape(exp_dev * capacity, model_width)
    slot_gate = jnp.concatenate([pair_gates.reshape(-1), jnp.zeros((1,), jnp.float32)], axis=0)[
        slot_pair
    ]
    partial_sum = (
        jnp.zeros((tok_grp + 1, model_width), jnp.float32)
        .at[slot_token]
        .add(slot_gate[:, None] * expert_out)[:tok_grp]
    )
    expert_sum = lax.psum_scatter(
        partial_sum.astype(jnp.bfloat16), "row", scatter_dimension=0, tiled=True
    ).astype(jnp.float32)
    block_dealt = (middle + RESIDUAL_SCALE * expert_sum).astype(jnp.bfloat16)
    sum_grad = (RESIDUAL_SCALE * dealt_grad.astype(jnp.float32)).astype(jnp.bfloat16)
    padded_grad = jnp.concatenate([sum_grad, jnp.zeros((1, model_width), jnp.bfloat16)], axis=0)
    slot_grad = padded_grad[slot_token].astype(jnp.float32)
    slot_inner = jnp.sum(slot_grad * expert_out, axis=1)
    pair_grad = (
        jnp.zeros((tok_grp * TOPK + 1,), jnp.float32)
        .at[slot_pair]
        .add(slot_inner)[: tok_grp * TOPK]
        .reshape(tok_grp, TOPK)
    )
    gates_grad = lax.psum(pair_grad, "row")
    chosen_grad = pair_gates * (
        gates_grad - jnp.sum(pair_gates * gates_grad, axis=1, keepdims=True)
    )
    expert_columns = jnp.arange(EXPERT_COUNT, dtype=jnp.int32)
    logits_grad = jnp.sum(
        chosen_grad[:, :, None] * (chosen_ids[:, :, None] == expert_columns).astype(jnp.float32),
        axis=1,
    ).astype(jnp.bfloat16)
    out_slot = (
        (slot_gate[:, None] * slot_grad)
        .astype(jnp.bfloat16)
        .reshape(exp_dev, capacity, model_width)
    )
    hidden_grad = jnp.einsum(
        "ecd,def->ecf", out_slot, down_full, preferred_element_type=jnp.float32
    )
    down_wgrad = jnp.einsum("ecf,ecd->def", hidden, out_slot, preferred_element_type=jnp.float32)
    gate_in_grad = (
        hidden_grad * up_in * sigmoid_gate * (1.0 + gate_in * (1.0 - sigmoid_gate))
    ).astype(jnp.bfloat16)
    up_in_grad = (hidden_grad * silu_gate).astype(jnp.bfloat16)
    gate_wgrad = jnp.einsum(
        "ecd,ecf->def", routed, gate_in_grad, preferred_element_type=jnp.float32
    )
    up_wgrad = jnp.einsum("ecd,ecf->def", routed, up_in_grad, preferred_element_type=jnp.float32)
    routed_grad = jnp.einsum(
        "ecf,def->ecd", gate_in_grad, gate_full, preferred_element_type=jnp.float32
    )
    routed_grad = routed_grad + jnp.einsum(
        "ecf,def->ecd", up_in_grad, up_full, preferred_element_type=jnp.float32
    )
    partial_rows = (
        jnp.zeros((tok_grp + 1, model_width), jnp.float32)
        .at[slot_token]
        .add(routed_grad.reshape(exp_dev * capacity, model_width))[:tok_grp]
    )
    moe_rows_grad = lax.psum_scatter(partial_rows, "row", scatter_dimension=0, tiled=True)
    own_logits_grad = lax.dynamic_slice_in_dim(logits_grad, row_base, device_tokens, 0)
    moe_rows_grad = moe_rows_grad + lax.dot_general(
        own_logits_grad, router_full, (((1,), (1,)), ((), ())), preferred_element_type=jnp.float32
    )
    router_wgrad = lax.dot_general(
        moe_rows, logits_grad, (((0,), (0,)), ((), ())), preferred_element_type=jnp.float32
    )
    middle_norm_grad, moe_gain_grad = norm_back(middle, moe_scale, moe_gain, moe_rows_grad)
    middle_grad = grad_out + middle_norm_grad
    attn_grad = (RESIDUAL_SCALE * middle_grad).astype(jnp.bfloat16)
    blended_gradient = jnp.dot(attn_grad, out_full, preferred_element_type=jnp.float32).astype(
        jnp.bfloat16
    )
    out_wgrad = lax.dot_general(
        attn_grad, blended_rows, (((0,), (0,)), ((), ())), preferred_element_type=jnp.float32
    )
    blended_gradient_heads = blended_gradient.reshape(
        device_tokens, KEY_VALUE_HEADS, head_repeat_count, HEAD_WIDTH
    )

    def attend_back(running, inputs):
        key_grad, value_grad = running
        block_start, logsum = inputs
        query_block, attention_logits = block_scores()
        prob_rows = jnp.exp(attention_logits - logsum[..., None])
        probs_low = prob_rows.astype(jnp.bfloat16)
        probs_grad = jnp.einsum(
            "qgjd,kgd->gjqk",
            blended_gradient_heads,
            head_values,
            preferred_element_type=jnp.float32,
        )
        inner_sum = jnp.sum(prob_rows * probs_grad, axis=-1, keepdims=True)
        scores_grad = (prob_rows * (probs_grad - inner_sum) * SCORE_SCALE).astype(jnp.bfloat16)
        gradient_query = jnp.einsum(
            "gjqk,kgd->qgjd", scores_grad, head_keys, preferred_element_type=jnp.float32
        )
        key_grad = key_grad + jnp.einsum(
            "gjqk,qgjd->kgd", scores_grad, query_block, preferred_element_type=jnp.float32
        )
        value_grad = value_grad + jnp.einsum(
            "gjqk,qgjd->kgd", probs_low, blended_gradient_heads, preferred_element_type=jnp.float32
        )
        return ((key_grad, value_grad), gradient_query)

    empty_head_rows = jnp.zeros((device_tokens, KEY_VALUE_HEADS, HEAD_WIDTH), jnp.float32)
    (key_grad, value_grad), blocks_of_query = lax.scan(
        attend_back, (empty_head_rows, empty_head_rows), (block_starts, logsum_blocks)
    )
    gradient_query = blocks_of_query.reshape(
        device_tokens, KEY_VALUE_HEADS, head_repeat_count, HEAD_WIDTH
    )
    qkv_grad_rows = (
        jnp.concatenate(
            [
                rotate_back(gradient_query, cos_four, sin_four),
                rotate_back(key_grad, cos_three, sin_three)[:, :, None],
                value_grad[:, :, None],
            ],
            axis=2,
        )
        .astype(jnp.bfloat16)
        .reshape(device_tokens, -1)
    )
    qkv_wgrad = lax.dot_general(
        attn_rows, qkv_grad_rows, (((0,), (0,)), ((), ())), preferred_element_type=jnp.float32
    )
    attn_rows_grad = lax.dot_general(
        qkv_grad_rows, qkv_full, (((1,), (1,)), ((), ())), preferred_element_type=jnp.float32
    )
    input_norm_grad, attn_gain_grad = norm_back(own_rows, attn_scale, attn_gain, attn_rows_grad)
    input_dealt = middle_grad + input_norm_grad
    qkv_part, out_part = (qkv_wgrad, out_wgrad)
    qkv_summed, out_summed, router_grad, gate_grad, up_grad, down_grad = (
        lax.psum_scatter(qkv_part, "col", scatter_dimension=0, tiled=True),
        lax.psum_scatter(out_part, "col", scatter_dimension=0, tiled=True),
        lax.psum_scatter(router_wgrad, "col", scatter_dimension=0, tiled=True),
        lax.psum_scatter(gate_wgrad, "col", scatter_dimension=0, tiled=True),
        lax.psum_scatter(up_wgrad, "col", scatter_dimension=0, tiled=True),
        lax.psum_scatter(down_wgrad, "col", scatter_dimension=0, tiled=True),
    )
    qkv_grad, out_grad = (
        lax.psum_scatter(qkv_summed, "row", scatter_dimension=1, tiled=True),
        lax.psum_scatter(out_summed, "row", scatter_dimension=1, tiled=True),
    )
    attn_gain_total, moe_gain_total = lax.psum((attn_gain_grad, moe_gain_grad), ("row", "col"))
    dealt_out, dealt_igrad = (
        lax.all_gather(block_dealt.astype(jnp.float32), "row", axis=0, tiled=True),
        lax.all_gather(input_dealt, "row", axis=0, tiled=True),
    )
    inverse = jnp.zeros((tok_grp,), jnp.int32).at[source_rows].set(positions)
    own_inverse = lax.dynamic_slice_in_dim(inverse, row_base, device_tokens, 0)
    block_out = dealt_out[own_inverse].astype(jnp.bfloat16)[None]
    input_grad = dealt_igrad[own_inverse][None]
    return (
        block_out,
        input_grad,
        attn_gain_total,
        qkv_grad,
        out_grad,
        moe_gain_total,
        router_grad,
        gate_grad,
        up_grad,
        down_grad,
    )


def solution(mesh):
    placed = (
        P("col", "row", None),
        P("col", "row", None),
        P("col", None),
        P("col", None),
        P("col", None, None),
        P("col", None, None),
        P(),
        P("col", "row"),
        P("col", "row"),
        P(),
        P("col", None),
        P("col", "row", None),
        P("col", "row", None),
        P("col", "row", None),
    )
    return jax.shard_map(
        body,
        mesh=mesh,
        in_specs=placed,
        out_specs=(
            P("col", "row", None),
            P("col", "row", None),
            P(),
            P("col", "row"),
            P("col", "row"),
            P(),
            P("col", None),
            P("col", "row", None),
            P("col", "row", None),
            P("col", "row", None),
        ),
        check_vma=False,
    )
```

profile of v0, /device:TPU:9, one launch (start us, length us, event | category | flops | bytes accessed | tf_op | source)
XLA Modules:
  0.0 1805.8 jit_solution(7181218536659667048)
XLA Ops:
  8.7 24.8 %all-gather.14.cloned.1.call-done = bf16[1024,512]{1,0:T(8,128)(2,1)} async-done(((bf16[128,512]{1,0:T(8,128)(2,1)}), bf16[1024,512]{1,0:T(8,128)(2,1)}) %all-gather.14.cloned.1.call-update) | async-done | bytes 1048592 | tf_op jit(solution)/shard_map/all_gather | solution.py:125
  50.0 37.1 %all-gather.32.cloned.1.call-done = bf16[1,2048,1024]{2,1,0:T(8,128)(2,1)} async-done(((bf16[1,512,1024]{2,1,0:T(8,128)(2,1)}), bf16[1,2048,1024]{2,1,0:T(8,128)(2,1)}) %all-gather.32.cloned.1.call-update) | async-done | bytes 4194320 | tf_op jit(solution)/shard_map/all_gather | solution.py:114
  93.5 48.0 %all-gather.16.cloned.1.call-done = bf16[1024,2048]{1,0:T(8,128)(2,1)} async-done(((bf16[1024,512]{1,0:T(8,128)(2,1)}), bf16[1024,2048]{1,0:T(8,128)(2,1)}) %all-gather.16.cloned.1.call-update) | async-done | bytes 4194320 | tf_op jit(solution)/shard_map/all_gather | solution.py:129
  192.1 60.3 %scatter_custom_fusion = s32[4096]{0:T(1024)S(1)} fusion(s32[16384]{0:T(1024)S(1)} %bitcast.174, s32[16384]{0:T(1024)S(1)} %reshape.474, s32[]{:T(128)} %constant.35.clone.1), kind=kCustom, calls=%fused_computation.143 | custom fusion | bytes 16388 | tf_op jit(solution)/shard_map/scatter | solution.py:204
  252.5 60.5 %scatter_custom_fusion.1 = s32[4096]{0:T(1024)S(1)} fusion(s32[16384]{0:T(1024)S(1)} %bitcast.175, s32[16384]{0:T(1024)S(1)} %iota.38, s32[]{:T(128)} %constant.61.clone.1), kind=kCustom, calls=%fused_computation.141 | custom fusion | bytes 16388 | tf_op jit(solution)/shard_map/scatter | solution.py:209
  347.4 23.7 %gather_fusion.5 = bf16[4096,1024]{1,0:T(8,128)(2,1)} fusion(bf16[2049,1024]{1,0:T(8,128)(2,1)} %concatenate.33, s32[4096]{0:T(1024)S(1)} %get-tuple-element.134), kind=kCustom, calls=%fused_computation.5 | custom fusion | bytes 16793600 | tf_op jit(solution)/shard_map/gather | solution.py:235
  374.6 130.6 %gather_fusion.7 = f32[16384]{0:T(1024)S(1)} fusion(f32[2048,32]{0,1:T(8,128)S(1)} %fusion.81, s32[16384]{0:T(1024)S(1)} %reshape.464), kind=kCustom, calls=%fused_computation.7 | custom fusion | bytes 262144 | tf_op jit(solution)/shard_map/jit(take_along_axis)/gather | solution.py:193
  509.2 23.0 %gather_fusion.1 = f32[4096]{0:T(1024)S(1)} fusion(f32[16385]{0:T(1024)S(1)} %pad_maximum_fusion.4, s32[4096]{0:T(1024)S(1)} %copy-done.40), kind=kCustom, calls=%fused_computation.1 | custom fusion | bytes 49152 | tf_op jit(solution)/shard_map/gather | solution.py:221
  536.8 24.0 %gather_fusion.2 = bf16[4096,1024]{1,0:T(8,128)(2,1)} fusion(bf16[2049,1024]{1,0:T(8,128)(2,1)} %concatenate.32, s32[4096]{0:T(1024)S(1)} %copy-done.32), kind=kCustom, calls=%fused_computation.2 | custom fusion | bytes 16793600 | tf_op jit(solution)/shard_map/gather | solution.py:212
  587.9 17.7 multiply_convert_fusion
  605.6 17.3 fusion.2
  622.9 28.6 %scatter_custom_fusion.5 = f32[16385]{0:T(1024)S(1)} fusion(s32[4096]{0:T(1024)} %get-tuple-element.132, f32[4096]{0:T(1024)S(1)} %bitcast.180, f32[]{:T(128)} %constant.36.clone.1), kind=kCustom, calls=%fused_computation.135 | custom fusion | flops 4096 | bytes 66052 | tf_op jit(solution)/shard_map/scatter-add | solution.py:240
  653.1 14.9 fusion.84
  668.0 16.0 convolution_add_fusion
  684.0 40.1 %scatter_custom_fusion.4 = f32[2049,1024]{1,0:T(8,128)} fusion(s32[4096]{0:T(1024)} %get-tuple-element.135, f32[4096,1024]{1,0:T(8,128)} %bitcast.153, f32[]{:T(128)} %constant.36.clone.1), kind=kCustom, calls=%fused_computation.55 | custom fusion | flops 4194304 | bytes 8393216 | tf_op jit(solution)/shard_map/scatter-add | solution.py:278
  744.0 40.4 %scatter_custom_fusion.2 = f32[2049,1024]{1,0:T(8,128)} fusion(s32[4096]{0:T(1024)} %get-tuple-element.135, f32[4096,1024]{1,0:T(8,128)} %bitcast_multiply_fusion.1, f32[]{:T(128)} %constant.36.clone.1), kind=kCustom, calls=%fused_computation.57 | custom fusion | flops 4194304 | bytes 8393216 | tf_op jit(solution)/shard_map/scatter-add | solution.py:227
  792.9 25.7 %reduce-scatter.13.cloned.1.call-done = f32[512,1024]{1,0:T(8,128)} async-done(((f32[2048,1024]{1,0:T(8,128)}), f32[512,1024]{1,0:T(8,128)}) %reduce-scatter.13.cloned.1.call-update) | async-done | bytes 2097168 | tf_op jit(solution)/shard_map/reduce_scatter | solution.py:280
  822.2 52.0 %reduce-scatter.11.cloned.1.call-done = bf16[512,1024]{1,0:T(8,128)(2,1)} async-done(((bf16[2048,1024]{1,0:T(8,128)(2,1)}), bf16[512,1024]{1,0:T(8,128)(2,1)}) %reduce-scatter.11.cloned.1.call-update) | async-done | bytes 1048592 | tf_op jit(solution)/shard_map/reduce_scatter | solution.py:229
  897.7 24.7 %fusion.34 = f32[512,8,64]{0,2,1:T(8,128)} fusion(f32[8,512,512,2]{2,1,3,0:T(8,128)} %fusion.52, f32[8,2,512,512]{2,3,1,0:T(8,128)} %get-tuple-element.145, f32[8,2,512]{2,1,0:T(2,128)S(1)} %bitcast.170, bf16[512,8,2,32]{0,3,2,1:T(8,128)(2,1)} %copy-done.25, bf16[512,8,2,32]{0,3,2,1:T(8,128)(2,1)} %copy-done.24), kind=kOutput, calls=%fused_computation.82 | convolution fusion | flops 568336896 | bytes 35684352 | tf_op jit(solution)/shard_map/while/body/eval_jaxpr/gjqk,qgjd->kgd/dot_general | solution.py:318
  924.6 24.1 %fusion.32 = f32[512,8,2,64]{0,3,2,1:T(8,128)} fusion(f32[8,512,512,2]{2,1,3,0:T(8,128)} %fusion.52, f32[8,2,512,512]{2,3,1,0:T(8,128)} %get-tuple-element.145, f32[8,2,512]{2,1,0:T(2,128)S(1)} %bitcast.171, bf16[512,8,32]{0,2,1:T(8,128)(2,1)} %copy-done.28, bf16[512,8,32]{0,2,1:T(8,128)(2,1)} %copy-done.27), kind=kOutput, calls=%fused_computation.78 | convolution fusion | flops 567288320 | bytes 36208640 | tf_op jit(solution)/shard_map/while/body/eval_jaxpr/gjqk,kgd->qgjd/dot_general | solution.py:315
  975.4 15.0 convolution_bitcast_fusion
  990.9 15.0 convolution_bitcast_fusion.1
  1006.0 15.0 convolution_bitcast_fusion.2
  1025.6 29.1 %reduce-scatter.15.cloned.1.call-done = f32[128,2048]{1,0:T(8,128)} async-done(((f32[1024,2048]{1,0:T(8,128)}), f32[128,2048]{1,0:T(8,128)}) %reduce-scatter.15.cloned.1.call-update) | async-done | bytes 1048592 | tf_op jit(solution)/shard_map/reduce_scatter | solution.py:355
  1063.0 41.8 %all-reduce.2 = (f32[1024]{0:T(1024)}, f32[1024]{0:T(1024)}) all-reduce(f32[1024]{0:T(1024)S(1)} %get-tuple-element.109, f32[1024]{0:T(1024)S(1)} %get-tuple-element.107), channel_id=1, replica_groups=mesh['row'=4,'col'=8] {'row','col'}, use_global_device_ids=true, to_apply=%region_28.29 | all-reduce | flops 2048 | bytes 16384 | tf_op jit(solution)/shard_map/psum | solution.py:366
  1117.2 83.9 %all-gather.30.cloned.1.call-done = f32[2048,1024]{1,0:T(8,128)} async-done(((f32[512,1024]{1,0:T(8,128)}), f32[2048,1024]{1,0:T(8,128)}) %all-gather.30.cloned.1.call-update) | async-done | bytes 8388624 | tf_op jit(solution)/shard_map/all_gather | solution.py:369
  1208.0 162.1 %reduce-scatter.29.cloned.1.call-done = f32[128,8,512]{2,0,1:T(8,128)} async-done(((f32[1024,8,512]{2,0,1:T(8,128)}), f32[128,8,512]{2,0,1:T(8,128)}) %reduce-scatter.29.cloned.1.call-update) | async-done | bytes 2097168 | tf_op jit(solution)/shard_map/reduce_scatter | solution.py:360
  1374.2 164.9 %reduce-scatter.27.cloned.1.call-done = f32[128,8,512]{0,2,1:T(8,128)} async-done(((f32[1024,8,512]{0,2,1:T(8,128)}), f32[128,8,512]{0,2,1:T(8,128)}) %reduce-scatter.27.cloned.1.call-update) | async-done | bytes 2097168 | tf_op jit(solution)/shard_map/reduce_scatter | solution.py:359
  1542.1 166.1 %reduce-scatter.25.cloned.1.call-done = f32[128,8,512]{0,2,1:T(8,128)} async-done(((f32[1024,8,512]{0,2,1:T(8,128)}), f32[128,8,512]{0,2,1:T(8,128)}) %reduce-scatter.25.cloned.1.call-update) | async-done | bytes 2097168 | tf_op jit(solution)/shard_map/reduce_scatter | solution.py:358
  1711.3 23.1 %reduce-scatter.23.cloned.1.call-done = f32[128,32]{0,1:T(8,128)} async-done(((f32[1024,32]{0,1:T(8,128)}), f32[128,32]{0,1:T(8,128)}) %reduce-scatter.23.cloned.1.call-update) | async-done | bytes 16400 | tf_op jit(solution)/shard_map/reduce_scatter | solution.py:357
  1734.4 32.8 %reduce-scatter.21.cloned.1.call-done = f32[128,256]{1,0:T(8,128)} async-done(((f32[128,1024]{1,0:T(8,128)}), f32[128,256]{1,0:T(8,128)}) %reduce-scatter.21.cloned.1.call-update) | async-done | bytes 131088 | tf_op jit(solution)/shard_map/reduce_scatter | solution.py:364
  1767.2 31.6 %reduce-scatter.17.cloned.1.call-done = f32[128,512]{1,0:T(8,128)} async-done(((f32[128,2048]{1,0:T(8,128)}), f32[128,512]{1,0:T(8,128)}) %reduce-scatter.17.cloned.1.call-update) | async-done | bytes 262160 | tf_op jit(solution)/shard_map/reduce_scatter | solution.py:363
  (262 shorter events, 276.5 us)
Async XLA Ops:
  7.2 41.6 %copy-start.54 = (s32[1,12]{1,0:T(1,128)S(1)}, s32[1,12]{1,0:T(1,128)}, u32[]{:S(2)}) copy-start(s32[1,12]{1,0:T(1,128)} %param.17) | copy-start | bytes 148
  7.2 26.4 %all-gather.14.cloned.1.call-start = ((), (), s32[]{:S(2)}) async-start(), calls=%async_computation.10 | async-start | bytes 1179648 | tf_op jit(solution)/shard_map/all_gather | solution.py:125
  7.9 79.2 %all-gather.32.cloned.1.call-start = ((), (), s32[]{:S(2)}) async-start(), calls=%async_computation.30 | async-start | bytes 5242880 | tf_op jit(solution)/shard_map/all_gather | solution.py:114
  8.7 132.9 %all-gather.16.cloned.1.call-start = ((), (), s32[]{:S(2)}) async-start(), calls=%async_computation.11 | async-start | bytes 5242880 | tf_op jit(solution)/shard_map/all_gather | solution.py:129
  33.6 144.9 %all-gather.18.cloned.1.call-start = ((), (), s32[]{:S(2)}) async-start(), calls=%async_computation.12 | async-start | bytes 2621440 | tf_op jit(solution)/shard_map/all_gather | solution.py:130
  48.1 279.7 %all-gather.34.cloned.1.call-start = ((), (), s32[]{:S(2)}) async-start(), calls=%async_computation.31 | async-start | bytes 5242880 | tf_op jit(solution)/shard_map/all_gather | solution.py:115
  48.7 322.4 %all-gather.20.cloned.1.call-start = ((), (), s32[]{:S(2)}) async-start(), calls=%async_computation.13 | async-start | bytes 5242880 | tf_op jit(solution)/shard_map/all_gather | solution.py:183
  50.0 96.6 %copy-start.11 = (f32[512,32]{0,1:T(8,128)}, f32[512,32]{0,1:T(8,128)S(1)}, u32[]{:S(2)}) copy-start(f32[512,32]{0,1:T(8,128)S(1)} %get-tuple-element.138) | copy-start | bytes 196612
  50.0 96.6 %copy-start.13 = (f32[512,32]{0,1:T(8,128)}, f32[512,32]{0,1:T(8,128)S(1)}, u32[]{:S(2)}) copy-start(f32[512,32]{0,1:T(8,128)S(1)} %get-tuple-element.139) | copy-start | bytes 196612
  87.1 54.4 %copy-start.51 = (f32[1024]{0:T(1024)S(1)}, f32[1024]{0:T(1024)}, u32[]{:S(2)}) copy-start(f32[1024]{0:T(1024)} %param.20) | copy-start | bytes 12292
  92.6 85.9 %copy-start.2 = (bf16[512,1024]{1,0:T(8,128)(2,1)}, bf16[512,1024]{1,0:T(8,128)(2,1)S(1)}, u32[]{:S(2)}) copy-start(bf16[512,1024]{1,0:T(8,128)(2,1)S(1)} %gather_fusion) | copy-start | bytes 3145732
  93.5 52.7 %copy-start.47 = (f32[512]{0:T(512)}, f32[512]{0:T(512)S(1)}, u32[]{:S(2)}) copy-start(f32[512]{0:T(512)S(1)} %get-tuple-element.141) | copy-start | bytes 6148
  184.1 376.8 %all-gather.24.cloned.1.call-start = ((), (), s32[]{:S(2)}) async-start(), calls=%async_computation.15 | async-start | bytes 9437184 | tf_op jit(solution)/shard_map/all_gather | solution.py:186
  185.5 389.0 %all-gather.22.cloned.1.call-start = ((), (), s32[]{:S(2)}) async-start(), calls=%async_computation.14 | async-start | bytes 9437184 | tf_op jit(solution)/shard_map/all_gather | solution.py:185
  186.8 401.1 %all-gather.26.cloned.1.call-start = ((), (), s32[]{:S(2)}) async-start(), calls=%async_computation.16 | async-start | bytes 9437184 | tf_op jit(solution)/shard_map/all_gather | solution.py:187
  188.2 602.5 %all-reduce.5.cloned.1.call-start = ((), (), s32[]{:S(2)}) async-start(), calls=%async_computation.20 | async-start | bytes 131072 | tf_op jit(solution)/shard_map/psum | solution.py:243
  188.6 124.4 %copy-start.50 = (bf16[128,32]{0,1:T(8,128)(2,1)S(1)}, bf16[128,32]{0,1:T(8,128)(2,1)}, u32[]{:S(2)}) copy-start(bf16[128,32]{0,1:T(8,128)(2,1)} %param.24) | copy-start | bytes 24580
  326.6 44.5 %copy-start.22 = (bf16[1024,32]{0,1:T(8,128)(2,1)}, bf16[1024,32]{0,1:T(8,128)(2,1)S(1)}, u32[]{:S(2)}) copy-start(bf16[1024,32]{0,1:T(8,128)(2,1)S(1)} %all_gather.45) | copy-start | bytes 196612
  374.6 131.5 %copy-start.9 = (s32[1,2048,8]{1,2,0:T(8,128)S(1)}, s32[1,2048,8]{1,2,0:T(8,128)}, u32[]{:S(2)}) copy-start(s32[1,2048,8]{1,2,0:T(8,128)} %param.18) | copy-start | bytes 196612
  653.0 165.5 %reduce-scatter.13.cloned.1.call-start = ((), (), s32[]{:S(2)}) async-start(), calls=%async_computation.19 | async-start | bytes 10485760 | tf_op jit(solution)/shard_map/reduce_scatter | solution.py:280
  732.4 141.8 %reduce-scatter.11.cloned.1.call-start = ((), (), s32[]{:S(2)}) async-start(), calls=%async_computation.17 | async-start | bytes 5242880 | tf_op jit(solution)/shard_map/reduce_scatter | solution.py:229
  790.6 83.5 %copy-start.49 = (f32[512]{0:T(512)S(1)}, f32[512]{0:T(512)}, u32[]{:S(2)}) copy-start(f32[512]{0:T(512)} %get-tuple-element.142) | copy-start | bytes 6148
  790.7 234.3 %reduce-scatter.19.cloned.1.call-start = ((), (), s32[]{:S(2)}) async-start(), calls=%async_computation.24 | async-start | bytes 4718592 | tf_op jit(solution)/shard_map/reduce_scatter | solution.py:356
  882.1 172.6 %reduce-scatter.15.cloned.1.call-start = ((), (), s32[]{:S(2)}) async-start(), calls=%async_computation.22 | async-start | bytes 9437184 | tf_op jit(solution)/shard_map/reduce_scatter | solution.py:355
  966.6 144.3 %all-gather.28.cloned.1.call-start = ((), (), s32[]{:S(2)}) async-start(), calls=%async_computation.18 | async-start | bytes 5242880 | tf_op jit(solution)/shard_map/all_gather | solution.py:368
  967.2 233.8 %all-gather.30.cloned.1.call-start = ((), (), s32[]{:S(2)}) async-start(), calls=%async_computation.21 | async-start | bytes 10485760 | tf_op jit(solution)/shard_map/all_gather | solution.py:369
  975.3 394.8 %reduce-scatter.29.cloned.1.call-start = ((), (), s32[]{:S(2)}) async-start(), calls=%async_computation.29 | async-start | bytes 18874368 | tf_op jit(solution)/shard_map/reduce_scatter | solution.py:360
  990.4 548.7 %reduce-scatter.27.cloned.1.call-start = ((), (), s32[]{:S(2)}) async-start(), calls=%async_computation.28 | async-start | bytes 18874368 | tf_op jit(solution)/shard_map/reduce_scatter | solution.py:359
  1005.9 702.3 %reduce-scatter.25.cloned.1.call-start = ((), (), s32[]{:S(2)}) async-start(), calls=%async_computation.27 | async-start | bytes 18874368 | tf_op jit(solution)/shard_map/reduce_scatter | solution.py:358
  1021.0 713.4 %reduce-scatter.23.cloned.1.call-start = ((), (), s32[]{:S(2)}) async-start(), calls=%async_computation.26 | async-start | bytes 147456 | tf_op jit(solution)/shard_map/reduce_scatter | solution.py:357
  1024.9 742.4 %reduce-scatter.21.cloned.1.call-start = ((), (), s32[]{:S(2)}) async-start(), calls=%async_computation.25 | async-start | bytes 655360 | tf_op jit(solution)/shard_map/reduce_scatter | solution.py:364
  1025.6 773.2 %reduce-scatter.17.cloned.1.call-start = ((), (), s32[]{:S(2)}) async-start(), calls=%async_computation.23 | async-start | bytes 1310720 | tf_op jit(solution)/shard_map/reduce_scatter | solution.py:363
  (45 other events, 403.8 us)
Sparse Core Ops, SparseCore 0:
  9.6 23.8 all-gather.13
  35.4 51.6 all-gather.31
  89.0 52.5 all-gather.15
  143.2 35.1 all-gather.17
  180.1 52.6 all-gather.33
  235.2 52.6 all-gather.19
  290.1 80.2 all-gather.23
  372.6 80.5 all-gather.21
  455.4 80.5 all-gather.25
  653.1 40.6 all-reduce.4
  732.5 85.9 reduce-scatter.12
  821.4 52.7 reduce-scatter.10
  882.2 48.4 reduce-scatter.18
  966.7 87.9 reduce-scatter.14
  1057.1 53.7 all-gather.27
  1113.4 87.5 all-gather.29
  1203.3 166.7 reduce-scatter.28
  1372.4 166.6 reduce-scatter.26
  1541.6 166.6 reduce-scatter.24
  1711.0 23.3 reduce-scatter.22
  1737.8 29.3 reduce-scatter.20
  1770.9 27.8 reduce-scatter.16
where the time goes:
time: 1810 us
  waiting for transfers between devices  895 us (49%)
  local copies, waits for them, and re-layouts  414 us (23%)
  matrix products  259 us (14%)
  other arithmetic  151 us (8%)
  blocking collectives  69.9 us (4%)
    reduce_scatter x1, waiting for transfers between devices, body(): lax.psum_scatter(gate_wgrad, 'col', scatter_dimension=0, tiled=True)  166 us
    reduce_scatter x1, waiting for transfers between devices, body(): lax.psum_scatter(up_wgrad, 'col', scatter_dimension=0, tiled=True)  165 us
    reduce_scatter x1, waiting for transfers between devices, body(): lax.psum_scatter(down_wgrad, 'col', scatter_dimension=0, tiled=True)  162 us
    gather x5, local copies, waits for them, and re-layouts, body(): chosen = jnp.take_along_axis(logits, chosen_ids, axis=1)  132 us
    all_gather x1, waiting for transfers between devices, body(): lax.all_gather(input_dealt, 'row', axis=0, tiled=True)  83.9 us
    scatter x1, local copies, waits for them, and re-layouts, body(): slot_pair = jnp.full((exp_dev * capacity,), tok_grp * TOPK, jnp.int32).at...  60.5 us
    scatter x1, local copies, waits for them, and re-layouts, body(): slot_token = jnp.full((exp_dev * capacity,), tok_grp, jnp.int32).at[slot_...  60.3 us
    reduce_scatter x1, waiting for transfers between devices, body(): lax.psum_scatter(partial_sum.astype(jnp.bfloat16), 'row', scatter_dimensi...  52 us
  transfers between devices with their start and end apart: 22, of which 15 were waited for; matrix products, arithmetic and copies ran while one was open for 41% of the time, Pallas kernels for 0%

commit v1 on v0

v1 whole, which is shorter than its diff:
```python
import functools

import jax
import jax.numpy as jnp
from jax import lax
from jax.experimental import pallas as pl
from jax.experimental.pallas import tpu as pltpu
from jax.sharding import PartitionSpec as P

HEAD_WIDTH = 64
QUERY_HEADS = 16
KEY_VALUE_HEADS = 8
EXPERT_COUNT = 32
TOPK = 8
EPSILON = 1e-06
RESIDUAL_SCALE = 0.22
SCORE_SCALE = 0.015625
ROPE_BASE = 10000.0
MASKED = -1e30
LANES = 128
MIB = 1024 * 1024
BF = jnp.bfloat16
F32 = jnp.float32
ANY = pl.BlockSpec(memory_space=pl.ANY)
FULL = pl.BlockSpec(memory_space=pltpu.VMEM)


def mm(a, b):
    return lax.dot_general(a, b, (((1,), (0,)), ((), ())), preferred_element_type=F32)


def mm_nt(a, b):
    return lax.dot_general(a, b, (((1,), (1,)), ((), ())), preferred_element_type=F32)


def mm_tn(a, b):
    return lax.dot_general(a, b, (((0,), (0,)), ((), ())), preferred_element_type=F32)


def iota(shape, dim):
    return lax.broadcasted_iota(jnp.int32, shape, dim)


def params(mib):
    return pltpu.CompilerParams(vmem_limit_bytes=mib * MIB)


def cost(flops, moved):
    return pl.CostEstimate(flops=int(flops), bytes_accessed=int(moved), transcendentals=0)


def row_scale(values):
    return lax.rsqrt(jnp.mean(values * values, axis=-1, keepdims=True) + EPSILON)


def swap_halves(values):
    width = values.shape[-1]
    half = HEAD_WIDTH // 2
    low = (iota(values.shape, 1) % HEAD_WIDTH) < half
    ahead = pltpu.roll(values, width - half, 1)
    behind = pltpu.roll(values, half, 1)
    return jnp.where(low, ahead, behind)


def masked_probs(q, k, row0, starts):
    rows, cols = q.shape[0], k.shape[0]
    scores = mm_nt(q, k) * SCORE_SCALE
    at = iota((rows, cols), 1)
    allowed = (at <= iota((rows, cols), 0) + row0) & (at >= starts)
    scores = jnp.where(allowed, scores, MASKED)
    top = jnp.max(scores, axis=-1, keepdims=True)
    raised = jnp.exp(scores - top)
    total = jnp.sum(raised, axis=-1, keepdims=True)
    return raised * (1.0 / total)


def front_kernel(nblk, *refs):
    xin = refs[:nblk]
    (src, starts, cos, sin, gain_a, gain_m, w_att) = refs[nblk : nblk + 7]
    (xd, attn, qkv, mixed, middle, moe) = refs[nblk + 7 :]
    tokens = xd.shape[0]
    half = tokens // 2
    qw = w_att.shape[2] * 2 // 3
    source = src[...]
    x = jnp.zeros((tokens, xd.shape[1]), F32)
    for j in range(nblk):
        pick = jnp.where(source == iota((tokens, tokens), 1) + j * tokens, 1.0, 0.0).astype(BF)
        x = x + mm(pick, xin[j][...])
    xd[...] = x.astype(BF)
    attn[...] = (x * row_scale(x) * gain_a[...]).astype(BF)
    groups = qw // (4 * HEAD_WIDTH)

    def project(j, carry):
        proj = mm(attn[...], w_att[j, :, :qw])
        cos_w = jnp.concatenate([cos[...]] * groups, axis=1)
        sin_w = jnp.concatenate([sin[...]] * groups, axis=1)
        turned = proj * cos_w + swap_halves(proj) * sin_w
        qkv[:, pl.ds(pl.multiple_of(j * qw, qw), qw)] = turned.astype(BF)
        return carry

    lax.fori_loop(0, nblk, project, 0)

    def group(g, carry):
        chunk = qkv[:, pl.ds(pl.multiple_of(g * 4 * HEAD_WIDTH, 4 * HEAD_WIDTH), 4 * HEAD_WIDTH)]
        k = chunk[:, 2 * HEAD_WIDTH : 3 * HEAD_WIDTH]
        v = chunk[:, 3 * HEAD_WIDTH :]
        for b in range(2):
            span = (b + 1) * half
            outs = []
            for h in range(2):
                q = chunk[b * half : (b + 1) * half, h * HEAD_WIDTH : (h + 1) * HEAD_WIDTH]
                probs = masked_probs(q, k[:span], b * half, starts[b * half : (b + 1) * half, :])
                outs.append(mm(probs.astype(BF), v[:span]))
            mixed[b * half : (b + 1) * half, pl.ds(pl.multiple_of(g * 2 * HEAD_WIDTH, 2 * HEAD_WIDTH), 2 * HEAD_WIDTH)] = (
                jnp.concatenate(outs, axis=1).astype(BF)
            )
        return carry

    lax.fori_loop(0, groups * nblk, group, 0)
    ow = w_att.shape[2] - qw
    out = jnp.zeros((tokens, xd.shape[1]), F32)
    for j in range(nblk):
        out = out + mm_nt(mixed[:, j * ow : (j + 1) * ow], w_att[j, :, qw:])
    mid = xd[...].astype(F32) + RESIDUAL_SCALE * out
    middle[...] = mid
    moe[...] = (mid * row_scale(mid) * gain_m[...]).astype(BF)


def front(xin, src, starts, cos, sin, gain_a, gain_m, w_att):
    tokens, width = xin[0].shape
    nblk = len(xin)
    qkv_width = nblk * w_att.shape[2] * 2 // 3
    head_width = nblk * w_att.shape[2] // 3
    shape = jax.ShapeDtypeStruct
    return pl.pallas_call(
        functools.partial(front_kernel, nblk),
        out_shape=(
            shape((tokens, width), BF),
            shape((tokens, width), BF),
            shape((tokens, qkv_width), BF),
            shape((tokens, head_width), BF),
            shape((tokens, width), F32),
            shape((tokens, width), BF),
        ),
        in_specs=[FULL] * (nblk + 7),
        out_specs=[FULL] * 6,
        compiler_params=params(48),
        cost_estimate=cost(10e9, 30 * MIB),
        name="attention_forward",
    )(*xin, src, starts, cos, sin, gain_a, gain_m, w_att)


def deal_kernel(nblk, *refs):
    cot = refs[:nblk]
    (src, ids, spots) = refs[nblk : nblk + 3]
    (dsum, dy, slot_cols, slot_rows, chosen) = refs[nblk + 3 :]
    tokens = cot[0].shape[0]

    def block(b, carry):
        at = pl.ds(pl.multiple_of(b * tokens, tokens), tokens)
        source = src[at, :]
        rows = jnp.zeros(cot[0].shape, F32)
        for j in range(nblk):
            pick = jnp.where(source == iota((tokens, tokens), 1) + j * tokens, 1.0, 0.0).astype(BF)
            rows = rows + mm(pick, cot[j][...])
        dsum[at, :] = (RESIDUAL_SCALE * rows).astype(BF)

        @pl.when(b == 0)
        def _():
            dy[...] = rows.astype(BF)

        lane = iota((tokens, LANES), 1)
        spot = jnp.zeros((tokens, LANES), F32)
        named = jnp.zeros((tokens, LANES), F32)
        own_ids = ids[at, :]
        own_spots = spots[at, :]
        for k in range(TOPK):
            hit = lane == own_ids[:, k : k + 1]
            named = jnp.where(hit, 1.0, named)
            spot = jnp.where(hit, own_spots[:, k : k + 1].astype(F32), spot)
        chosen[at, :] = named
        slot = jnp.where(named > 0.0, spot, -1.0)
        slot_cols[at, :] = slot
        slot_rows[:, at] = slot.T
        return carry

    lax.fori_loop(0, nblk, block, 0)


def deal(cot, src, ids, spots):
    tokens, width = cot[0].shape
    nblk = len(cot)
    total = nblk * tokens
    shape = jax.ShapeDtypeStruct
    return pl.pallas_call(
        functools.partial(deal_kernel, nblk),
        out_shape=(
            shape((total, width), BF),
            shape((tokens, width), BF),
            shape((total, LANES), F32),
            shape((LANES, total), F32),
            shape((total, LANES), F32),
        ),
        in_specs=[FULL] * (nblk + 3),
        out_specs=[FULL] * 5,
        compiler_params=params(40),
        cost_estimate=cost(9e9, 20 * MIB),
        name="deal_cotangent",
    )(*cot, src, ids, spots)


def router_kernel(nblk, *refs):
    moe = refs[:nblk]
    (w_router, chosen, gates, packed) = refs[nblk:]
    tokens = moe[0].shape[0]
    local = EXPERT_COUNT // nblk
    for j in range(nblk):
        at = slice(j * tokens, (j + 1) * tokens)
        logits = mm(moe[j][...], w_router[...])
        named = chosen[at, :] > 0.0
        logits = jnp.where(named, logits, MASKED)
        top = jnp.max(logits, axis=-1, keepdims=True)
        raised = jnp.where(named, jnp.exp(logits - top), 0.0)
        gate = raised / jnp.sum(raised, axis=-1, keepdims=True)
        gates[at, :] = gate
        lane = iota((tokens, LANES), 1)
        own = jnp.where(lane < local, gate, 0.0)
        high = own.astype(BF).astype(F32)
        rest = own - high
        mid = rest.astype(BF).astype(F32)
        low = rest - mid
        packed[at, :] = (high + pltpu.roll(mid, local, 1) + pltpu.roll(low, 2 * local, 1)).astype(BF)


def router(moe, w_router, chosen):
    tokens = moe[0].shape[0]
    nblk = len(moe)
    total = nblk * tokens
    shape = jax.ShapeDtypeStruct
    return pl.pallas_call(
        functools.partial(router_kernel, nblk),
        out_shape=(shape((total, LANES), F32), shape((total, LANES), BF)),
        in_specs=[FULL] * (nblk + 2),
        out_specs=[FULL] * 2,
        compiler_params=params(24),
        cost_estimate=cost(1e9, 7 * MIB),
        name="router",
    )(*moe, w_router, chosen)


def expert_kernel(nblk, base, first, last, local, capacity, *refs):
    moe_hbm = refs[:nblk]
    refs = refs[nblk:]
    if first:
        (dsum_hbm, slot_rows, slot_cols, packed, w) = refs[:5]
        refs = refs[5:]
    else:
        (dsum_hbm, slot_rows, slot_cols, packed, w, acc_in, accg_in) = refs[:7]
        refs = refs[7:]
    if last:
        (grads, sums, dgates) = refs[:3]
    else:
        (grads, acc_out, accg_out) = refs[:3]
    (moe, dsum, acc, accg, sel, selt, routed, dsl, dslot, y1, y2, sems) = refs[3:]
    step = pl.program_id(0)
    steps = pl.num_programs(0)
    e = base + step
    tokens, width = moe_hbm[0].shape
    total = nblk * tokens
    fe = w.shape[4]
    shard = w.shape[3]
    tile = 256
    tiles = width // tile
    copies = []
    for j in range(nblk):
        copies.append(
            pltpu.make_async_copy(moe_hbm[j], moe.at[pl.ds(j * tokens, tokens)], sems.at[j])
        )
    copies.append(pltpu.make_async_copy(dsum_hbm, dsum, sems.at[nblk]))
    loads = []
    if not first:
        loads.append(pltpu.make_async_copy(acc_in, acc, sems.at[nblk + 1]))
        loads.append(pltpu.make_async_copy(accg_in, accg, sems.at[nblk + 2]))

    @pl.when(step == 0)
    def _():
        for c in copies:
            c.start()
        for c in loads:
            c.start()
        if first:
            acc[...] = jnp.zeros(acc.shape, F32)
            accg[...] = jnp.zeros(accg.shape, F32)

    row = slot_rows[pl.ds(e, 1), :]
    lanes = iota((tokens, LANES), 1)
    for j in range(nblk):
        at = slice(j * tokens, (j + 1) * tokens)
        sel[:, at] = jnp.where(
            iota((capacity, tokens), 0).astype(F32) == row[:, at], 1.0, 0.0
        ).astype(BF)
        col = jnp.sum(jnp.where(lanes == e, slot_cols[at, :], 0.0), axis=1, keepdims=True)
        selt[at, :] = jnp.where(
            col == iota((tokens, capacity), 1).astype(F32), 1.0, 0.0
        ).astype(BF)

    @pl.when(step == 0)
    def _():
        for c in copies:
            c.wait()

    def dispatch(n, carry):
        at = pl.ds(pl.multiple_of(n * tile, tile), tile)
        routed[:, at] = mm(sel[...], moe[:, at]).astype(BF)
        dsl[:, at] = mm(sel[...], dsum[:, at]).astype(BF)
        return carry

    lax.fori_loop(0, tiles, dispatch, 0)
    lane = iota((capacity, LANES), 1)
    picked = mm(sel[...], packed[...])
    mine = (lane == e) | (lane == e + local) | (lane == e + 2 * local)
    gate = jnp.sum(jnp.where(mine, picked, 0.0), axis=1, keepdims=True)
    dslot[...] = (gate * dsl[...].astype(F32)).astype(BF)

    def weight(i):
        return w[:, 0, i].reshape(width, fe)

    per = tile // shard

    def weight_tile(i, n):
        return w[pl.ds(n * per, per), 0, i].reshape(tile, fe)

    gate_in = mm(routed[...], weight(0))
    up_in = mm(routed[...], weight(1))
    sig = jax.nn.sigmoid(gate_in)
    silu = gate_in * sig
    hidden = (silu * up_in).astype(BF)

    def down(n, inner):
        at = pl.ds(pl.multiple_of(n * tile, tile), tile)
        out = mm_nt(hidden, weight_tile(2, n))
        y1[:, at] = (gate * out).astype(BF)
        return inner + jnp.sum(dsl[:, at].astype(F32) * out, axis=1, keepdims=True)

    inner = lax.fori_loop(0, tiles, down, jnp.zeros((capacity, 1), F32))
    high = inner.astype(BF).astype(F32)
    rest = inner - high
    mid = rest.astype(BF).astype(F32)
    low = rest - mid
    spread = jnp.where(
        lane == e,
        high,
        jnp.where(lane == e + local, mid, jnp.where(lane == e + 2 * local, low, 0.0)),
    ).astype(BF)
    dhidden = mm(dslot[...], weight(2))
    dgate = (dhidden * up_in * sig * (1.0 + gate_in * (1.0 - sig))).astype(BF)
    dup = (dhidden * silu).astype(BF)

    def back(n, carry):
        at = pl.ds(pl.multiple_of(n * tile, tile), tile)
        devs = pl.ds(n * per, per)
        grads[devs, 0, 2] = mm_tn(dslot[:, at], hidden).astype(BF).reshape(per, shard, fe)
        rows = routed[:, at]
        grads[devs, 0, 0] = mm_tn(rows, dgate).astype(BF).reshape(per, shard, fe)
        grads[devs, 0, 1] = mm_tn(rows, dup).astype(BF).reshape(per, shard, fe)
        y2[:, at] = (mm_nt(dgate, weight_tile(0, n)) + mm_nt(dup, weight_tile(1, n))).astype(BF)
        return carry

    lax.fori_loop(0, tiles, back, 0)

    if not first:

        @pl.when(step == 0)
        def _():
            for c in loads:
                c.wait()

    def combine(b, carry):
        at = pl.ds(pl.multiple_of(b * tokens, tokens), tokens)
        chosen = selt[at, :]
        acc[0, at, :] += mm(chosen, y1[...])
        acc[1, at, :] += mm(chosen, y2[...])
        accg[at, :] += mm(chosen, spread)
        return carry

    lax.fori_loop(0, nblk, combine, 0)

    @pl.when(step == steps - 1)
    def _():
        if last:
            moe[...] = acc[0].astype(BF)
            dsum[...] = acc[1].astype(BF)
            outs = [
                pltpu.make_async_copy(moe, sums.at[0], sems.at[0]),
                pltpu.make_async_copy(dsum, sums.at[1], sems.at[1]),
                pltpu.make_async_copy(accg, dgates, sems.at[2]),
            ]
        else:
            outs = [
                pltpu.make_async_copy(acc, acc_out, sems.at[0]),
                pltpu.make_async_copy(accg, accg_out, sems.at[1]),
            ]
        for c in outs:
            c.start()
        for c in outs:
            c.wait()


def experts(moe, dsum, slot_rows, slot_cols, packed, w, carried, base, last, capacity):
    nblk = len(moe)
    tokens, width = moe[0].shape
    total = nblk * tokens
    cols, ne, three, shard, fe = w.shape
    local = EXPERT_COUNT // nblk
    first = carried is None
    shape = jax.ShapeDtypeStruct
    wspec = pl.BlockSpec((cols, 1, three, shard, fe), lambda s: (0, s, 0, 0, 0))
    ins = [*moe, dsum, slot_rows, slot_cols, packed, w]
    in_specs = [ANY] * (nblk + 1) + [FULL, FULL, FULL, wspec]
    aliases = {}
    if not first:
        ins += list(carried)
        in_specs += [ANY, ANY]
        aliases = {} if last else {len(ins) - 2: 1, len(ins) - 1: 2}
    if last:
        outs = (shape((2, total, width), BF), shape((total, LANES), F32))
    else:
        outs = (shape((2, total, width), F32), shape((total, LANES), F32))
    return pl.pallas_call(
        functools.partial(expert_kernel, nblk, base, first, last, local, capacity),
        grid=(ne,),
        out_shape=(shape(w.shape, BF), *outs),
        in_specs=in_specs,
        out_specs=[wspec, ANY, ANY],
        scratch_shapes=[
            pltpu.VMEM((total, width), BF),
            pltpu.VMEM((total, width), BF),
            pltpu.VMEM((2, total, width), F32),
            pltpu.VMEM((total, LANES), F32),
            pltpu.VMEM((capacity, total), BF),
            pltpu.VMEM((total, capacity), BF),
            pltpu.VMEM((capacity, width), BF),
            pltpu.VMEM((capacity, width), BF),
            pltpu.VMEM((capacity, width), BF),
            pltpu.VMEM((capacity, width), BF),
            pltpu.VMEM((capacity, width), BF),
            pltpu.SemaphoreType.DMA((nblk + 3,)),
        ],
        input_output_aliases=aliases,
        compiler_params=params(60),
        cost_estimate=cost(14e9 * ne, 40 * MIB),
        name="experts",
    )(*ins)


def back_kernel(nblk, *refs):
    dm = refs[:nblk]
    dg = refs[nblk : 2 * nblk]
    (gates, middle, moe, dy, mixed, qkv, attn, xd, w_att, w_router, starts, cos, sin, gain_a, gain_m) = refs[
        2 * nblk : 2 * nblk + 15
    ]
    (igrad, qkv_grad, out_grad, router_grad, gains) = refs[2 * nblk + 15 : 2 * nblk + 20]
    (dmid, dmix, dproj) = refs[2 * nblk + 20 :]
    tokens, width = xd.shape
    half = tokens // 2
    local = EXPERT_COUNT // nblk
    qw = w_att.shape[2] * 2 // 3
    ow = w_att.shape[2] - qw
    hw = HEAD_WIDTH
    lane = iota((tokens, LANES), 1)
    dgate = jnp.zeros((tokens, LANES), F32)
    for j in range(nblk):
        part = dg[j][...]
        part = part + pltpu.roll(part, LANES - local, 1) + pltpu.roll(part, LANES - 2 * local, 1)
        part = jnp.where(lane < local, part, 0.0)
        dgate = dgate + (part if j == 0 else pltpu.roll(part, j * local, 1))
    gate = gates[...]
    dchosen = gate * (dgate - jnp.sum(gate * dgate, axis=1, keepdims=True))
    dlogits = dchosen.astype(BF)
    router_grad[...] = mm_tn(moe[...], dlogits)
    dmoe = mm_nt(dlogits, w_router[...])
    for j in range(nblk):
        dmoe = dmoe + dm[j][...].astype(F32)
    mid = middle[...]
    r = row_scale(mid)
    scaled = dmoe * gain_m[...]
    inner = jnp.mean(scaled * mid, axis=-1, keepdims=True)
    dmid[...] = dy[...].astype(F32) + (r * scaled - mid * (r * r * r) * inner)
    gains[1:2, :] = jnp.sum(dmoe * mid * r, axis=0, keepdims=True)
    dattn = (RESIDUAL_SCALE * dmid[...]).astype(BF)
    for j in range(nblk):
        dmix[:, j * ow : (j + 1) * ow] = mm(dattn, w_att[j, :, qw:]).astype(BF)
        out_grad[j] = mm_tn(dattn, mixed[:, j * ow : (j + 1) * ow]).astype(BF)

    def group(g, carry):
        chunk = qkv[:, pl.ds(pl.multiple_of(g * 4 * hw, 4 * hw), 4 * hw)]
        dm_chunk = dmix[:, pl.ds(pl.multiple_of(g * 2 * hw, 2 * hw), 2 * hw)]
        k = chunk[:, 2 * hw : 3 * hw]
        v = chunk[:, 3 * hw :]
        dk = jnp.zeros((tokens, hw), F32)
        dv = jnp.zeros((tokens, hw), F32)
        dq = [[None, None], [None, None]]
        for b in range(2):
            span = (b + 1) * half
            rows = slice(b * half, (b + 1) * half)
            for h in range(2):
                q = chunk[rows, h * hw : (h + 1) * hw]
                dmh = dm_chunk[rows, h * hw : (h + 1) * hw]
                probs = masked_probs(q, k[:span], b * half, starts[rows, :])
                dprobs = mm_nt(dmh, v[:span])
                total = jnp.sum(probs * dprobs, axis=-1, keepdims=True)
                dscores = (probs * (dprobs - total) * SCORE_SCALE).astype(BF)
                dq[h][b] = mm(dscores, k[:span])
                dk_part = mm_tn(dscores, q)
                dv_part = mm_tn(probs.astype(BF), dmh)
                if span < tokens:
                    pad = jnp.zeros((tokens - span, hw), F32)
                    dk_part = jnp.concatenate([dk_part, pad], axis=0)
                    dv_part = jnp.concatenate([dv_part, pad], axis=0)
                dk = dk + dk_part
                dv = dv + dv_part
        d = jnp.concatenate(
            [
                jnp.concatenate(dq[0], axis=0),
                jnp.concatenate(dq[1], axis=0),
                dk,
                dv,
            ],
            axis=1,
        )
        d = d * cos[...] - swap_halves(d) * sin[...]
        dproj[:, pl.ds(pl.multiple_of(g * 4 * hw, 4 * hw), 4 * hw)] = d.astype(BF)
        return carry

    lax.fori_loop(0, nblk * qw // (4 * hw), group, 0)
    dattn_in = jnp.zeros((tokens, width), F32)
    for j in range(nblk):
        part = dproj[:, j * qw : (j + 1) * qw]
        qkv_grad[j] = mm_tn(attn[...], part).astype(BF)
        dattn_in = dattn_in + mm_nt(part, w_att[j, :, :qw])
    x = xd[...].astype(F32)
    r = row_scale(x)
    scaled = dattn_in * gain_a[...]
    inner = jnp.mean(scaled * x, axis=-1, keepdims=True)
    igrad[...] = (dmid[...] + (r * scaled - x * (r * r * r) * inner)).astype(BF)
    gains[0:1, :] = jnp.sum(dattn_in * x * r, axis=0, keepdims=True)


def backward(dm, dg, *rest):
    nblk = len(dm)
    tokens, width = dm[0].shape
    w_att = rest[8]
    qw = w_att.shape[2] * 2 // 3
    ow = w_att.shape[2] - qw
    shape = jax.ShapeDtypeStruct
    return pl.pallas_call(
        functools.partial(back_kernel, nblk),
        out_shape=(
            shape((tokens, width), BF),
            shape((nblk, width, qw), BF),
            shape((nblk, width, ow), BF),
            shape((width, LANES), F32),
            shape((2, width), F32),
        ),
        in_specs=[FULL] * (2 * nblk + 15),
        out_specs=[FULL] * 5,
        scratch_shapes=[
            pltpu.VMEM((tokens, width), F32),
            pltpu.VMEM((tokens, nblk * ow), BF),
            pltpu.VMEM((tokens, nblk * qw), BF),
        ],
        compiler_params=params(60),
        cost_estimate=cost(20e9, 40 * MIB),
        name="attention_backward",
    )(*dm, *dg, *rest)


def given_kernel(nblk, *refs):
    rows = refs[:nblk]
    src, out = refs[nblk:]
    tokens, width = out.shape
    total = jnp.zeros((tokens, width), F32)
    for j in range(nblk):
        at = src[:, j * tokens : (j + 1) * tokens]
        pick = jnp.where(iota((tokens, tokens), 0) == at, 1.0, 0.0).astype(BF)
        total = total + mm(pick, rows[j][...])
    out[...] = total.astype(out.dtype)


def to_given(rows, src_row, dtype):
    nblk = len(rows)
    return pl.pallas_call(
        functools.partial(given_kernel, nblk),
        out_shape=jax.ShapeDtypeStruct(rows[0].shape, dtype),
        in_specs=[FULL] * (nblk + 1),
        out_specs=FULL,
        compiler_params=params(24),
        cost_estimate=cost(2e9, 6 * MIB),
        name="to_given_order",
    )(*rows, src_row)


def swap_over(value, axis, size, step):
    return lax.ppermute(value, axis, [(i, i ^ step) for i in range(size)])


def spread_rows(value, axis, size, step=1):
    return [value] + [swap_over(value, axis, size, j) for j in range(step, size, step)]


def sum_over(value, axis, size):
    return functools.reduce(lambda a, b: a + b, spread_rows(value, axis, size))


def body(
    block_in,
    cotangent,
    seq_lengths,
    seq_order,
    expert_ids,
    places,
    attn_gain,
    w_qkv,
    w_out,
    moe_gain,
    w_router,
    w_gate,
    w_up,
    w_down,
):
    tokens = block_in.shape[1]
    width = block_in.shape[2]
    rows = lax.axis_size("row")
    cols = lax.axis_size("col")
    total = tokens * rows
    r = lax.axis_index("row")
    c = lax.axis_index("col")
    parity = c % 2
    local = w_gate.shape[1]
    shard = w_gate.shape[0]
    fe = w_gate.shape[2]
    capacity = total * TOPK // EXPERT_COUNT
    pairs = cols // 2
    qw = w_qkv.shape[1]
    ow = w_out.shape[1]

    stacked = jnp.stack([w_gate, w_up, w_down]).transpose(2, 0, 1, 3)
    chunk = 2
    gathered = [
        lax.all_gather(stacked[i : i + chunk], "col", axis=0) for i in range(0, local, chunk)
    ]

    given_in = spread_rows(block_in[0], "row", rows)

    w_own = jnp.concatenate([w_qkv, w_out], axis=1)
    w_half = jnp.stack(spread_rows(w_own, "col", cols, 2))
    w_rows = jnp.stack(spread_rows(w_half, "row", rows))
    w_other = swap_over(w_rows, "col", cols, 1)
    base = c // 2

    def join_parity(mine, other, axis):
        even = jnp.where(parity == 0, mine, other)
        odd = jnp.where(parity == 0, other, mine)
        both = jnp.stack([even, odd], axis=axis + 1)
        return jnp.concatenate(
            [lax.dynamic_slice_in_dim(both, base ^ i, 1, axis) for i in range(pairs)], axis=axis
        )

    w_att = join_parity(w_rows, w_other, 1).reshape(rows, cols * shard, qw + ow)

    lengths = seq_lengths[0]
    perm = seq_order[0]
    seq_ids = jnp.arange(lengths.shape[0], dtype=jnp.int32)
    picked = perm[:, None] == seq_ids[None, :]
    dealt_len = jnp.sum(jnp.where(picked, lengths[None, :], 0), axis=1)
    before = seq_ids[None, :] < perm[:, None]
    source_base = jnp.sum(jnp.where(before, lengths[None, :], 0), axis=1)
    upto = seq_ids[None, :] <= seq_ids[:, None]
    seq_ends = jnp.sum(jnp.where(upto, dealt_len[None, :], 0), axis=1)
    dealt_start = seq_ends - dealt_len
    turn = r * tokens
    pos = jnp.arange(total, dtype=jnp.int32) ^ turn
    inside = (pos[:, None] >= dealt_start[None, :]) & (pos[:, None] < seq_ends[None, :])
    seq_starts = jnp.sum(jnp.where(inside, dealt_start[None, :], 0), axis=1)
    offset = pos - seq_starts
    source = jnp.sum(jnp.where(inside, source_base[None, :], 0), axis=1) + offset
    source = source ^ turn
    src_col = source[:, None]
    src_row = source[None, :]
    own_offset = offset[:tokens]
    own_starts = (seq_starts[:tokens] - turn)[:, None]

    half = HEAD_WIDTH // 2
    frequency = ROPE_BASE ** (-jnp.arange(half, dtype=F32) * 2.0 / HEAD_WIDTH)
    turned = own_offset.astype(F32)[:, None] * frequency[None, :]
    cosine, sine = jnp.cos(turned), jnp.sin(turned)
    ones, zeros = jnp.ones_like(cosine), jnp.zeros_like(cosine)
    cos_w = jnp.concatenate([cosine] * 6 + [ones] * 2, axis=1)
    sin_w = jnp.concatenate([-sine, sine] * 3 + [zeros] * 2, axis=1)

    gain_a = attn_gain[None, :]
    gain_m = moe_gain[None, :]
    xd, attn, qkv, mixed, middle, moe_own = front(
        given_in, src_col[:tokens], own_starts, cos_w, sin_w, gain_a, gain_m, w_att
    )
    moe = spread_rows(moe_own, "row", rows)

    held = lax.optimization_barrier((cotangent[0], given_in[-1]))[0]
    given_cot = spread_rows(held, "row", rows)

    def by_block(table):
        blocks = table.reshape(rows, tokens, TOPK)
        return jnp.concatenate(
            [lax.dynamic_slice_in_dim(blocks, r ^ j, 1, 0) for j in range(rows)], axis=0
        ).reshape(total, TOPK)

    ids = by_block(expert_ids[0])
    spots = by_block(places[0])
    ids = ((ids // local) ^ r) * local + ids % local
    spots = jnp.where(spots < capacity, spots, -1)
    dsum, dy, slot_cols, slot_rows, chosen = deal(given_cot, src_col, ids, spots)

    router_half = jnp.stack(spread_rows(w_router, "col", cols, 2))
    router_full = join_parity(router_half, swap_over(router_half, "col", cols, 1), 0)
    router_blocks = router_full.reshape(width, rows, local)
    router_x = jnp.concatenate(
        [lax.dynamic_slice_in_dim(router_blocks, r ^ j, 1, 1) for j in range(rows)], axis=1
    ).reshape(width, EXPERT_COUNT)
    router_x = jnp.pad(router_x, ((0, 0), (0, LANES - EXPERT_COUNT)))
    gates, packed = router(moe, router_x, chosen)

    carried = None
    summed = []
    for i, w in enumerate(gathered):
        last = i == len(gathered) - 1
        grads, *carried = experts(
            moe, dsum, slot_rows, slot_cols, packed, w, carried, i * chunk, last, capacity
        )
        summed.append(lax.psum_scatter(grads, "col", scatter_dimension=0, tiled=False))
    sums, dgates = carried

    def send_blocks(value):
        blocks = value.reshape(rows, tokens, value.shape[-1])
        return [blocks[0]] + [swap_over(blocks[j], "row", rows, j) for j in range(1, rows)]

    dg = send_blocks(dgates)
    dm = send_blocks(sums[1])
    es = send_blocks(lax.optimization_barrier((sums[0], dm[-1]))[0])
    dm[0] = lax.optimization_barrier((dm[0], summed[0]))[0]
    igrad, qkv_part, out_part, router_part, gain_part = backward(
        dm,
        dg,
        gates[:tokens],
        middle,
        moe_own,
        dy,
        mixed,
        qkv,
        attn,
        xd,
        w_att,
        router_x,
        own_starts,
        cos_w,
        sin_w,
        gain_a,
        gain_m,
    )
    expert_sum = functools.reduce(lambda a, b: a + b, [v.astype(F32) for v in es])
    block_dealt = (middle + RESIDUAL_SCALE * expert_sum).astype(BF)
    igrad = lax.optimization_barrier((igrad, summed[1]))[0]
    block_out = to_given(spread_rows(block_dealt, "row", rows), src_row, BF)[None]
    input_grad = to_given(spread_rows(igrad, "row", rows), src_row, F32)[None]

    part = jnp.concatenate([qkv_part, out_part], axis=2).reshape(
        rows, pairs, 2, shard, qw + ow
    )
    mine = jnp.where(parity == 0, part[:, :, 0], part[:, :, 1])
    other = jnp.where(parity == 0, part[:, :, 1], part[:, :, 0])
    chip = (mine.astype(F32) + swap_over(other, "col", cols, 1).astype(F32)).astype(BF)
    row_sum = functools.reduce(
        lambda a, b: a + b,
        [chip[0].astype(F32)]
        + [swap_over(chip[j], "row", rows, j).astype(F32) for j in range(1, rows)],
    ).astype(BF)
    z_own = [
        lax.dynamic_index_in_dim(row_sum, base ^ i, 0, keepdims=False) for i in range(pairs)
    ]
    att_sum = functools.reduce(
        lambda a, b: a + b,
        [z_own[0].astype(F32)]
        + [swap_over(z_own[i], "col", cols, 2 * i).astype(F32) for i in range(1, pairs)],
    )
    qkv_grad = att_sum[:, :qw]
    out_grad = att_sum[:, qw:]

    blocks = router_part[:, :EXPERT_COUNT].reshape(width, rows, local)
    router_std = jnp.concatenate(
        [lax.dynamic_slice_in_dim(blocks, r ^ j, 1, 1) for j in range(rows)], axis=1
    ).reshape(width * EXPERT_COUNT // width, width)
    small = jnp.concatenate([router_std, gain_part], axis=0)
    small = sum_over(small, "row", rows)
    small = sum_over(small, "col", cols)
    router_all = small[:EXPERT_COUNT].reshape(width, EXPERT_COUNT)
    router_grad = lax.dynamic_slice_in_dim(router_all, c * shard, shard, 0)
    attn_gain_total = small[EXPERT_COUNT]
    moe_gain_total = small[EXPERT_COUNT + 1]

    grads = jnp.concatenate(summed, axis=0).astype(F32).transpose(1, 2, 0, 3)
    return (
        block_out,
        input_grad,
        attn_gain_total,
        qkv_grad,
        out_grad,
        moe_gain_total,
        router_grad,
        grads[0],
        grads[1],
        grads[2],
    )


def solution(mesh):
    tokens = P("col", "row", None)
    weight = P("col", "row")
    expert = P("col", "row", None)
    return jax.shard_map(
        body,
        mesh=mesh,
        in_specs=(
            tokens,
            tokens,
            P("col", None),
            P("col", None),
            P("col", None, None),
            P("col", None, None),
            P(),
            weight,
            weight,
            P(),
            P("col", None),
            expert,
            expert,
            expert,
        ),
        out_specs=(
            tokens,
            tokens,
            P(),
            weight,
            weight,
            P(),
            P("col", None),
            expert,
            expert,
            expert,
        ),
        check_vma=False,
    )
```

time: 1810 us -> 794 us (0.44)
  waiting for transfers between devices: 895 us -> 239 us
  local copies, waits for them, and re-layouts: 414 us -> 64.2 us
  Pallas kernels: 0 us -> 318 us
  matrix products: 259 us -> 0 us
  other arithmetic: 151 us -> 32.6 us
  starting transfers between devices: 1.51 us -> 118 us
  blocking collectives: 69.9 us -> 0 us
    reduce_scatter x10 -> x4, waiting for transfers between devices: 687 us -> 0.01 us  [body(): lax.psum_scatter(grads, 'col', scatter_dimension=0, tiled=False)]
    pallas_call x0 -> x10, Pallas kernels: none -> 318 us  [the longest x4 211 us: experts(): pl.pallas_call(functools.partial(expert_kernel, nblk, base, first, last,...]
    dot_general x24 -> x0, matrix products: 259 us -> none  [the longest x1 24.7 us: attend_back(): jnp.einsum('gjqk,qgjd->kgd', scores_grad, query_block, preferred_element_...]
    ppermute x0 -> x52, waiting for transfers between devices: none -> 236 us  [swap_over(): return lax.ppermute(value, axis, [(i, i ^ step) for i in range(size)])]
    gather x12 -> x0, local copies, waits for them, and re-layouts: 235 us -> none  [the longest x5 132 us: body(): chosen = jnp.take_along_axis(logits, chosen_ids, axis=1)]
    all_gather x11 -> x4, waiting for transfers between devices: 204 us -> 0.06 us  [body(): lax.all_gather(stacked[i:i + chunk], 'col', axis=0)]
    scatter x3 -> x0, local copies, waits for them, and re-layouts: 129 us -> none  [the longest x1 60.5 us: body(): slot_pair = jnp.full((exp_dev * capacity,), tok_grp * TOPK, jnp.int32).at...]
    ppermute x0 -> x52, starting transfers between devices: none -> 118 us  [swap_over(): return lax.ppermute(value, axis, [(i, i ^ step) for i in range(size)])]
  transfers between devices with their start and end apart: 22 -> 60, of which waited for: 15 -> 22; matrix products, arithmetic and copies ran while one was open for 41% -> 9% of each run, Pallas kernels for 0% -> 40%
where the time goes in v1:
time: 794 us; the launch traced here: 787 us
  Pallas kernels  318 us (40%)
  waiting for transfers between devices  239 us (30%)
  starting transfers between devices  118 us (15%)
  local copies, waits for them, and re-layouts  64.2 us (8%)
  other arithmetic  32.6 us (4%)
  between operations  15.2 us (2%)
    ppermute x52, waiting for transfers between devices, swap_over(): return lax.ppermute(value, axis, [(i, i ^ step) for i in range(size)])  236 us
    pallas_call x4, Pallas kernels, experts(): pl.pallas_call(functools.partial(expert_kernel, nblk, base, first, last,...  211 us
    ppermute x52, starting transfers between devices, swap_over(): return lax.ppermute(value, axis, [(i, i ^ step) for i in range(size)])  118 us
    pallas_call x1, Pallas kernels, backward(): pl.pallas_call(functools.partial(back_kernel, nblk), out_shape=(shape((to...  44.8 us
    pallas_call x1, Pallas kernels, front(): pl.pallas_call(functools.partial(front_kernel, nblk), out_shape=(shape((t...  31.6 us
    unnamed x115, local copies, waits for them, and re-layouts  24.2 us
    pallas_call x1, Pallas kernels, deal(): pl.pallas_call(functools.partial(deal_kernel, nblk), out_shape=(shape((to...  17.3 us
  transfers between devices with their start and end apart: 60, of which 22 were waited for; matrix products, arithmetic and copies ran while one was open for 9% of the time, Pallas kernels for 40%

profile of v1, /device:TPU:9, one launch (start us, length us, event | category | flops | bytes accessed | tf_op | source)
XLA Modules:
  0.0 786.5 jit_solution(13214247942408435127)
XLA Ops:
  18.4 6.6 collective-permute-done.5
  25.0 4.5 collective-permute-done.3
  29.5 12.8 %collective-permute-done.4 = bf16[128,768]{1,0:T(8,128)(2,1)S(1)} collective-permute-done((bf16[128,768]{1,0:T(8,128)(2,1)S(1)}, bf16[128,768]{1,0:T(8,128)(2,1)S(1)}, u32[]{:S(2)}, u32[]{:S(2)}) %collective-permute-start.4) | collective-permute-done | bytes 196640 | tf_op jit(solution)/shard_map/ppermute | solution.py:604
  50.0 6.3 collective-permute-done.6
  59.3 14.7 %collective-permute-done.8 = bf16[4,128,768]{2,1,0:T(8,128)(2,1)S(1)} collective-permute-done((bf16[4,128,768]{2,1,0:T(8,128)(2,1)}, bf16[4,128,768]{2,1,0:T(8,128)(2,1)S(1)}, u32[]{:S(2)}, u32[]{:S(2)}) %collective-permute-start.8) | collective-permute-done | bytes 786464 | tf_op jit(solution)/shard_map/ppermute | solution.py:604
  76.0 20.4 %collective-permute-start.9 = (bf16[4,4,128,768]{3,2,1,0:T(8,128)(2,1)}, bf16[4,4,128,768]{3,2,1,0:T(8,128)(2,1)}, u32[]{:S(2)}, u32[]{:S(2)}) collective-permute-start(bf16[4,4,128,768]{3,2,1,0:T(8,128)(2,1)} %pad_maximum_fusion.2), channel_id=1, source_target_pairs={{0,1},{1,0},{2,3},{3,2},{4,5},{5,4},{6,7},{7,6},{8,9},{9,8},{10,11... | collective-permute-start | bytes 9437192 | tf_op jit(solution)/shard_map/ppermute | solution.py:604
  131.1 31.6 %attention_forward.1 = (bf16[512,1024]{1,0:T(8,128)(2,1)S(1)}, bf16[512,1024]{1,0:T(8,128)(2,1)S(1)}, bf16[512,2048]{1,0:T(8,128)(2,1)}, bf16[512,1024]{1,0:T(8,...) custom-call(bf16[512,1024]{1,0:T(8,128)(2,1)} %bitcast.refs_0_, ...), custom_call_target="tpu_custom_call" | custom-call | flops 10000000000 | bytes 31457280 | tf_op jit(solution)/shard_map/attention_forward/pallas_call | solution.py:135
  175.3 17.3 %deal_cotangent.1 = (bf16[2048,1024]{1,0:T(8,128)(2,1)}, bf16[512,1024]{1,0:T(8,128)(2,1)S(1)}, f32[2048,128]{1,0:T(8,128)S(1)}, f32[128,2048]{1,0:T(8,128)S(1)}, f32[2048,128]{1,0:T(8,128)S(1)}) custom-call(bf16[512,1024]{1,0:T(8,128)(2,1)S(1)} %bitcast.144, bf16[512,1024]{1,0:T(8,128)(2,1)S(1)} %copy-done.8, ...), custom_call_target="tpu_custom_call" | custom-call | flops 8999999488 | bytes 20971520 | tf_op jit(solution)/shard_map/deal_cotangent/pallas_call | solution.py:195
  195.5 25.4 %collective-permute-done.11.refs_2_ = bf16[512,1024]{1,0:T(8,128)(2,1)} collective-permute-done((bf16[512,1024]{1,0:T(8,128)(2,1)}, bf16[512,1024]{1,0:T(8,128)(2,1)}, u32[]{:S(2)}, u32[]{:S(2)}) %collective-permute-start.11) | collective-permute-done | bytes 1048608 | tf_op jit(solution)/shard_map/ppermute | solution.py:604
  220.9 4.8 router.1
  226.5 53.7 %experts.4 = (bf16[8,2,3,128,512]{4,3,2,1,0:T(8,128)(2,1)}, f32[2,2048,1024]{2,1,0:T(8,128)}, f32[2048,128]{1,0:T(8,128)}) custom-call(bf16[512,1024]{1,0:T(8,128)(2,1)} %get-tuple-element.45.refs_0_.refs_10_, bf16[512,1024]{1,0:T(8,128)(2,1)} %collective-permute-done.10.refs_1_, bf16[512,1024]{1,0:T(8,128)(2,1)} %collective-permute-done.11.refs_2_, ...), custom_call_target="tpu_custom_call" | custom-call | flops 28000000000 | bytes 41943040 | tf_op jit(solution)/shard_map/experts/pallas_call | solution.py:429
  280.3 53.5 %experts.5 = (bf16[8,2,3,128,512]{4,3,2,1,0:T(8,128)(2,1)}, f32[2,2048,1024]{2,1,0:T(8,128)}, f32[2048,128]{1,0:T(8,128)}) custom-call(bf16[512,1024]{1,0:T(8,128)(2,1)} %get-tuple-element.45.refs_0_.refs_10_, bf16[512,1024]{1,0:T(8,128)(2,1)} %collective-permute-done.10.refs_1_, ...), custom_call_target="tpu_custom_call", output_to_operand_aliasing={{1}: (9, {}), {2}: (10, {})} | custom-call | flops 28000000000 | bytes 41943040 | tf_op jit(solution)/shard_map/experts/pallas_call | solution.py:429
  333.9 53.1 %experts.6 = (bf16[8,2,3,128,512]{4,3,2,1,0:T(8,128)(2,1)}, f32[2,2048,1024]{2,1,0:T(8,128)}, f32[2048,128]{1,0:T(8,128)}) custom-call(bf16[512,1024]{1,0:T(8,128)(2,1)} %get-tuple-element.45.refs_0_.refs_10_, bf16[512,1024]{1,0:T(8,128)(2,1)} %collective-permute-done.10.refs_1_, ...), custom_call_target="tpu_custom_call", output_to_operand_aliasing={{1}: (9, {}), {2}: (10, {})} | custom-call | flops 28000000000 | bytes 41943040 | tf_op jit(solution)/shard_map/experts/pallas_call | solution.py:429
  387.1 50.9 %experts.7 = (bf16[8,2,3,128,512]{4,3,2,1,0:T(8,128)(2,1)}, bf16[2,2048,1024]{2,1,0:T(8,128)(2,1)}, f32[2048,128]{1,0:T(8,128)}) custom-call(bf16[512,1024]{1,0:T(8,128)(2,1)} %get-tuple-element.45.refs_0_.refs_10_, bf16[512,1024]{1,0:T(8,128)(2,1)} %collective-permute-done.10.refs_1_, bf16[512,1024]{1,0:T(8,128)(2,1)} %collective-permute-done.11.refs_2_, ...), custom_call_target="tpu_custom_call" | custom-call | flops 28000000000 | bytes 41943040 | tf_op jit(solution)/shard_map/experts/pallas_call | solution.py:429
  438.8 4.0 slice_bitcast_fusion.6
  447.7 49.1 %collective-permute-done.29.refs_5_ = f32[512,128]{1,0:T(8,128)S(1)} collective-permute-done((f32[512,128]{1,0:T(8,128)S(1)}, f32[512,128]{1,0:T(8,128)S(1)}, u32[]{:S(2)}, u32[]{:S(2)}) %collective-permute-start.29) | collective-permute-done | bytes 262176 | tf_op jit(solution)/shard_map/ppermute | solution.py:604
  498.3 6.4 collective-permute-done.31.refs_7_
  504.6 44.8 %attention_backward.1 = (bf16[512,1024]{1,0:T(8,128)(2,1)}, bf16[4,1024,512]{2,1,0:T(8,128)(2,1)}, bf16[4,1024,256]{2,1,0:T(8,128)(2,1)}, f32[1024,128]{1,0:T(8,128)}, f32[2,1024]{1,0:T(2,128)}) custom-call(bf16[512,1024]{1,0:T(8,128)(2,1)} %get-tuple-element.61.refs_0_, bf16[512,1024]{1,0:T(8,128)(2,1)} %collective-permute-done.27.refs_1_, ...), custom_call_target="tpu_custom_call" | custom-call | flops 20000000000 | bytes 41943040 | tf_op jit(solution)/shard_map/attention_backward/pallas_call | solution.py:556
  570.7 18.3 %collective-permute-done.21 = bf16[512,1024]{1,0:T(8,128)(2,1)S(1)} collective-permute-done((bf16[512,1024]{1,0:T(8,128)(2,1)}, bf16[512,1024]{1,0:T(8,128)(2,1)S(1)}, u32[]{:S(2)}, u32[]{:S(2)}) %collective-permute-start.21) | collective-permute-done | bytes 1048608 | tf_op jit(solution)/shard_map/ppermute | solution.py:604
  589.0 22.3 %collective-permute-done.22 = bf16[512,1024]{1,0:T(8,128)(2,1)} collective-permute-done((bf16[512,1024]{1,0:T(8,128)(2,1)}, bf16[512,1024]{1,0:T(8,128)(2,1)}, u32[]{:S(2)}, u32[]{:S(2)}) %collective-permute-start.22) | collective-permute-done | bytes 1048608 | tf_op jit(solution)/shard_map/ppermute | solution.py:604
  623.7 5.2 fusion
  630.5 8.9 %collective-permute-done.24.refs_1_ = bf16[512,1024]{1,0:T(8,128)(2,1)S(1)} collective-permute-done((bf16[512,1024]{1,0:T(8,128)(2,1)S(1)}, bf16[512,1024]{1,0:T(8,128)(2,1)S(1)}, u32[]{:S(2)}, u32[]{:S(2)}) %collective-permute-start.24) | collective-permute-done | bytes 1048608 | tf_op jit(solution)/shard_map/ppermute | solution.py:604
  639.4 22.8 %collective-permute-done.26.refs_3_ = bf16[512,1024]{1,0:T(8,128)(2,1)S(1)} collective-permute-done((bf16[512,1024]{1,0:T(8,128)(2,1)S(1)}, bf16[512,1024]{1,0:T(8,128)(2,1)S(1)}, u32[]{:S(2)}, u32[]{:S(2)}) %collective-permute-start.26) | collective-permute-done | bytes 1048608 | tf_op jit(solution)/shard_map/ppermute | solution.py:604
  665.5 5.5 collective-permute-start.40
  678.1 8.8 %collective-permute-start.44 = (f32[34,1024]{1,0:T(8,128)S(1)}, f32[34,1024]{1,0:T(8,128)S(1)}, u32[]{:S(2)}, u32[]{:S(2)}) collective-permute-start(f32[34,1024]{1,0:T(8,128)S(1)} %add_add_fusion.1), channel_id=1, source_target_pairs={{0,7},{1,6},{2,5},{3,4},{4,3},{5,2},{6,1},{7,0},{8,15},{9,14},{10,... | collective-permute-start | bytes 417800 | tf_op jit(solution)/shard_map/ppermute | solution.py:604
  689.6 9.7 %collective-permute-done.43 = f32[34,1024]{1,0:T(8,128)S(1)} collective-permute-done((f32[34,1024]{1,0:T(8,128)S(1)}, f32[34,1024]{1,0:T(8,128)S(1)}, u32[]{:S(2)}, u32[]{:S(2)}) %collective-permute-start.43) | collective-permute-done | bytes 139296 | tf_op jit(solution)/shard_map/ppermute | solution.py:604
  713.7 6.6 collective-permute-done.48
  723.3 30.8 %collective-permute-start.49 = (bf16[128,768]{1,0:T(8,128)(2,1)}, bf16[128,768]{1,0:T(8,128)(2,1)}, u32[]{:S(2)}, u32[]{:S(2)}) collective-permute-start(bf16[128,768]{1,0:T(8,128)(2,1)} %get-tuple-element.159), channel_id=1, source_target_pairs={{0,2},{1,3},{2,0},{3,1},{4,6},{5,7},{6,4},{7,5},{8,10},{9,11},{10,... | collective-permute-start | bytes 589832 | tf_op jit(solution)/shard_map/ppermute | solution.py:604
  754.2 5.8 collective-permute-start.50
  761.9 4.2 collective-permute-done.33.refs_2_
  766.1 4.9 to_given_order.3
  772.6 4.2 collective-permute-done.51
  (296 shorter events, 153.3 us)
Async XLA Ops:
  7.2 219.4 %all-gather.15.cloned.1.call-start = ((), (), s32[]{:S(2)}) async-start(), calls=%async_computation.11 | async-start | bytes 7077888 | tf_op jit(solution)/shard_map/all_gather | solution.py:650
  13.2 267.2 %all-gather.13.cloned.1.call-start = ((), (), s32[]{:S(2)}) async-start(), calls=%async_computation.10 | async-start | bytes 7077888 | tf_op jit(solution)/shard_map/all_gather | solution.py:650
  13.9 320.0 %all-gather.11.cloned.1.call-start = ((), (), s32[]{:S(2)}) async-start(), calls=%async_computation.9 | async-start | bytes 7077888 | tf_op jit(solution)/shard_map/all_gather | solution.py:650
  14.6 372.5 %all-gather.9.cloned.1.call-start = ((), (), s32[]{:S(2)}) async-start(), calls=%async_computation.8 | async-start | bytes 7077888 | tf_op jit(solution)/shard_map/all_gather | solution.py:650
  18.3 479.9 %reduce-scatter.5.cloned.1.call-start = ((), (), s32[]{:S(2)}) async-start(), calls=%async_computation.4 | async-start | bytes 7077888 | tf_op jit(solution)/shard_map/reduce_scatter | solution.py:739
  46.0 55.8 %collective-permute-start.16 = (bf16[128,32]{0,1:T(8,128)(2,1)S(1)}, bf16[128,32]{0,1:T(8,128)(2,1)S(1)}, u32[]{:S(2)}, u32[]{:S(2)}) collective-permute-start(bf16[128,32]{0,1:T(8,128)(2,1)S(1)} %copy-done.49), channel_id=1, source_target_pairs={{0,2},{1,3},{2,0},{3,1},{4,6},{5,7},{6,4},{7,5},{8,10},{9,11},{10,... | collective-permute-start | bytes 24584 | tf_op jit(solution)/shard_map/ppermute | solution.py:604
  47.9 55.2 %collective-permute-start.17 = (bf16[128,32]{0,1:T(8,128)(2,1)S(1)}, bf16[128,32]{0,1:T(8,128)(2,1)S(1)}, u32[]{:S(2)}, u32[]{:S(2)}) collective-permute-start(bf16[128,32]{0,1:T(8,128)(2,1)S(1)} %copy-done.49), channel_id=1, source_target_pairs={{0,4},{1,5},{2,6},{3,7},{4,0},{5,1},{6,2},{7,3},{8,12},{9,13},{10,... | collective-permute-start | bytes 24584 | tf_op jit(solution)/shard_map/ppermute | solution.py:604
  56.3 47.4 %collective-permute-start.18 = (bf16[128,32]{0,1:T(8,128)(2,1)S(1)}, bf16[128,32]{0,1:T(8,128)(2,1)S(1)}, u32[]{:S(2)}, u32[]{:S(2)}) collective-permute-start(bf16[128,32]{0,1:T(8,128)(2,1)S(1)} %copy-done.49), channel_id=1, source_target_pairs={{0,6},{1,7},{2,4},{3,5},{4,2},{5,3},{6,0},{7,1},{8,14},{9,15},{10,... | collective-permute-start | bytes 24584 | tf_op jit(solution)/shard_map/ppermute | solution.py:604
  57.1 57.3 %collective-permute-start.2 = (bf16[512,1024]{1,0:T(8,128)(2,1)}, bf16[512,1024]{1,0:T(8,128)(2,1)}, u32[]{:S(2)}, u32[]{:S(2)}) collective-permute-start(bf16[512,1024]{1,0:T(8,128)(2,1)} %bitcast.refs_0_), channel_id=1, source_target_pairs={{0,24},{8,16},{16,8},{24,0},{1,25},{9,17},{17,9},{25,1},{2,26},{10... | collective-permute-start | bytes 3145736 | tf_op jit(solution)/shard_map/ppermute | solution.py:604
  114.4 52.5 %collective-permute-start.13 = (bf16[512,1024]{1,0:T(8,128)(2,1)}, bf16[512,1024]{1,0:T(8,128)(2,1)S(1)}, u32[]{:S(2)}, u32[]{:S(2)}) collective-permute-start(bf16[512,1024]{1,0:T(8,128)(2,1)} %bitcast.141), channel_id=1, source_target_pairs={{0,8},{8,0},{16,24},{24,16},{1,9},{9,1},{17,25},{25,17},{2,10},{10... | collective-permute-start | bytes 3145736 | tf_op jit(solution)/shard_map/ppermute | solution.py:604
  114.5 58.3 %collective-permute-start.14 = (bf16[512,1024]{1,0:T(8,128)(2,1)}, bf16[512,1024]{1,0:T(8,128)(2,1)}, u32[]{:S(2)}, u32[]{:S(2)}) collective-permute-start(bf16[512,1024]{1,0:T(8,128)(2,1)} %bitcast.142), channel_id=1, source_target_pairs={{0,16},{8,24},{16,0},{24,8},{1,17},{9,25},{17,1},{25,9},{2,18},{10... | collective-permute-start | bytes 3145736 | tf_op jit(solution)/shard_map/ppermute | solution.py:604
  115.6 57.2 %collective-permute-start.15 = (bf16[512,1024]{1,0:T(8,128)(2,1)}, bf16[512,1024]{1,0:T(8,128)(2,1)}, u32[]{:S(2)}, u32[]{:S(2)}) collective-permute-start(bf16[512,1024]{1,0:T(8,128)(2,1)} %bitcast.143), channel_id=1, source_target_pairs={{0,24},{8,16},{16,8},{24,0},{1,25},{9,17},{17,9},{25,1},{2,26},{10... | collective-permute-start | bytes 3145736 | tf_op jit(solution)/shard_map/ppermute | solution.py:604
  165.6 55.3 %collective-permute-start.11 = (bf16[512,1024]{1,0:T(8,128)(2,1)}, bf16[512,1024]{1,0:T(8,128)(2,1)}, u32[]{:S(2)}, u32[]{:S(2)}) collective-permute-start(bf16[512,1024]{1,0:T(8,128)(2,1)} %get-tuple-element.45.refs_0_.refs_10_), channel_id=1, source_target_pairs={{0,16},{8,24},{16,0},{24,8},{1,17},{9,25},{17,1},{25,9},{2,18},{10... | collective-permute-start | bytes 3145736 | tf_op jit(solution)/shard_map/ppermute | solution.py:604
  167.9 53.0 %collective-permute-start.12 = (bf16[512,1024]{1,0:T(8,128)(2,1)}, bf16[512,1024]{1,0:T(8,128)(2,1)}, u32[]{:S(2)}, u32[]{:S(2)}) collective-permute-start(bf16[512,1024]{1,0:T(8,128)(2,1)} %get-tuple-element.45.refs_0_.refs_10_), channel_id=1, source_target_pairs={{0,24},{8,16},{16,8},{24,0},{1,25},{9,17},{17,9},{25,1},{2,26},{10... | collective-permute-start | bytes 3145736 | tf_op jit(solution)/shard_map/ppermute | solution.py:604
  280.3 385.3 %reduce-scatter.7.cloned.1.call-start = ((), (), s32[]{:S(2)}) async-start(), calls=%async_computation.5 | async-start | bytes 7077888 | tf_op jit(solution)/shard_map/reduce_scatter | solution.py:739
  333.9 339.8 %reduce-scatter.11.cloned.1.call-start = ((), (), s32[]{:S(2)}) async-start(), calls=%async_computation.7 | async-start | bytes 7077888 | tf_op jit(solution)/shard_map/reduce_scatter | solution.py:739
  438.1 235.6 %reduce-scatter.9.cloned.1.call-start = ((), (), s32[]{:S(2)}) async-start(), calls=%async_computation.6 | async-start | bytes 7077888 | tf_op jit(solution)/shard_map/reduce_scatter | solution.py:739
  442.8 61.8 %collective-permute-start.20 = (bf16[512,1024]{1,0:T(8,128)(2,1)}, bf16[512,1024]{1,0:T(8,128)(2,1)}, u32[]{:S(2)}, u32[]{:S(2)}) collective-permute-start(bf16[512,1024]{1,0:T(8,128)(2,1)} %get-tuple-element.135), channel_id=1, source_target_pairs={{0,24},{8,16},{16,8},{24,0},{1,25},{9,17},{17,9},{25,1},{2,26},{10... | collective-permute-start | bytes 3145736 | tf_op jit(solution)/shard_map/ppermute | solution.py:604
  442.8 61.8 %collective-permute-start.27 = (bf16[512,1024]{1,0:T(8,128)(2,1)S(1)}, bf16[512,1024]{1,0:T(8,128)(2,1)}, u32[]{:S(2)}, u32[]{:S(2)}) collective-permute-start(bf16[512,1024]{1,0:T(8,128)(2,1)S(1)} %get-tuple-element.133), channel_id=1, source_target_pairs={{0,8},{8,0},{16,24},{24,16},{1,9},{9,1},{17,25},{25,17},{2,10},{10... | collective-permute-start | bytes 3145736 | tf_op jit(solution)/shard_map/ppermute | solution.py:604
  445.4 59.3 %collective-permute-start.28 = (bf16[512,1024]{1,0:T(8,128)(2,1)S(1)}, bf16[512,1024]{1,0:T(8,128)(2,1)}, u32[]{:S(2)}, u32[]{:S(2)}) collective-permute-start(bf16[512,1024]{1,0:T(8,128)(2,1)S(1)} %get-tuple-element.132), channel_id=1, source_target_pairs={{0,16},{8,24},{16,0},{24,8},{1,17},{9,25},{17,1},{25,9},{2,18},{10... | collective-permute-start | bytes 3145736 | tf_op jit(solution)/shard_map/ppermute | solution.py:604
  446.4 50.5 %collective-permute-start.29 = (f32[512,128]{1,0:T(8,128)S(1)}, f32[512,128]{1,0:T(8,128)S(1)}, u32[]{:S(2)}, u32[]{:S(2)}) collective-permute-start(f32[512,128]{1,0:T(8,128)S(1)} %get-tuple-element.157), channel_id=1, source_target_pairs={{0,8},{8,0},{16,24},{24,16},{1,9},{9,1},{17,25},{25,17},{2,10},{10... | collective-permute-start | bytes 786440 | tf_op jit(solution)/shard_map/ppermute | solution.py:604
  446.5 51.7 %collective-permute-start.30 = (f32[512,128]{1,0:T(8,128)}, f32[512,128]{1,0:T(8,128)}, u32[]{:S(2)}, u32[]{:S(2)}) collective-permute-start(f32[512,128]{1,0:T(8,128)} %get-tuple-element.156), channel_id=1, source_target_pairs={{0,16},{8,24},{16,0},{24,8},{1,17},{9,25},{17,1},{25,9},{2,18},{10... | collective-permute-start | bytes 786440 | tf_op jit(solution)/shard_map/ppermute | solution.py:604
  556.4 64.9 %collective-permute-start.45 = (bf16[4,4,128,768]{3,2,1,0:T(8,128)(2,1)}, bf16[4,4,128,768]{3,2,1,0:T(8,128)(2,1)}, u32[]{:S(2)}, u32[]{:S(2)}) collective-permute-start(bf16[4,4,128,768]{3,2,1,0:T(8,128)(2,1)} %select_bitcast_fusion), channel_id=1, source_target_pairs={{0,1},{1,0},{2,3},{3,2},{4,5},{5,4},{6,7},{7,6},{8,9},{9,8},{10,11... | collective-permute-start | bytes 9437192 | tf_op jit(solution)/shard_map/ppermute | solution.py:604
  563.9 47.4 %collective-permute-start.22 = (bf16[512,1024]{1,0:T(8,128)(2,1)}, bf16[512,1024]{1,0:T(8,128)(2,1)}, u32[]{:S(2)}, u32[]{:S(2)}) collective-permute-start(bf16[512,1024]{1,0:T(8,128)(2,1)} %get-tuple-element.147), channel_id=1, source_target_pairs={{0,16},{8,24},{16,0},{24,8},{1,17},{9,25},{17,1},{25,9},{2,18},{10... | collective-permute-start | bytes 3145736 | tf_op jit(solution)/shard_map/ppermute | solution.py:604
  564.5 46.8 %collective-permute-start.23 = (bf16[512,1024]{1,0:T(8,128)(2,1)}, bf16[512,1024]{1,0:T(8,128)(2,1)}, u32[]{:S(2)}, u32[]{:S(2)}) collective-permute-start(bf16[512,1024]{1,0:T(8,128)(2,1)} %get-tuple-element.146), channel_id=1, source_target_pairs={{0,24},{8,16},{16,8},{24,0},{1,25},{9,17},{17,9},{25,1},{2,26},{10... | collective-permute-start | bytes 3145736 | tf_op jit(solution)/shard_map/ppermute | solution.py:604
  619.8 51.1 %collective-permute-start.38 = (f32[34,1024]{1,0:T(8,128)S(1)}, f32[34,1024]{1,0:T(8,128)S(1)}, u32[]{:S(2)}, u32[]{:S(2)}) collective-permute-start(f32[34,1024]{1,0:T(8,128)S(1)} %add_add_fusion.1), channel_id=1, source_target_pairs={{0,1},{1,0},{2,3},{3,2},{4,5},{5,4},{6,7},{7,6},{8,9},{9,8},{10,11... | collective-permute-start | bytes 417800 | tf_op jit(solution)/shard_map/ppermute | solution.py:604
  621.3 52.2 %collective-permute-start.39 = (f32[34,1024]{1,0:T(8,128)S(1)}, f32[34,1024]{1,0:T(8,128)S(1)}, u32[]{:S(2)}, u32[]{:S(2)}) collective-permute-start(f32[34,1024]{1,0:T(8,128)S(1)} %add_add_fusion.1), channel_id=1, source_target_pairs={{0,2},{1,3},{2,0},{3,1},{4,6},{5,7},{6,4},{7,5},{8,10},{9,11},{10,... | collective-permute-start | bytes 417800 | tf_op jit(solution)/shard_map/ppermute | solution.py:604
  639.4 69.6 %collective-permute-start.46 = (bf16[4,128,768]{2,1,0:T(8,128)(2,1)}, bf16[4,128,768]{2,1,0:T(8,128)(2,1)}, u32[]{:S(2)}, u32[]{:S(2)}) collective-permute-start(bf16[4,128,768]{2,1,0:T(8,128)(2,1)} %get-tuple-element.148), channel_id=1, source_target_pairs={{0,8},{8,0},{16,24},{24,16},{1,9},{9,1},{17,25},{25,17},{2,10},{10... | collective-permute-start | bytes 2359304 | tf_op jit(solution)/shard_map/ppermute | solution.py:604
  676.4 83.7 %collective-permute-start.32 = (bf16[512,1024]{1,0:T(8,128)(2,1)S(1)}, bf16[512,1024]{1,0:T(8,128)(2,1)S(1)}, u32[]{:S(2)}, u32[]{:S(2)}) collective-permute-start(bf16[512,1024]{1,0:T(8,128)(2,1)S(1)} %copy-done.6), channel_id=1, source_target_pairs={{0,8},{8,0},{16,24},{24,16},{1,9},{9,1},{17,25},{25,17},{2,10},{10... | collective-permute-start | bytes 3145736 | tf_op jit(solution)/shard_map/ppermute | solution.py:604
  708.1 58.0 %collective-permute-start.33 = (bf16[512,1024]{1,0:T(8,128)(2,1)S(1)}, bf16[512,1024]{1,0:T(8,128)(2,1)S(1)}, u32[]{:S(2)}, u32[]{:S(2)}) collective-permute-start(bf16[512,1024]{1,0:T(8,128)(2,1)S(1)} %copy-done.6), channel_id=1, source_target_pairs={{0,16},{8,24},{16,0},{24,8},{1,17},{9,25},{17,1},{25,9},{2,18},{10... | collective-permute-start | bytes 3145736 | tf_op jit(solution)/shard_map/ppermute | solution.py:604
  709.0 57.1 %collective-permute-start.34 = (bf16[512,1024]{1,0:T(8,128)(2,1)S(1)}, bf16[512,1024]{1,0:T(8,128)(2,1)}, u32[]{:S(2)}, u32[]{:S(2)}) collective-permute-start(bf16[512,1024]{1,0:T(8,128)(2,1)S(1)} %copy-done.6), channel_id=1, source_target_pairs={{0,24},{8,16},{16,8},{24,0},{1,25},{9,17},{17,9},{25,1},{2,26},{10... | collective-permute-start | bytes 3145736 | tf_op jit(solution)/shard_map/ppermute | solution.py:604
  723.3 47.7 %collective-permute-start.49 = (bf16[128,768]{1,0:T(8,128)(2,1)}, bf16[128,768]{1,0:T(8,128)(2,1)}, u32[]{:S(2)}, u32[]{:S(2)}) collective-permute-start(bf16[128,768]{1,0:T(8,128)(2,1)} %get-tuple-element.159), channel_id=1, source_target_pairs={{0,2},{1,3},{2,0},{3,1},{4,6},{5,7},{6,4},{7,5},{8,10},{9,11},{10,... | collective-permute-start | bytes 589832 | tf_op jit(solution)/shard_map/ppermute | solution.py:604
  (82 other events, 1231.6 us)
Sparse Core Ops, SparseCore 0:
  13.3 72.0 all-gather.14
  87.0 65.8 all-gather.12
  154.6 63.5 all-gather.10
  219.6 63.3 all-gather.8
  285.2 68.7 reduce-scatter.4
  356.2 68.1 reduce-scatter.6
  438.2 69.5 reduce-scatter.10
  510.0 68.4 reduce-scatter.8

commit v2 on v1

v2 whole, which is shorter than its diff:
```python
import functools

import jax
import jax.numpy as jnp
from jax import lax
from jax.experimental import pallas as pl
from jax.experimental.pallas import tpu as pltpu
from jax.sharding import PartitionSpec as P

HEAD_WIDTH = 64
QUERY_HEADS = 16
KEY_VALUE_HEADS = 8
EXPERT_COUNT = 32
TOPK = 8
EPSILON = 1e-06
RESIDUAL_SCALE = 0.22
SCORE_SCALE = 0.015625
ROPE_BASE = 10000.0
MASKED = -1e30
LANES = 128
MIB = 1024 * 1024
BF = jnp.bfloat16
F32 = jnp.float32
ANY = pl.BlockSpec(memory_space=pl.ANY)
FULL = pl.BlockSpec(memory_space=pltpu.VMEM)


def mm(a, b):
    return lax.dot_general(a, b, (((1,), (0,)), ((), ())), preferred_element_type=F32)


def mm_nt(a, b):
    return lax.dot_general(a, b, (((1,), (1,)), ((), ())), preferred_element_type=F32)


def mm_tn(a, b):
    return lax.dot_general(a, b, (((0,), (0,)), ((), ())), preferred_element_type=F32)


def iota(shape, dim):
    return lax.broadcasted_iota(jnp.int32, shape, dim)


def params(mib):
    return pltpu.CompilerParams(vmem_limit_bytes=mib * MIB)


def cost(flops, moved):
    return pl.CostEstimate(flops=int(flops), bytes_accessed=int(moved), transcendentals=0)


def row_scale(values):
    return lax.rsqrt(jnp.mean(values * values, axis=-1, keepdims=True) + EPSILON)


def swap_halves(values):
    width = values.shape[-1]
    half = HEAD_WIDTH // 2
    low = (iota(values.shape, 1) % HEAD_WIDTH) < half
    ahead = pltpu.roll(values, width - half, 1)
    behind = pltpu.roll(values, half, 1)
    return jnp.where(low, ahead, behind)


def masked_probs(q, k, row0, starts):
    rows, cols = q.shape[0], k.shape[0]
    scores = mm_nt(q, k) * SCORE_SCALE
    at = iota((rows, cols), 1)
    allowed = (at <= iota((rows, cols), 0) + row0) & (at >= starts)
    scores = jnp.where(allowed, scores, MASKED)
    top = jnp.max(scores, axis=-1, keepdims=True)
    raised = jnp.exp(scores - top)
    total = jnp.sum(raised, axis=-1, keepdims=True)
    return raised * (1.0 / total)


def link(src, dst, sems, index, device):
    return pltpu.make_async_remote_copy(
        src_ref=src,
        dst_ref=dst,
        send_sem=sems.at[0, index],
        recv_sem=sems.at[1, index],
        device_id=device,
        device_id_type=pl.DeviceIdType.MESH,
    )


def greet(devices):
    barrier = pltpu.get_barrier_semaphore()
    for device in devices:
        pl.semaphore_signal(barrier, inc=1, device_id=device, device_id_type=pl.DeviceIdType.MESH)
    pl.semaphore_wait(barrier, len(devices))


class RowGather:
    count = 6

    def __init__(self, own, slot, sems, base, r, c):
        near, far = (r ^ 1, c), (r ^ 2, c)
        self.copies = {
            (1, 1): link(own(1), slot(1, 1), sems, base, near),
            (2, 0): link(own(0), slot(2, 0), sems, base + 1, far),
            (1, 0): link(own(0), slot(1, 0), sems, base + 2, near),
            (2, 1): link(own(1), slot(2, 1), sems, base + 3, far),
            (3, 0): link(slot(2, 0), slot(3, 0), sems, base + 4, near),
            (3, 1): link(slot(1, 1), slot(3, 1), sems, base + 5, far),
        }

    def start(self, half):
        order = ((2, 0), (1, 0)) if half == 0 else ((1, 1), (2, 1))
        for key in order:
            self.copies[key].start()

    def forward(self, half):
        self.copies[(2, 0) if half == 0 else (1, 1)].wait_recv()
        self.copies[(3, half)].start()

    def wait(self, *keys):
        for key in keys:
            self.copies[key].wait_recv()

    def drain(self):
        for copy in self.copies.values():
            copy.wait_send()


def front_kernel(
    xin,
    cot,
    w_own,
    src,
    starts,
    cos,
    sin,
    gain_a,
    gain_m,
    ids,
    spots,
    src_row,
    xd,
    attn,
    qkv,
    mixed,
    middle,
    moe_all,
    dsum,
    dy,
    slot_cols,
    slot_rows,
    chosen,
    w_att,
    moe,
    slot_given,
    mid16,
    xb,
    cb,
    sems,
    local_sems,
):
    nblk, tokens, width = xb.shape
    half = tokens // 2
    pairs = w_att.shape[1]
    qw = w_att.shape[4] * 2 // 3
    rank = w_att.shape[1] * 2 * w_att.shape[3]
    r = lax.axis_index("row")
    c = lax.axis_index("col")
    z = c // 2
    k = c % 2
    others = [(r, 2 * (z ^ i) + k) for i in range(1, pairs)]
    sibling = (r, c ^ 1)
    greet([(r ^ 1, c), (r ^ 2, c), sibling] + others)

    def cut(ref):
        return lambda h: ref.at[pl.ds(h * half, half)]

    def cut_slot(ref):
        return lambda j, h: ref.at[j, pl.ds(h * half, half)]

    def w_slot(j, h):
        return w_att.at[j, pl.ds(h * (pairs // 2), pairs // 2), k]

    n = RowGather.count
    xs = RowGather(cut(xin), cut_slot(xb), sems, 0, r, c)
    ws = RowGather(lambda h: w_slot(0, h), w_slot, sems, n, r, c)
    cs = RowGather(cut(cot), cut_slot(cb), sems, 2 * n, r, c)
    ms = RowGather(cut(moe), cut_slot(moe_all), sems, 3 * n, r, c)
    across = [
        link(w_own, w_att.at[0, z, k], sems, 4 * n + i, others[i]) for i in range(pairs - 1)
    ]
    base = 4 * n + pairs - 1
    share = [link(w_att.at[j, :, k], w_att.at[j, :, k], sems, base + j, sibling) for j in range(nblk)]
    keep = [
        pltpu.make_async_copy(w_own, w_att.at[0, z, k], local_sems.at[0]),
        pltpu.make_async_copy(xin, xb.at[0], local_sems.at[1]),
        pltpu.make_async_copy(cot, cb.at[0], local_sems.at[2]),
    ]
    for copy in across:
        copy.start()
    xs.start(1)
    xs.start(0)
    for copy in keep:
        copy.start()
    keep[0].wait()
    for copy in across:
        copy.wait_recv()
    ws.start(1)
    ws.start(0)
    share[0].start()
    xs.forward(0)
    xs.forward(1)
    keep[1].wait()

    source = src[:tokens, :]

    def pick(at, j):
        return jnp.where(at == iota((tokens, tokens), 1) + j * tokens, 1.0, 0.0).astype(BF)

    x = mm(pick(source, 0), xb[0])
    xs.wait((1, 0))
    x = x + mm(pick(source, 1), xb[1])
    xs.wait((2, 1))
    x = x + mm(pick(source, 2), xb[2])
    ws.forward(0)
    ws.forward(1)
    ws.wait((1, 0), (2, 1))
    share[1].start()
    share[2].start()
    xs.wait((3, 0), (3, 1))
    x = x + mm(pick(source, 3), xb[3])
    xd[...] = x.astype(BF)
    attn[...] = (x * row_scale(x) * gain_a[...]).astype(BF)
    groups = qw // (4 * HEAD_WIDTH)

    def project(j):
        proj = mm(attn[...], w_att[j, :, :, :, :qw].reshape(rank, qw))
        cos_w = jnp.concatenate([cos[...]] * groups, axis=1)
        sin_w = jnp.concatenate([sin[...]] * groups, axis=1)
        turned = proj * cos_w + swap_halves(proj) * sin_w
        qkv[:, pl.ds(pl.multiple_of(j * qw, qw), qw)] = turned.astype(BF)

    ws.wait((3, 0), (3, 1))
    share[3].start()
    cs.start(1)
    cs.start(0)
    for j in range(nblk):
        share[j].wait_recv()

    @pl.loop(0, nblk)
    def _(j):
        project(j)

    pair = 2 * HEAD_WIDTH
    for b in range(2):
        rows = slice(b * half, (b + 1) * half)
        span = (b + 1) * half

        @pl.loop(0, groups * nblk)
        def _(g):
            chunk = qkv[:span, pl.ds(pl.multiple_of(g * 2 * pair, 2 * pair), 2 * pair)]
            k_rows = chunk[:, pair : pair + HEAD_WIDTH]
            v_rows = chunk[:, pair + HEAD_WIDTH :]
            outs = []
            for h in range(2):
                q = chunk[b * half :, h * HEAD_WIDTH : (h + 1) * HEAD_WIDTH]
                probs = masked_probs(q, k_rows, b * half, starts[rows, :])
                outs.append(mm(probs.astype(BF), v_rows))
            mixed[rows, pl.ds(pl.multiple_of(g * pair, pair), pair)] = jnp.concatenate(
                outs, axis=1
            ).astype(BF)

        if b == 1:
            cs.forward(0)
            cs.forward(1)
            ms.forward(0)
        ow = w_att.shape[4] - qw
        out = jnp.zeros((half, width), F32)
        for j in range(nblk):
            w_out = w_att[j, :, :, :, qw:].reshape(rank, ow)
            out = out + mm_nt(mixed[rows, j * ow : (j + 1) * ow], w_out)
        mid = xd[rows, :].astype(F32) + RESIDUAL_SCALE * out
        middle[rows, :] = mid
        mid16[rows, :] = mid.astype(BF)
        moe[rows, :] = (mid * row_scale(mid) * gain_m[...]).astype(BF)
        ms.start(b)

    place = pltpu.make_async_copy(moe, moe_all.at[0], local_sems.at[3])
    place.start()
    keep[2].wait()
    cs.wait((1, 0), (2, 1), (3, 0), (3, 1))

    def deal_block(b):
        at = pl.ds(pl.multiple_of(b * tokens, tokens), tokens)
        source = src[at, :]
        dealt = mm(pick(source, 0), cb[0])
        for j in range(1, nblk):
            dealt = dealt + mm(pick(source, j), cb[j])
        dsum[at, :] = (RESIDUAL_SCALE * dealt).astype(BF)

        @pl.when(b == 0)
        def _():
            dy[...] = dealt.astype(BF)

        lane = iota((tokens, LANES), 1)
        spot = jnp.zeros((tokens, LANES), F32)
        named = jnp.zeros((tokens, LANES), F32)
        own_ids = ids[at, :]
        own_spots = spots[at, :]
        for i in range(TOPK):
            hit = lane == own_ids[:, i : i + 1]
            named = jnp.where(hit, 1.0, named)
            spot = jnp.where(hit, own_spots[:, i : i + 1].astype(F32), spot)
        chosen[at, :] = named
        slot = jnp.where(named > 0.0, spot, -1.0)
        slot_cols[at, :] = slot
        slot_rows[:, at] = slot.T

    for part in range(2):

        @pl.loop(part * nblk // 2, (part + 1) * nblk // 2)
        def _(b):
            deal_block(b)

        if part == 0:
            ms.forward(1)

    @pl.loop(0, nblk)
    def _(b):
        at = pl.ds(pl.multiple_of(b * tokens, tokens), tokens)
        found = jnp.zeros((tokens, LANES), F32)
        for j in range(nblk):
            part = slice(j * tokens, (j + 1) * tokens)
            match = iota((tokens, tokens), 0) + b * tokens == src_row[:, part]
            match = jnp.where(match, 1.0, 0.0).astype(BF)
            value = slot_cols[part, :] + 1.0
            high = jnp.floor(value * 0.0625)
            low = value - 16.0 * high
            found = found + 16.0 * mm(match, high.astype(BF)) + mm(match, low.astype(BF))
        slot_given[at, :] = found - 1.0

    ms.wait((1, 0), (2, 1), (3, 0), (3, 1))
    place.wait()
    for gather in (xs, ws, cs, ms):
        gather.drain()
    for copy in across + share:
        copy.wait_send()


def front(xin, cot, w_own, src, starts, cos, sin, gain_a, gain_m, ids, spots, src_row, nblk, pairs):
    tokens, width = xin.shape
    shard, both = w_own.shape
    total = nblk * tokens
    qkv_width = nblk * both * 2 // 3
    head_width = nblk * both // 3
    shape = jax.ShapeDtypeStruct
    count = 4 * RowGather.count + pairs - 1 + nblk
    return pl.pallas_call(
        front_kernel,
        out_shape=(
            shape((tokens, width), BF),
            shape((tokens, width), BF),
            shape((tokens, qkv_width), BF),
            shape((tokens, head_width), BF),
            shape((tokens, width), F32),
            shape((nblk, tokens, width), BF),
            shape((total, width), BF),
            shape((tokens, width), BF),
            shape((total, LANES), F32),
            shape((LANES, total), F32),
            shape((total, LANES), F32),
            shape((nblk, pairs, 2, shard, both), BF),
            shape((tokens, width), BF),
            shape((total, LANES), F32),
            shape((tokens, width), BF),
        ),
        in_specs=[ANY] * 3 + [FULL] * 9,
        out_specs=[FULL] * 5 + [ANY] + [FULL] * 9,
        scratch_shapes=[
            pltpu.VMEM((nblk, tokens, width), BF),
            pltpu.VMEM((nblk, tokens, width), BF),
            pltpu.SemaphoreType.DMA((2, count)),
            pltpu.SemaphoreType.DMA((4,)),
        ],
        compiler_params=pltpu.CompilerParams(
            vmem_limit_bytes=58 * MIB, collective_id=1, has_side_effects=True
        ),
        cost_estimate=cost(20e9, 60 * MIB),
        name="attention_forward",
    )(xin, cot, w_own, src, starts, cos, sin, gain_a, gain_m, ids, spots, src_row)


def router_kernel(moe, w_router, chosen, gates, packed):
    nblk, tokens, _ = moe.shape
    local = EXPERT_COUNT // nblk
    for j in range(nblk):
        at = slice(j * tokens, (j + 1) * tokens)
        logits = mm(moe[j], w_router[...])
        named = chosen[at, :] > 0.0
        logits = jnp.where(named, logits, MASKED)
        top = jnp.max(logits, axis=-1, keepdims=True)
        raised = jnp.where(named, jnp.exp(logits - top), 0.0)
        gate = raised / jnp.sum(raised, axis=-1, keepdims=True)
        gates[at, :] = gate
        lane = iota((tokens, LANES), 1)
        own = jnp.where(lane < local, gate, 0.0)
        high = own.astype(BF).astype(F32)
        rest = own - high
        mid = rest.astype(BF).astype(F32)
        low = rest - mid
        packed[at, :] = (high + pltpu.roll(mid, local, 1) + pltpu.roll(low, 2 * local, 1)).astype(BF)


def router(moe, w_router, chosen):
    nblk, tokens, _ = moe.shape
    total = nblk * tokens
    shape = jax.ShapeDtypeStruct
    return pl.pallas_call(
        router_kernel,
        out_shape=(shape((total, LANES), F32), shape((total, LANES), BF)),
        in_specs=[FULL] * 3,
        out_specs=[FULL] * 2,
        compiler_params=params(24),
        cost_estimate=cost(1e9, 7 * MIB),
        name="router",
    )(moe, w_router, chosen)


def expert_kernel(base, first, last, local, capacity, *refs):
    moe_hbm = refs[0]
    refs = refs[1:]
    if first:
        (dsum_hbm, slot_rows, slot_cols, slot_given, packed, w) = refs[:6]
        refs = refs[6:]
    else:
        (dsum_hbm, slot_rows, slot_cols, slot_given, packed, w, acc_in, accg_in) = refs[:8]
        refs = refs[8:]
    if last:
        (grads, es_out, dm_out, dgates) = refs[:4]
        refs = refs[4:]
    else:
        (grads, acc_out, accg_out) = refs[:3]
        refs = refs[3:]
    (moe, dsum, acc, accg, sel, selt, routed, dsl, dslot, y1, y2, sems) = refs
    step = pl.program_id(0)
    steps = pl.num_programs(0)
    e = base + step
    nblk, tokens, width = moe_hbm.shape
    total = nblk * tokens
    fe = w.shape[4]
    shard = w.shape[3]
    tile = 256
    tiles = width // tile
    copies = []
    for j in range(nblk):
        copies.append(
            pltpu.make_async_copy(moe_hbm.at[j], moe.at[pl.ds(j * tokens, tokens)], sems.at[j])
        )
    copies.append(pltpu.make_async_copy(dsum_hbm, dsum, sems.at[nblk]))
    loads = []
    if not first:
        loads.append(pltpu.make_async_copy(acc_in, acc, sems.at[nblk + 1]))
        loads.append(pltpu.make_async_copy(accg_in, accg, sems.at[nblk + 2]))

    @pl.when(step == 0)
    def _():
        for c in copies:
            c.start()
        for c in loads:
            c.start()
        if first:
            acc[...] = jnp.zeros(acc.shape, F32)
            accg[...] = jnp.zeros(accg.shape, F32)

    row = slot_rows[pl.ds(e, 1), :]
    lanes = iota((tokens, LANES), 1)
    for j in range(nblk):
        at = slice(j * tokens, (j + 1) * tokens)
        sel[:, at] = jnp.where(
            iota((capacity, tokens), 0).astype(F32) == row[:, at], 1.0, 0.0
        ).astype(BF)
        col = jnp.sum(jnp.where(lanes == e, slot_cols[at, :], 0.0), axis=1, keepdims=True)
        selt[at, :] = jnp.where(
            col == iota((tokens, capacity), 1).astype(F32), 1.0, 0.0
        ).astype(BF)

    @pl.when(step == 0)
    def _():
        for c in copies:
            c.wait()

    def dispatch(n, carry):
        at = pl.ds(pl.multiple_of(n * tile, tile), tile)
        routed[:, at] = mm(sel[...], moe[:, at]).astype(BF)
        dsl[:, at] = mm(sel[...], dsum[:, at]).astype(BF)
        return carry

    lax.fori_loop(0, tiles, dispatch, 0)
    lane = iota((capacity, LANES), 1)
    picked = mm(sel[...], packed[...])
    mine = (lane == e) | (lane == e + local) | (lane == e + 2 * local)
    gate = jnp.sum(jnp.where(mine, picked, 0.0), axis=1, keepdims=True)
    dslot[...] = (gate * dsl[...].astype(F32)).astype(BF)

    def weight(i):
        return w[:, 0, i].reshape(width, fe)

    per = tile // shard

    def weight_tile(i, n):
        return w[pl.ds(n * per, per), 0, i].reshape(tile, fe)

    gate_in = mm(routed[...], weight(0))
    up_in = mm(routed[...], weight(1))
    sig = jax.nn.sigmoid(gate_in)
    silu = gate_in * sig
    hidden = (silu * up_in).astype(BF)

    def down(n, inner):
        at = pl.ds(pl.multiple_of(n * tile, tile), tile)
        out = mm_nt(hidden, weight_tile(2, n))
        y1[:, at] = (gate * out).astype(BF)
        return inner + jnp.sum(dsl[:, at].astype(F32) * out, axis=1, keepdims=True)

    inner = lax.fori_loop(0, tiles, down, jnp.zeros((capacity, 1), F32))
    high = inner.astype(BF).astype(F32)
    rest = inner - high
    mid = rest.astype(BF).astype(F32)
    low = rest - mid
    spread = jnp.where(
        lane == e,
        high,
        jnp.where(lane == e + local, mid, jnp.where(lane == e + 2 * local, low, 0.0)),
    ).astype(BF)
    dhidden = mm(dslot[...], weight(2))
    dgate = (dhidden * up_in * sig * (1.0 + gate_in * (1.0 - sig))).astype(BF)
    dup = (dhidden * silu).astype(BF)

    def back(n, carry):
        at = pl.ds(pl.multiple_of(n * tile, tile), tile)
        devs = pl.ds(n * per, per)
        grads[devs, 0, 2] = mm_tn(dslot[:, at], hidden).astype(BF).reshape(per, shard, fe)
        rows = routed[:, at]
        grads[devs, 0, 0] = mm_tn(rows, dgate).astype(BF).reshape(per, shard, fe)
        grads[devs, 0, 1] = mm_tn(rows, dup).astype(BF).reshape(per, shard, fe)
        y2[:, at] = (mm_nt(dgate, weight_tile(0, n)) + mm_nt(dup, weight_tile(1, n))).astype(BF)
        return carry

    lax.fori_loop(0, tiles, back, 0)

    if not first:

        @pl.when(step == 0)
        def _():
            for c in loads:
                c.wait()

    def combine(b, carry):
        at = pl.ds(pl.multiple_of(b * tokens, tokens), tokens)
        chosen = selt[at, :]
        acc[1, at, :] += mm(chosen, y2[...])
        accg[at, :] += mm(chosen, spread)
        col = jnp.sum(jnp.where(lanes == e, slot_given[at, :], 0.0), axis=1, keepdims=True)
        given = jnp.where(col == iota((tokens, capacity), 1).astype(F32), 1.0, 0.0).astype(BF)
        acc[0, at, :] += mm(given, y1[...])
        return carry

    lax.fori_loop(0, nblk, combine, 0)

    @pl.when(step == steps - 1)
    def _():
        if last:
            moe[...] = acc[0].astype(BF)
            dsum[...] = acc[1].astype(BF)
            summed = accg[...]
            summed = (
                summed
                + pltpu.roll(summed, LANES - local, 1)
                + pltpu.roll(summed, LANES - 2 * local, 1)
            )
            dgates[...] = summed.T[:local, :]
            outs = []
            for j in range(nblk):
                part = pl.ds(j * tokens, tokens)
                outs.append(pltpu.make_async_copy(moe.at[part], es_out.at[j], sems.at[2 * j]))
                outs.append(pltpu.make_async_copy(dsum.at[part], dm_out.at[j], sems.at[2 * j + 1]))
        else:
            outs = [
                pltpu.make_async_copy(acc, acc_out, sems.at[0]),
                pltpu.make_async_copy(accg, accg_out, sems.at[1]),
            ]
        for c in outs:
            c.start()
        for c in outs:
            c.wait()


def experts(moe, dsum, slot_rows, slot_cols, slot_given, packed, w, carried, base, last, capacity):
    nblk, tokens, width = moe.shape
    total = nblk * tokens
    cols, ne, three, shard, fe = w.shape
    local = EXPERT_COUNT // nblk
    first = carried is None
    shape = jax.ShapeDtypeStruct
    wspec = pl.BlockSpec((cols, 1, three, shard, fe), lambda s: (0, s, 0, 0, 0))
    ins = [moe, dsum, slot_rows, slot_cols, slot_given, packed, w]
    in_specs = [ANY] * 2 + [FULL, FULL, FULL, FULL, wspec]
    aliases = {}
    if not first:
        ins += list(carried)
        in_specs += [ANY, ANY]
        aliases = {} if last else {len(ins) - 2: 1, len(ins) - 1: 2}
    if last:
        blocks = shape((nblk, tokens, width), BF)
        outs = (blocks, blocks, shape((local, total), F32))
        out_specs = [wspec, ANY, ANY, FULL]
    else:
        outs = (shape((2, total, width), F32), shape((total, LANES), F32))
        out_specs = [wspec, ANY, ANY]
    return pl.pallas_call(
        functools.partial(expert_kernel, base, first, last, local, capacity),
        grid=(ne,),
        out_shape=(shape(w.shape, BF), *outs),
        in_specs=in_specs,
        out_specs=out_specs,
        scratch_shapes=[
            pltpu.VMEM((total, width), BF),
            pltpu.VMEM((total, width), BF),
            pltpu.VMEM((2, total, width), F32),
            pltpu.VMEM((total, LANES), F32),
            pltpu.VMEM((capacity, total), BF),
            pltpu.VMEM((total, capacity), BF),
            pltpu.VMEM((capacity, width), BF),
            pltpu.VMEM((capacity, width), BF),
            pltpu.VMEM((capacity, width), BF),
            pltpu.VMEM((capacity, width), BF),
            pltpu.VMEM((capacity, width), BF),
            pltpu.SemaphoreType.DMA((2 * nblk,)),
        ],
        input_output_aliases=aliases,
        compiler_params=params(60),
        cost_estimate=cost(14e9 * ne, 40 * MIB),
        name="experts",
    )(*ins)


class RowScatter:
    count = 6

    def __init__(self, block, mixed_in, across, landed, sems, base, r, c):
        near, far = (r ^ 1, c), (r ^ 2, c)
        self.copies = {
            "diag0": link(block(3, 0), across(0), sems, base, near),
            "diag1": link(block(3, 1), across(1), sems, base + 1, far),
            "near0": link(block(1, 0), landed(1, 0), sems, base + 2, near),
            "far1": link(block(2, 1), landed(2, 1), sems, base + 3, far),
            "far0": link(mixed_in(0), landed(2, 0), sems, base + 4, far),
            "near1": link(mixed_in(1), landed(1, 1), sems, base + 5, near),
        }

    def start(self):
        for key in ("diag0", "diag1", "near0", "far1"):
            self.copies[key].start()

    def arrived(self, half):
        self.copies["diag0" if half == 0 else "diag1"].wait_recv()

    def send(self, half):
        self.copies["far0" if half == 0 else "near1"].start()

    def finish(self):
        for key in ("near0", "far1", "far0", "near1"):
            self.copies[key].wait_recv()

    def drain(self):
        for copy in self.copies.values():
            copy.wait_send()


def tree_sum(parts):
    while len(parts) > 1:
        parts = [parts[i] + parts[i + 1] for i in range(0, len(parts), 2)]
    return parts[0]


def plus(a, b):
    return (a.astype(F32) + b.astype(F32)).astype(BF)


def back_kernel(nblk, *refs):
    dm, es, dgates = refs[:3]
    mids = refs[3 : 3 + nblk]
    refs = refs[3 + nblk :]
    (gates, middle, moe, dy, mixed, qkv, attn, xd, w_att, w_router) = refs[:10]
    (starts, cos, sin, gain_a, gain_m, src_row) = refs[10:16]
    (block_out, input_grad, att_grad, small, e_across, e_landed) = refs[16:22]
    (own, d_across, d_landed, dg_land, e_mix, e_load, igb, dmid, dmix, dproj, dkv, wg, wg_sib) = refs[22:35]
    (w_across, w_landed, w_z, rowsum, s_own, s_sib, s_sum, s_row, s_chip, s_z, sems, lsems) = refs[35:]
    tokens, width = xd.shape
    half = tokens // 2
    local = EXPERT_COUNT // nblk
    pairs = w_att.shape[1]
    shard = w_att.shape[3]
    qw = w_att.shape[4] * 2 // 3
    ow = w_att.shape[4] - qw
    hw = HEAD_WIDTH
    r = lax.axis_index("row")
    c = lax.axis_index("col")
    z = c // 2
    k = c % 2
    row_peers = [(r ^ j, c) for j in range(1, nblk)]
    z_peers = [(r, 2 * (z ^ i) + k) for i in range(1, pairs)]
    sibling = (r, c ^ 1)
    greet(row_peers + z_peers + [sibling])

    def part(h):
        return pl.ds(h * half, half)

    zhalf = pairs // 2

    def zpart(h):
        return pl.ds(h * zhalf, zhalf)

    n = RowScatter.count
    dms = RowScatter(
        lambda j, h: dm.at[j, part(h)],
        lambda h: own.at[2 - h, part(h)],
        lambda h: d_across.at[h],
        lambda j, h: d_landed.at[j - 1, part(h)],
        sems,
        0,
        r,
        c,
    )
    ess = RowScatter(
        lambda j, h: es.at[j, part(h)],
        lambda h: e_mix.at[h],
        lambda h: e_across.at[h],
        lambda j, h: e_landed.at[j - 1, part(h)],
        sems,
        n,
        r,
        c,
    )
    wgs = RowScatter(
        lambda j, h: wg.at[j, zpart(h), k],
        lambda h: wg.at[2 - h, zpart(h), k],
        lambda h: w_across.at[h],
        lambda j, h: w_landed.at[j - 1, zpart(h)],
        sems,
        2 * n,
        r,
        c,
    )
    igs = RowGather(
        lambda h: igb.at[0, part(h)], lambda j, h: igb.at[j, part(h)], sems, 3 * n, r, c
    )
    at = 3 * n + RowGather.count
    dgs = [
        link(dgates.at[:, pl.ds(j * tokens, tokens)], dg_land.at[j - 1], sems, at + j - 1, (r ^ j, c))
        for j in range(1, nblk)
    ]
    at += nblk - 1
    wg_share = [
        link(wg.at[j, :, 1 - k], wg_sib.at[j], sems, at + j, sibling) for j in range(nblk)
    ]
    at += nblk
    wg_z = [
        link(rowsum.at[z ^ i], w_z.at[i - 1], sems, at + i - 1, z_peers[i - 1])
        for i in range(1, pairs)
    ]
    at += pairs - 1
    s_share = link(s_own, s_sib, sems, at, sibling)
    s_rows = [link(s_sum, s_row.at[j], sems, at + 1 + j, row_peers[j]) for j in range(nblk - 1)]
    at += nblk
    s_zs = [link(s_chip, s_z.at[i], sems, at + i, z_peers[i]) for i in range(pairs - 1)]

    dms.start()
    for copy in dgs:
        copy.start()
    loads = [
        pltpu.make_async_copy(dm.at[0], own.at[0], lsems.at[0]),
        pltpu.make_async_copy(dm.at[1, part(1)], own.at[1, part(1)], lsems.at[1]),
        pltpu.make_async_copy(dm.at[2, part(0)], own.at[2, part(0)], lsems.at[2]),
        pltpu.make_async_copy(middle, dmid, lsems.at[3]),
    ]
    for copy in loads:
        copy.start()

    def match(j):
        hit = iota((tokens, tokens), 0) == src_row[:, j * tokens : (j + 1) * tokens]
        return jnp.where(hit, 1.0, 0.0).astype(BF)

    total = jnp.zeros((tokens, width), F32)
    for j in range(nblk):
        get = pltpu.make_async_copy(mids[j], dmix, lsems.at[4])
        get.start()
        hit = match(j)
        get.wait()
        total = total + mm(hit, dmix[...])
    input_grad[...] = total
    for copy in loads:
        copy.wait()
    for h in range(2):
        dms.arrived(h)
        rows = part(h)
        own[2 - h, rows, :] = plus(own[2 - h, rows, :], d_across[h])
        dms.send(h)

    for copy in dgs:
        copy.wait_recv()
    parts = [dgates[:, :tokens]] + [dg_land[j] for j in range(nblk - 1)]
    pad = jnp.zeros((LANES - EXPERT_COUNT, tokens), F32)
    dgate = jnp.concatenate(parts + [pad], axis=0).T
    gate = gates[...]
    dchosen = gate * (dgate - jnp.sum(gate * dgate, axis=1, keepdims=True))
    dlogits = dchosen.astype(BF)
    router_t = mm_tn(dlogits, moe[...])
    for j in range(nblk):
        s_own[pl.ds(pl.multiple_of((r ^ j) * local, local), local), :] = router_t[
            j * local : (j + 1) * local, :
        ]
    dmoe = mm_nt(dlogits, w_router[...]) + own[0].astype(F32)
    dms.finish()
    ess.start()
    dmoe = dmoe + (d_landed[0].astype(F32) + d_landed[1].astype(F32))
    mid = dmid[...]
    rr = row_scale(mid)
    scaled = dmoe * gain_m[...]
    inner = jnp.mean(scaled * mid, axis=-1, keepdims=True)
    gain_m_part = jnp.sum(dmoe * mid * rr, axis=0, keepdims=True)
    dmid[...] = dy[...].astype(F32) + (rr * scaled - mid * (rr * rr * rr) * inner)
    dattn = (RESIDUAL_SCALE * dmid[...]).astype(BF)
    for j in range(nblk):
        cols = slice(j * ow, (j + 1) * ow)
        dmix[:, cols] = mm(dattn, w_att[j, :, :, :, qw:].reshape(width, ow)).astype(BF)
        wg[j, :, :, :, qw:] = (
            mm_tn(dattn, mixed[:, cols]).astype(BF).reshape(pairs, 2, shard, ow)
        )

    quad = 4 * hw
    groups = nblk * qw // quad
    gain_a_part = jnp.zeros((1, width), F32)
    e_loads = [
        pltpu.make_async_copy(es.at[2, part(0)], e_mix.at[0], lsems.at[5]),
        pltpu.make_async_copy(es.at[1, part(1)], e_mix.at[1], lsems.at[6]),
    ]
    for copy in e_loads:
        copy.start()
    for b in (1, 0):
        span = (b + 1) * half
        rows = slice(b * half, (b + 1) * half)

        @pl.loop(0, groups)
        def _(g):
            chunk = qkv[:span, pl.ds(pl.multiple_of(g * quad, quad), quad)]
            dm_chunk = dmix[rows, pl.ds(pl.multiple_of(g * 2 * hw, 2 * hw), 2 * hw)]
            k_rows = chunk[:, 2 * hw : 3 * hw]
            v_rows = chunk[:, 3 * hw :]
            dk = jnp.zeros((span, hw), F32)
            dv = jnp.zeros((span, hw), F32)
            dqs = []
            for h in range(2):
                q = chunk[b * half :, h * hw : (h + 1) * hw]
                dmh = dm_chunk[:, h * hw : (h + 1) * hw]
                probs = masked_probs(q, k_rows, b * half, starts[rows, :])
                dprobs = mm_nt(dmh, v_rows)
                total = jnp.sum(probs * dprobs, axis=-1, keepdims=True)
                dscores = (probs * (dprobs - total) * SCORE_SCALE).astype(BF)
                dqs.append(mm(dscores, k_rows))
                dk = dk + mm_tn(dscores, q)
                dv = dv + mm_tn(probs.astype(BF), dmh)
            dkv_new = jnp.concatenate([dk, dv], axis=1)
            pair = pl.ds(pl.multiple_of(g * 2 * hw, 2 * hw), 2 * hw)
            if b == 1:
                dkv[:, pair] = dkv_new[:half]
                dkv_own = dkv_new[half:]
            else:
                dkv_own = dkv_new + dkv[:, pair]
            d = jnp.concatenate(dqs + [dkv_own], axis=1)
            d = d * cos[rows, :] - swap_halves(d) * sin[rows, :]
            dproj[rows, pl.ds(pl.multiple_of(g * quad, quad), quad)] = d.astype(BF)

        dattn_in = jnp.zeros((half, width), F32)
        for j in range(nblk):
            dattn_in = dattn_in + mm_nt(
                dproj[rows, j * qw : (j + 1) * qw],
                w_att[j, :, :, :, :qw].reshape(width, qw),
            )
        x = xd[rows, :].astype(F32)
        rx = row_scale(x)
        scaled = dattn_in * gain_a[...]
        inner = jnp.mean(scaled * x, axis=-1, keepdims=True)
        igb[0, rows, :] = (dmid[rows, :] + (rx * scaled - x * (rx * rx * rx) * inner)).astype(BF)
        gain_a_part = gain_a_part + jnp.sum(dattn_in * x * rx, axis=0, keepdims=True)
        igs.start(b)
        if b == 1:
            for h in range(2):
                ess.arrived(h)
                get = pltpu.make_async_copy(e_across.at[h], e_load, lsems.at[7])
                get.start()
                get.wait()
                e_loads[h].wait()
                e_mix[h] = plus(e_mix[h], e_load[...])
                ess.send(h)

    s_own[EXPERT_COUNT : EXPERT_COUNT + 8, :] = jnp.concatenate(
        [gain_a_part, gain_m_part, jnp.zeros((6, width), F32)], axis=0
    )
    s_share.start()
    for j in range(nblk):
        wg[j, :, :, :, :qw] = (
            mm_tn(attn[...], dproj[:, j * qw : (j + 1) * qw])
            .astype(BF)
            .reshape(pairs, 2, shard, qw)
        )
        wg_share[j].start()
    igs.forward(1)
    igs.forward(0)
    s_share.wait_recv()
    s_sum[...] = s_own[...] + s_sib[...]
    for copy in s_rows:
        copy.start()
    for j in (3, 1, 2, 0):
        wg_share[j].wait_recv()
        wg[j, :, pl.ds(k, 1)] = plus(wg[j, :, pl.ds(k, 1)], wg_sib[j][:, None])
    wgs.start()

    ess.finish()
    e_gets = [
        pltpu.make_async_copy(es.at[0], own.at[0], lsems.at[0]),
        pltpu.make_async_copy(e_landed.at[0], own.at[1], lsems.at[1]),
        pltpu.make_async_copy(e_landed.at[1], own.at[2], lsems.at[2]),
    ]
    dms.drain()
    for copy in e_gets:
        copy.start()
    for copy in e_gets:
        copy.wait()
    summed = own[0].astype(F32) + (own[1].astype(F32) + own[2].astype(F32))
    block_out[...] = (input_grad[...] + RESIDUAL_SCALE * summed).astype(BF)

    for h in range(2):
        wgs.arrived(h)
        hz = zpart(h)
        wg[2 - h, hz, pl.ds(k, 1)] = plus(wg[2 - h, hz, pl.ds(k, 1)], w_across[h][:, None])
        wgs.send(h)
    for copy in s_rows:
        copy.wait_recv()
    s_chip[...] = tree_sum([s_sum[...]] + [s_row[j] for j in range(nblk - 1)])
    for copy in s_zs:
        copy.start()
    igs.wait((1, 0), (2, 1))
    total = mm(match(0), igb[0])
    for j in (1, 2):
        total = total + mm(match(j), igb[j])
    igs.wait((3, 0), (3, 1))
    total = total + mm(match(3), igb[3])
    input_grad[...] = total
    wgs.finish()
    rowsum[...] = (
        wg[0, :, pl.ds(k, 1)].reshape(rowsum.shape).astype(F32)
        + (w_landed[0].astype(F32) + w_landed[1].astype(F32))
    ).astype(BF)
    for copy in wg_z:
        copy.start()
    for copy in s_zs:
        copy.wait_recv()
    small[...] = tree_sum([s_chip[...]] + [s_z[i] for i in range(pairs - 1)])
    for copy in wg_z:
        copy.wait_recv()
    att_grad[...] = tree_sum(
        [rowsum[pl.ds(z, 1)].reshape(att_grad.shape).astype(F32)]
        + [w_z[i].astype(F32) for i in range(pairs - 1)]
    )
    for group in (ess, wgs, igs):
        group.drain()
    for copy in dgs + wg_share + wg_z + [s_share] + s_rows + s_zs:
        copy.wait_send()


def backward(dm, es, dgates, mids, *rest):
    nblk, tokens, width = dm.shape
    w_att = rest[8]
    pairs, shard, both = w_att.shape[1], w_att.shape[3], w_att.shape[4]
    half = tokens // 2
    local = EXPERT_COUNT // nblk
    shape = jax.ShapeDtypeStruct
    count = (
        3 * RowScatter.count
        + RowGather.count
        + (nblk - 1)
        + nblk
        + (pairs - 1)
        + 1
        + (nblk - 1)
        + (pairs - 1)
    )
    small = (EXPERT_COUNT + 8, width)
    outs = pl.pallas_call(
        functools.partial(back_kernel, nblk),
        out_shape=(
            shape((tokens, width), BF),
            shape((tokens, width), F32),
            shape((shard, both), F32),
            shape(small, F32),
            shape((2, half, width), BF),
            shape((2, tokens, width), BF),
        ),
        in_specs=[ANY] * 2 + [FULL] + [ANY] * nblk + [FULL, ANY] + [FULL] * 14,
        out_specs=[FULL] * 4 + [ANY] * 2,
        scratch_shapes=[
            pltpu.VMEM((3, tokens, width), BF),
            pltpu.VMEM((2, half, width), BF),
            pltpu.VMEM((2, tokens, width), BF),
            pltpu.VMEM((nblk - 1, local, tokens), F32),
            pltpu.VMEM((2, half, width), BF),
            pltpu.VMEM((half, width), BF),
            pltpu.VMEM((nblk, tokens, width), BF),
            pltpu.VMEM((tokens, width), F32),
            pltpu.VMEM((tokens, width), BF),
            pltpu.VMEM((tokens, 2 * width), BF),
            pltpu.VMEM((half, width), F32),
            pltpu.VMEM(w_att.shape, BF),
            pltpu.VMEM((nblk, pairs, shard, both), BF),
            pltpu.VMEM((2, pairs // 2, shard, both), BF),
            pltpu.VMEM((2, pairs, shard, both), BF),
            pltpu.VMEM((pairs - 1, shard, both), BF),
            pltpu.VMEM((pairs, shard, both), BF),
            pltpu.VMEM(small, F32),
            pltpu.VMEM(small, F32),
            pltpu.VMEM(small, F32),
            pltpu.VMEM((nblk - 1, *small), F32),
            pltpu.VMEM(small, F32),
            pltpu.VMEM((pairs - 1, *small), F32),
            pltpu.SemaphoreType.DMA((2, count)),
            pltpu.SemaphoreType.DMA((8,)),
        ],
        compiler_params=pltpu.CompilerParams(
            vmem_limit_bytes=62 * MIB, collective_id=2, has_side_effects=True
        ),
        cost_estimate=cost(60e9, 100 * MIB),
        name="attention_backward",
    )(dm, es, dgates, *mids, *rest)
    return outs[:4]


def swap_over(value, axis, size, step):
    return lax.ppermute(value, axis, [(i, i ^ step) for i in range(size)])


def spread_rows(value, axis, size, step=1):
    return [value] + [swap_over(value, axis, size, j) for j in range(step, size, step)]


def body(
    block_in,
    cotangent,
    seq_lengths,
    seq_order,
    expert_ids,
    places,
    attn_gain,
    w_qkv,
    w_out,
    moe_gain,
    w_router,
    w_gate,
    w_up,
    w_down,
):
    tokens = block_in.shape[1]
    width = block_in.shape[2]
    rows = lax.axis_size("row")
    cols = lax.axis_size("col")
    total = tokens * rows
    r = lax.axis_index("row")
    c = lax.axis_index("col")
    parity = c % 2
    local = w_gate.shape[1]
    shard = w_gate.shape[0]
    fe = w_gate.shape[2]
    capacity = total * TOPK // EXPERT_COUNT
    pairs = cols // 2
    qw = w_qkv.shape[1]
    ow = w_out.shape[1]

    stacked = jnp.stack([w_gate, w_up, w_down]).transpose(2, 0, 1, 3)
    chunk = 2
    gathered = [
        lax.all_gather(stacked[i : i + chunk], "col", axis=0) for i in range(0, local, chunk)
    ]

    w_own = jnp.concatenate([w_qkv, w_out], axis=1)
    base = c // 2

    def join_parity(mine, other, axis):
        even = jnp.where(parity == 0, mine, other)
        odd = jnp.where(parity == 0, other, mine)
        both = jnp.stack([even, odd], axis=axis + 1)
        return jnp.concatenate(
            [lax.dynamic_slice_in_dim(both, base ^ i, 1, axis) for i in range(pairs)], axis=axis
        )

    lengths = seq_lengths[0]
    perm = seq_order[0]
    seq_ids = jnp.arange(lengths.shape[0], dtype=jnp.int32)
    picked = perm[:, None] == seq_ids[None, :]
    dealt_len = jnp.sum(jnp.where(picked, lengths[None, :], 0), axis=1)
    before = seq_ids[None, :] < perm[:, None]
    source_base = jnp.sum(jnp.where(before, lengths[None, :], 0), axis=1)
    upto = seq_ids[None, :] <= seq_ids[:, None]
    seq_ends = jnp.sum(jnp.where(upto, dealt_len[None, :], 0), axis=1)
    dealt_start = seq_ends - dealt_len
    turn = r * tokens
    pos = jnp.arange(total, dtype=jnp.int32) ^ turn
    inside = (pos[:, None] >= dealt_start[None, :]) & (pos[:, None] < seq_ends[None, :])
    seq_starts = jnp.sum(jnp.where(inside, dealt_start[None, :], 0), axis=1)
    offset = pos - seq_starts
    source = jnp.sum(jnp.where(inside, source_base[None, :], 0), axis=1) + offset
    source = source ^ turn
    src_col = source[:, None]
    src_row = source[None, :]
    own_offset = offset[:tokens]
    own_starts = (seq_starts[:tokens] - turn)[:, None]

    half = HEAD_WIDTH // 2
    frequency = ROPE_BASE ** (-jnp.arange(half, dtype=F32) * 2.0 / HEAD_WIDTH)
    turned = own_offset.astype(F32)[:, None] * frequency[None, :]
    cosine, sine = jnp.cos(turned), jnp.sin(turned)
    ones, zeros = jnp.ones_like(cosine), jnp.zeros_like(cosine)
    cos_w = jnp.concatenate([cosine] * 6 + [ones] * 2, axis=1)
    sin_w = jnp.concatenate([-sine, sine] * 3 + [zeros] * 2, axis=1)

    gain_a = attn_gain[None, :]
    gain_m = moe_gain[None, :]
    def by_block(table):
        blocks = table.reshape(rows, tokens, TOPK)
        return jnp.concatenate(
            [lax.dynamic_slice_in_dim(blocks, r ^ j, 1, 0) for j in range(rows)], axis=0
        ).reshape(total, TOPK)

    ids = by_block(expert_ids[0])
    spots = by_block(places[0])
    ids = ((ids // local) ^ r) * local + ids % local
    spots = jnp.where(spots < capacity, spots, -1)
    (xd, attn, qkv, mixed, middle, moe, dsum, dy, slot_cols, slot_rows, chosen, w_att, moe_own, slot_given, mid16) = front(
        block_in[0],
        cotangent[0],
        w_own,
        src_col,
        own_starts,
        cos_w,
        sin_w,
        gain_a,
        gain_m,
        ids,
        spots,
        src_row,
        rows,
        pairs,
    )

    router_half = jnp.stack(spread_rows(w_router, "col", cols, 2))
    router_full = join_parity(router_half, swap_over(router_half, "col", cols, 1), 0)
    router_blocks = router_full.reshape(width, rows, local)
    router_x = jnp.concatenate(
        [lax.dynamic_slice_in_dim(router_blocks, r ^ j, 1, 1) for j in range(rows)], axis=1
    ).reshape(width, EXPERT_COUNT)
    router_x = jnp.pad(router_x, ((0, 0), (0, LANES - EXPERT_COUNT)))
    gates, packed = router(moe, router_x, chosen)

    mids = spread_rows(mid16, "row", rows)
    carried = None
    summed = []
    for i, w in enumerate(gathered):
        last = i == len(gathered) - 1
        if i == 2:
            w, *mids = lax.optimization_barrier((w, *mids))
        grads, *carried = experts(
            moe,
            dsum,
            slot_rows,
            slot_cols,
            slot_given,
            packed,
            w,
            carried,
            i * chunk,
            last,
            capacity,
        )
        summed.append(lax.psum_scatter(grads, "col", scatter_dimension=0, tiled=False))
    es, dm, dgates = carried
    dgates = lax.optimization_barrier((dgates, summed[0], summed[1]))[0]
    block_out, input_grad, att_grad, small = backward(
        dm,
        es,
        dgates,
        mids,
        gates[:tokens],
        middle,
        moe_own,
        dy,
        mixed,
        qkv,
        attn,
        xd,
        w_att,
        router_x,
        own_starts,
        cos_w,
        sin_w,
        gain_a,
        gain_m,
        src_row,
    )
    router_all = small[:EXPERT_COUNT].T
    router_grad = lax.dynamic_slice_in_dim(router_all, c * shard, shard, 0)
    grads = jnp.concatenate(summed, axis=0).astype(F32).transpose(1, 2, 0, 3)
    return (
        block_out[None],
        input_grad[None],
        small[EXPERT_COUNT],
        att_grad[:, :qw],
        att_grad[:, qw:],
        small[EXPERT_COUNT + 1],
        router_grad,
        grads[0],
        grads[1],
        grads[2],
    )


def solution(mesh):
    tokens = P("col", "row", None)
    weight = P("col", "row")
    expert = P("col", "row", None)
    return jax.shard_map(
        body,
        mesh=mesh,
        in_specs=(
            tokens,
            tokens,
            P("col", None),
            P("col", None),
            P("col", None, None),
            P("col", None, None),
            P(),
            weight,
            weight,
            P(),
            P("col", None),
            expert,
            expert,
            expert,
        ),
        out_specs=(
            tokens,
            tokens,
            P(),
            weight,
            weight,
            P(),
            P("col", None),
            expert,
            expert,
            expert,
        ),
        check_vma=False,
    )
```

time: 794 us -> 680 us (0.86)
  Pallas kernels: 318 us -> 559 us
  waiting for transfers between devices: 239 us -> 45.8 us
  starting transfers between devices: 118 us -> 7.25 us
  local copies, waits for them, and re-layouts: 64.2 us -> 36.9 us
  other arithmetic: 32.6 us -> 9.99 us
    ppermute x52 -> x7, waiting for transfers between devices: 236 us -> 43.1 us  [swap_over(): return lax.ppermute(value, axis, [(i, i ^ step) for i in range(size)])]
    pallas_call x1, Pallas kernels: 44.8 us -> 171 us  [backward(): pl.pallas_call(functools.partial(back_kernel, nblk), out_shape=(shape((to...]
    pallas_call x9 -> x6, Pallas kernels: 273 us -> 388 us  [the longest x4 212 us: experts(): pl.pallas_call(functools.partial(expert_kernel, base, first, last, local,...]
    ppermute x52 -> x7, starting transfers between devices: 118 us -> 6.93 us  [swap_over(): return lax.ppermute(value, axis, [(i, i ^ step) for i in range(size)])]
    convert_element_type x3 -> x0, other arithmetic: 11 us -> none  [the longest x1 5.21 us: body(): (mine.astype(F32) + swap_over(other, 'col', cols, 1).astype(F32)).astype(BF)]
    squeeze x4 -> x0, local copies, waits for them, and re-layouts: 9.13 us -> none  [the longest x1 4.02 us: send_blocks(): blocks[j]]
    unnamed x115 -> x46, local copies, waits for them, and re-layouts: 24.2 us -> 17.4 us
  transfers between devices with their start and end apart: 60 -> 15, of which waited for: 22 -> 3; matrix products, arithmetic and copies ran while one was open for 9% -> 3% of each run, Pallas kernels for 40% -> 83%
where the time goes in v2:
time: 680 us; the launch traced here: 674 us
  Pallas kernels  559 us (82%)
  waiting for transfers between devices  45.8 us (7%)
  local copies, waits for them, and re-layouts  36.9 us (5%)
  between operations  14.8 us (2%)
  other arithmetic  9.99 us (1%)
  starting transfers between devices  7.25 us (1%)
    pallas_call x4, Pallas kernels, experts(): pl.pallas_call(functools.partial(expert_kernel, base, first, last, local,...  212 us
    pallas_call x1, Pallas kernels, front(): pl.pallas_call(front_kernel, out_shape=(shape((tokens, width), BF), shape...  173 us
    pallas_call x1, Pallas kernels, backward(): pl.pallas_call(functools.partial(back_kernel, nblk), out_shape=(shape((to...  171 us
    ppermute x7, waiting for transfers between devices, swap_over(): return lax.ppermute(value, axis, [(i, i ^ step) for i in range(size)])  43.1 us
    unnamed x46, local copies, waits for them, and re-layouts  17.4 us
  transfers between devices with their start and end apart: 15, of which 3 were waited for; matrix products, arithmetic and copies ran while one was open for 3% of the time, Pallas kernels for 83%

profile of v2, /device:TPU:9, one launch (start us, length us, event | category | flops | bytes accessed | tf_op | source)
XLA Modules:
  0.0 673.6 jit_solution(3992902747514340051)
XLA Ops:
  7.2 1.5 copy.112
  8.8 2.2 copy_bitcast_fusion
  11.3 1.8 fusion.14
  14.8 2.5 collective-permute-start.1
  18.7 1.3 copy.93
  20.1 1.3 copy.94
  23.1 2.0 fusion.2.ids
  26.1 1.1 add_xor_fusion.src
  28.8 1.5 concatenate.32.cos.refs_18_
  30.4 1.3 concatenate.34.sin.refs_19_
  31.8 1.6 collective-permute-start.3
  33.3 173.1 %attention_forward.1 = (bf16[512,1024]{1,0:T(8,128)(2,1)}, bf16[512,1024]{1,0:T(8,128)(2,1)}, bf16[512,2048]{1,0:T(8,128)(2,1)}, bf16[512,1024]{1,0:T(8,128)(2,1...) custom-call(bf16[512,1024]{1,0:T(8,128)(2,1)} %bitcast.108, ...), custom_call_target="tpu_custom_call" | custom-call | flops 20000000000 | bytes 62914560 | tf_op jit(solution)/shard_map/attention_forward/pallas_call | solution.py:356
  206.9 2.3 copy-done
  209.2 1.2 copy-done.1
  210.4 2.6 router.1
  213.9 53.3 %experts.4 = (bf16[8,2,3,128,512]{4,3,2,1,0:T(8,128)(2,1)}, f32[2,2048,1024]{2,1,0:T(8,128)}, f32[2048,128]{1,0:T(8,128)}) custom-call(bf16[4,512,1024]{2,1,0:T(8,128)(2,1)} %get-tuple-element.50.moe.refs_0_, bf16[2048,1024]{1,0:T(8,128)(2,1)} %get-tuple-element.51.refs_1_, f32[128,2048]{1,0:T(8,128)} %get-tuple-element.52.refs_2_, ...), custom_call_target="tpu_custom_call" | custom-call | flops 28000000000 | bytes 41943040 | tf_op jit(solution)/shard_map/experts/pallas_call | solution.py:618
  267.2 53.5 %experts.5 = (bf16[8,2,3,128,512]{4,3,2,1,0:T(8,128)(2,1)}, f32[2,2048,1024]{2,1,0:T(8,128)}, f32[2048,128]{1,0:T(8,128)}) custom-call(bf16[4,512,1024]{2,1,0:T(8,128)(2,1)} %get-tuple-element.50.moe.refs_0_, bf16[2048,1024]{1,0:T(8,128)(2,1)} %get-tuple-element.51.refs_1_, ...), custom_call_target="tpu_custom_call", output_to_operand_aliasing={{1}: (7, {}), {2}: (8, {})} | custom-call | flops 28000000000 | bytes 41943040 | tf_op jit(solution)/shard_map/experts/pallas_call | solution.py:618
  323.6 1.1 collective-permute-start.6
  324.7 20.3 %collective-permute-done.4.refs_4_ = bf16[512,1024]{1,0:T(8,128)(2,1)S(1)} collective-permute-done((bf16[512,1024]{1,0:T(8,128)(2,1)S(1)}, bf16[512,1024]{1,0:T(8,128)(2,1)S(1)}, u32[]{:S(2)}, u32[]{:S(2)}) %collective-permute-start.4) | collective-permute-done | bytes 1048608 | tf_op jit(solution)/shard_map/ppermute | solution.py:1047
  345.0 1.1 collective-permute-done.5.refs_5_
  347.1 21.7 %collective-permute-done.6.refs_6_ = bf16[512,1024]{1,0:T(8,128)(2,1)} collective-permute-done((bf16[512,1024]{1,0:T(8,128)(2,1)S(1)}, bf16[512,1024]{1,0:T(8,128)(2,1)}, u32[]{:S(2)}, u32[]{:S(2)}) %collective-permute-start.6) | collective-permute-done | bytes 1048608 | tf_op jit(solution)/shard_map/ppermute | solution.py:1047
  368.8 53.5 %experts.6 = (bf16[8,2,3,128,512]{4,3,2,1,0:T(8,128)(2,1)}, f32[2,2048,1024]{2,1,0:T(8,128)}, f32[2048,128]{1,0:T(8,128)}) custom-call(bf16[4,512,1024]{2,1,0:T(8,128)(2,1)} %get-tuple-element.50.moe.refs_0_, bf16[2048,1024]{1,0:T(8,128)(2,1)} %get-tuple-element.51.refs_1_, ...), custom_call_target="tpu_custom_call", output_to_operand_aliasing={{1}: (7, {}), {2}: (8, {})} | custom-call | flops 28000000000 | bytes 41943040 | tf_op jit(solution)/shard_map/experts/pallas_call | solution.py:618
  422.2 51.9 %experts.7 = (bf16[8,2,3,128,512]{4,3,2,1,0:T(8,128)(2,1)}, bf16[4,512,1024]{2,1,0:T(8,128)(2,1)}, bf16[4,512,1024]{2,1,0:T(8,128)(2,1)}, f32[8,2048]{1,0:T(8,128)}) custom-call(bf16[4,512,1024]{2,1,0:T(8,128)(2,1)} %get-tuple-element.50.moe.refs_0_, bf16[2048,1024]{1,0:T(8,128)(2,1)} %get-tuple-element.51.refs_1_, f32[128,2048]{1,0:T(8,128)} %get-tuple-element.52.refs_2_, ...), custom_call_target="tpu_custom_call" | custom-call | flops 28000000000 | bytes 41943040 | tf_op jit(solution)/shard_map/experts/pallas_call | solution.py:618
  475.6 171.0 %attention_backward.1 = (bf16[512,1024]{1,0:T(8,128)(2,1)}, f32[512,1024]{1,0:T(8,128)}, f32[128,768]{1,0:T(8,128)}, f32[40,1024]{1,0:T(8,128)}, bf16[2,256,1024...) custom-call(bf16[4,512,1024]{2,1,0:T(8,128)(2,1)} %get-tuple-element.65.refs_0_, ...), custom_call_target="tpu_custom_call" | custom-call | flops 60000002048 | bytes 104857600 | tf_op jit(solution)/shard_map/attention_backward/pallas_call | solution.py:998
  646.6 1.7 slice.53
  648.3 1.6 slice.54
  650.8 1.4 fusion.15
  652.2 2.7 convert_bitcast_fusion
  656.0 2.5 copy.106
  658.5 2.5 copy.107
  661.1 2.5 copy.108
  665.2 1.3 copy.120
  (105 shorter events, 17.7 us)
Async XLA Ops:
  7.2 206.7 %all-gather.15.cloned.1.call-start = ((), (), s32[]{:S(2)}) async-start(), calls=%async_computation.11 | async-start | bytes 7077888 | tf_op jit(solution)/shard_map/all_gather | solution.py:1089
  11.3 3.4 copy-start.14
  13.1 4.4 copy-start.11
  13.1 4.4 copy-start.12
  13.1 5.1 copy-start.15
  13.1 5.2 copy-start.16
  13.2 254.0 %all-gather.13.cloned.1.call-start = ((), (), s32[]{:S(2)}) async-start(), calls=%async_computation.10 | async-start | bytes 7077888 | tf_op jit(solution)/shard_map/all_gather | solution.py:1089
  13.9 354.8 %all-gather.11.cloned.1.call-start = ((), (), s32[]{:S(2)}) async-start(), calls=%async_computation.9 | async-start | bytes 7077888 | tf_op jit(solution)/shard_map/all_gather | solution.py:1089
  14.7 407.6 %all-gather.9.cloned.1.call-start = ((), (), s32[]{:S(2)}) async-start(), calls=%async_computation.8 | async-start | bytes 7077888 | tf_op jit(solution)/shard_map/all_gather | solution.py:1089
  14.7 17.0 %collective-permute-start = (bf16[128,32]{0,1:T(8,128)(2,1)S(1)}, bf16[128,32]{0,1:T(8,128)(2,1)S(1)}, u32[]{:S(2)}, u32[]{:S(2)}) collective-permute-start(bf16[128,32]{0,1:T(8,128)(2,1)S(1)} %copy-done.14), channel_id=1, source_target_pairs={{0,2},{1,3},{2,0},{3,1},{4,6},{5,7},{6,4},{7,5},{8,10},{9,11},{10,... | collective-permute-start | bytes 24584 | tf_op jit(solution)/shard_map/ppermute | solution.py:1047
  14.8 16.9 %collective-permute-start.1 = (bf16[128,32]{0,1:T(8,128)(2,1)S(1)}, bf16[128,32]{0,1:T(8,128)(2,1)S(1)}, u32[]{:S(2)}, u32[]{:S(2)}) collective-permute-start(bf16[128,32]{0,1:T(8,128)(2,1)S(1)} %copy-done.14), channel_id=1, source_target_pairs={{0,4},{1,5},{2,6},{3,7},{4,0},{5,1},{6,2},{7,3},{8,12},{9,13},{10,... | collective-permute-start | bytes 24584 | tf_op jit(solution)/shard_map/ppermute | solution.py:1047
  17.3 14.5 %collective-permute-start.2 = (bf16[128,32]{0,1:T(8,128)(2,1)S(1)}, bf16[128,32]{0,1:T(8,128)(2,1)S(1)}, u32[]{:S(2)}, u32[]{:S(2)}) collective-permute-start(bf16[128,32]{0,1:T(8,128)(2,1)S(1)} %copy-done.14), channel_id=1, source_target_pairs={{0,6},{1,7},{2,4},{3,5},{4,2},{5,3},{6,0},{7,1},{8,14},{9,15},{10,... | collective-permute-start | bytes 24584 | tf_op jit(solution)/shard_map/ppermute | solution.py:1047
  17.4 458.2 %reduce-scatter.7.cloned.1.call-start = ((), (), s32[]{:S(2)}) async-start(), calls=%async_computation.5 | async-start | bytes 7077888 | tf_op jit(solution)/shard_map/reduce_scatter | solution.py:1191
  21.4 4.7 copy-start.4
  21.4 4.7 copy-start.5
  25.0 2.2 copy-start.10
  25.0 2.2 copy-start.13
  31.8 174.7 %collective-permute-start.3 = (bf16[4,128,32]{1,2,0:T(8,128)(2,1)S(1)}, bf16[4,128,32]{1,2,0:T(8,128)(2,1)S(1)}, u32[]{:S(2)}, u32[]{:S(2)}) collective-permute-start(bf16[4,128,32]{1,2,0:T(8,128)(2,1)S(1)} %pad_maximum_fusion.2), channel_id=1, source_target_pairs={{0,1},{1,0},{2,3},{3,2},{4,5},{5,4},{6,7},{7,6},{8,9},{9,8},{10,11... | collective-permute-start | bytes 98312 | tf_op jit(solution)/shard_map/ppermute | solution.py:1047
  206.9 60.3 %copy-start.2 = (bf16[1024,128]{1,0:T(8,128)(2,1)}, bf16[1024,128]{1,0:T(8,128)(2,1)S(1)}, u32[]{:S(2)}) copy-start(bf16[1024,128]{1,0:T(8,128)(2,1)S(1)} %pad.4.w_router.refs_16_) | copy-start | bytes 786436
  206.9 2.3 copy-start
  209.2 1.2 copy-start.1
  320.8 154.8 %reduce-scatter.5.cloned.1.call-start = ((), (), s32[]{:S(2)}) async-start(), calls=%async_computation.4 | async-start | bytes 7077888 | tf_op jit(solution)/shard_map/reduce_scatter | solution.py:1191
  320.8 1.2 copy-start.17
  321.4 330.9 %reduce-scatter.11.cloned.1.call-start = ((), (), s32[]{:S(2)}) async-start(), calls=%async_computation.7 | async-start | bytes 7077888 | tf_op jit(solution)/shard_map/reduce_scatter | solution.py:1191
  322.0 22.9 %collective-permute-start.4 = (bf16[512,1024]{1,0:T(8,128)(2,1)S(1)}, bf16[512,1024]{1,0:T(8,128)(2,1)S(1)}, u32[]{:S(2)}, u32[]{:S(2)}) collective-permute-start(bf16[512,1024]{1,0:T(8,128)(2,1)S(1)} %copy-done.17), channel_id=1, source_target_pairs={{0,8},{8,0},{16,24},{24,16},{1,9},{9,1},{17,25},{25,17},{2,10},{10... | collective-permute-start | bytes 3145736 | tf_op jit(solution)/shard_map/ppermute | solution.py:1047
  323.1 23.0 %collective-permute-start.5 = (bf16[512,1024]{1,0:T(8,128)(2,1)S(1)}, bf16[512,1024]{1,0:T(8,128)(2,1)S(1)}, u32[]{:S(2)}, u32[]{:S(2)}) collective-permute-start(bf16[512,1024]{1,0:T(8,128)(2,1)S(1)} %copy-done.17), channel_id=1, source_target_pairs={{0,16},{8,24},{16,0},{24,8},{1,17},{9,25},{17,1},{25,9},{2,18},{10... | collective-permute-start | bytes 3145736 | tf_op jit(solution)/shard_map/ppermute | solution.py:1047
  323.6 45.2 %collective-permute-start.6 = (bf16[512,1024]{1,0:T(8,128)(2,1)S(1)}, bf16[512,1024]{1,0:T(8,128)(2,1)}, u32[]{:S(2)}, u32[]{:S(2)}) collective-permute-start(bf16[512,1024]{1,0:T(8,128)(2,1)S(1)} %copy-done.17), channel_id=1, source_target_pairs={{0,24},{8,16},{16,8},{24,0},{1,25},{9,17},{17,9},{25,1},{2,26},{10... | collective-permute-start | bytes 3145736 | tf_op jit(solution)/shard_map/ppermute | solution.py:1047
  474.1 178.1 %reduce-scatter.9.cloned.1.call-start = ((), (), s32[]{:S(2)}) async-start(), calls=%async_computation.6 | async-start | bytes 7077888 | tf_op jit(solution)/shard_map/reduce_scatter | solution.py:1191
  475.6 176.6 %copy-start.8 = (bf16[1,2,3,128,512]{4,3,2,1,0:T(8,128)(2,1)S(1)}, bf16[1,2,3,128,512]{4,3,2,1,0:T(8,128)(2,1)}, u32[]{:S(2)}) copy-start(bf16[1,2,3,128,512]{4,3,2,1,0:T(8,128)(2,1)} %reduce-scatter.7.cloned.1.call-done) | copy-start | bytes 2359300
  475.6 176.6 %copy-start.9 = (bf16[1,2,3,128,512]{4,3,2,1,0:T(8,128)(2,1)S(1)}, bf16[1,2,3,128,512]{4,3,2,1,0:T(8,128)(2,1)}, u32[]{:S(2)}) copy-start(bf16[1,2,3,128,512]{4,3,2,1,0:T(8,128)(2,1)} %reduce-scatter.5.cloned.1.call-done) | copy-start | bytes 2359300
  661.1 3.1 copy-start.7
  661.1 4.1 copy-start.6
  (3 other events, 2.9 us)
Sparse Core Ops, SparseCore 0:
  13.3 77.7 all-gather.14
  92.7 66.3 all-gather.12
  160.8 63.3 all-gather.10
  225.7 63.3 all-gather.8
  320.9 69.4 reduce-scatter.6
  392.6 68.1 reduce-scatter.4
  474.3 70.5 reduce-scatter.10
  547.2 81.2 reduce-scatter.8

commit v3 on v2

v3 whole, which is shorter than its diff:
```python
import functools

import jax
import jax.numpy as jnp
from jax import lax
from jax.experimental import pallas as pl
from jax.experimental.pallas import tpu as pltpu
from jax.sharding import PartitionSpec as P

HEAD_WIDTH = 64
QUERY_HEADS = 16
KEY_VALUE_HEADS = 8
EXPERT_COUNT = 32
TOPK = 8
EPSILON = 1e-06
RESIDUAL_SCALE = 0.22
SCORE_SCALE = 0.015625
ROPE_BASE = 10000.0
MASKED = -1e30
LANES = 128
MIB = 1024 * 1024
BF = jnp.bfloat16
F32 = jnp.float32
ANY = pl.BlockSpec(memory_space=pl.ANY)
FULL = pl.BlockSpec(memory_space=pltpu.VMEM)


def mm(a, b):
    return lax.dot_general(a, b, (((1,), (0,)), ((), ())), preferred_element_type=F32)


def mm_nt(a, b):
    return lax.dot_general(a, b, (((1,), (1,)), ((), ())), preferred_element_type=F32)


def mm_tn(a, b):
    return lax.dot_general(a, b, (((0,), (0,)), ((), ())), preferred_element_type=F32)


def iota(shape, dim):
    return lax.broadcasted_iota(jnp.int32, shape, dim)


def params(mib):
    return pltpu.CompilerParams(vmem_limit_bytes=mib * MIB)


def cost(flops, moved):
    return pl.CostEstimate(flops=int(flops), bytes_accessed=int(moved), transcendentals=0)


def row_scale(values):
    return lax.rsqrt(jnp.mean(values * values, axis=-1, keepdims=True) + EPSILON)


def swap_halves(values):
    width = values.shape[-1]
    half = HEAD_WIDTH // 2
    low = (iota(values.shape, 1) % HEAD_WIDTH) < half
    ahead = pltpu.roll(values, width - half, 1)
    behind = pltpu.roll(values, half, 1)
    return jnp.where(low, ahead, behind)


def attention_bias(row0, rows, cols, starts):
    at = iota((rows, cols), 1)
    allowed = (at <= iota((rows, cols), 0) + row0) & (at >= starts)
    return jnp.where(allowed, 0.0, MASKED)


def masked_probs(q, k, bias):
    scores = mm_nt(q, k) + bias
    raised = jnp.exp(scores - jnp.max(scores, axis=-1, keepdims=True))
    return raised * (1.0 / jnp.sum(raised, axis=-1, keepdims=True))


def link(src, dst, sems, index, device):
    return pltpu.make_async_remote_copy(
        src_ref=src,
        dst_ref=dst,
        send_sem=sems.at[0, index],
        recv_sem=sems.at[1, index],
        device_id=device,
        device_id_type=pl.DeviceIdType.MESH,
    )


def greet(devices):
    barrier = pltpu.get_barrier_semaphore()
    for device in devices:
        pl.semaphore_signal(barrier, inc=1, device_id=device, device_id_type=pl.DeviceIdType.MESH)
    pl.semaphore_wait(barrier, len(devices))


class RowGather:
    count = 6

    def __init__(self, own, slot, sems, base, r, c):
        near, far = (r ^ 1, c), (r ^ 2, c)
        self.copies = {
            (1, 1): link(own(1), slot(1, 1), sems, base, near),
            (2, 0): link(own(0), slot(2, 0), sems, base + 1, far),
            (1, 0): link(own(0), slot(1, 0), sems, base + 2, near),
            (2, 1): link(own(1), slot(2, 1), sems, base + 3, far),
            (3, 0): link(slot(2, 0), slot(3, 0), sems, base + 4, near),
            (3, 1): link(slot(1, 1), slot(3, 1), sems, base + 5, far),
        }

    def start(self, half):
        order = ((2, 0), (1, 0)) if half == 0 else ((1, 1), (2, 1))
        for key in order:
            self.copies[key].start()

    def forward(self, half):
        self.copies[(2, 0) if half == 0 else (1, 1)].wait_recv()
        self.copies[(3, half)].start()

    def wait(self, *keys):
        for key in keys:
            self.copies[key].wait_recv()

    def drain(self):
        for copy in self.copies.values():
            copy.wait_send()


def front_kernel(
    xin,
    w_half,
    src,
    starts,
    cos,
    sin,
    gain_a,
    gain_m,
    ids,
    spots,
    src_row,
    xd,
    attn,
    qkv,
    mixed,
    middle,
    moe_all,
    slot_cols,
    slot_rows,
    chosen,
    w_att,
    moe,
    slot_given,
    given_rows,
    mid16,
    w_router,
    xb,
    bias,
    sems,
    local_sems,
):
    nblk, tokens, width = xb.shape
    half = tokens // 2
    capacity = nblk * tokens * TOPK // EXPERT_COUNT
    pairs = w_att.shape[1]
    qw = w_att.shape[4] * 2 // 3
    rank = w_att.shape[1] * 2 * w_att.shape[3]
    r = lax.axis_index("row")
    c = lax.axis_index("col")
    z = c // 2
    k = c % 2
    both = w_att.shape[4]
    local = EXPERT_COUNT // nblk
    sibling = (r, c ^ 1)
    greet([(r ^ 1, c), (r ^ 2, c), sibling])

    def cut(ref):
        return lambda h: ref.at[pl.ds(h * half, half)]

    def cut_slot(ref):
        return lambda j, h: ref.at[j, pl.ds(h * half, half)]

    def w_slot(j, h):
        return w_att.at[j, pl.ds(h * (pairs // 2), pairs // 2), k]

    n = RowGather.count
    xs = RowGather(cut(xin), cut_slot(xb), sems, 0, r, c)
    ws = RowGather(lambda h: w_slot(0, h), w_slot, sems, n, r, c)
    ms = RowGather(cut(moe), cut_slot(moe_all), sems, 2 * n, r, c)
    base = 3 * n
    share = [link(w_att.at[j, :, k], w_att.at[j, :, k], sems, base + j, sibling) for j in range(nblk)]
    share.append(link(w_router.at[:, k], w_router.at[:, k], sems, base + nblk, sibling))
    xs.start(1)
    xs.start(0)
    keep = [pltpu.make_async_copy(xin, xb.at[0], local_sems.at[0])]
    for i in range(pairs):
        keep.append(
            pltpu.make_async_copy(
                w_half.at[i, :, pl.ds(0, both)], w_att.at[0, z ^ i, k], local_sems.at[2 + 2 * i]
            )
        )
        keep.append(
            pltpu.make_async_copy(
                w_half.at[i, :, pl.ds(both, LANES)], w_router.at[z ^ i, k], local_sems.at[3 + 2 * i]
            )
        )
    for copy in keep:
        copy.start()
    for copy in keep:
        copy.wait()
    ws.start(1)
    ws.start(0)
    share[0].start()
    share[nblk].start()
    xs.forward(0)
    xs.forward(1)

    source = src[:tokens, :]

    def pick(at, j):
        return jnp.where(at == iota((tokens, tokens), 1) + j * tokens, 1.0, 0.0).astype(BF)

    x = mm(pick(source, 0), xb[0])
    xs.wait((1, 0))
    x = x + mm(pick(source, 1), xb[1])
    xs.wait((2, 1))
    x = x + mm(pick(source, 2), xb[2])
    ws.forward(0)
    ws.forward(1)
    ws.wait((1, 0), (2, 1))
    share[1].start()
    share[2].start()
    xs.wait((3, 0), (3, 1))
    x = x + mm(pick(source, 3), xb[3])
    xd[...] = x.astype(BF)
    attn[...] = (x * row_scale(x) * gain_a[...]).astype(BF)
    groups = qw // (4 * HEAD_WIDTH)

    def project(j):
        proj = mm(attn[...], w_att[j, :, :, :, :qw].reshape(rank, qw))
        cos_w = jnp.concatenate([cos[...]] * groups, axis=1)
        sin_w = jnp.concatenate([sin[...]] * groups, axis=1)
        turned = proj * cos_w + swap_halves(proj) * sin_w
        qkv[:, pl.ds(pl.multiple_of(j * qw, qw), qw)] = turned.astype(BF)

    ws.wait((3, 0), (3, 1))
    share[3].start()
    for copy in share:
        copy.wait_recv()

    @pl.loop(0, nblk)
    def _(j):
        project(j)

    pair = 2 * HEAD_WIDTH
    for b in range(2):
        rows = slice(b * half, (b + 1) * half)
        span = (b + 1) * half
        bias[:, :span] = attention_bias(b * half, half, span, starts[rows, :])

        @pl.loop(0, groups * nblk)
        def _(g):
            chunk = qkv[:span, pl.ds(pl.multiple_of(g * 2 * pair, 2 * pair), 2 * pair)]
            k_rows = chunk[:, pair : pair + HEAD_WIDTH]
            v_rows = chunk[:, pair + HEAD_WIDTH :]
            outs = []
            for h in range(2):
                q = chunk[b * half :, h * HEAD_WIDTH : (h + 1) * HEAD_WIDTH]
                probs = masked_probs(q, k_rows, bias[:, :span])
                outs.append(mm(probs.astype(BF), v_rows))
            mixed[rows, pl.ds(pl.multiple_of(g * pair, pair), pair)] = jnp.concatenate(
                outs, axis=1
            ).astype(BF)

        if b == 1:
            ms.forward(0)
        ow = w_att.shape[4] - qw
        out = jnp.zeros((half, width), F32)
        for j in range(nblk):
            w_out = w_att[j, :, :, :, qw:].reshape(rank, ow)
            out = out + mm_nt(mixed[rows, j * ow : (j + 1) * ow], w_out)
        mid = xd[rows, :].astype(F32) + RESIDUAL_SCALE * out
        middle[rows, :] = mid
        mid16[rows, :] = mid.astype(BF)
        moe[rows, :] = (mid * row_scale(mid) * gain_m[...]).astype(BF)
        ms.start(b)

    place = pltpu.make_async_copy(moe, moe_all.at[0], local_sems.at[1])
    place.start()

    @pl.loop(0, nblk)
    def _(b):
        at = pl.ds(pl.multiple_of(b * tokens, tokens), tokens)
        lane = iota((tokens, LANES), 1)
        spot = jnp.zeros((tokens, LANES), F32)
        named = jnp.zeros((tokens, LANES), F32)
        there = pl.ds(pl.multiple_of((b ^ r) * tokens, tokens), tokens)
        own_ids = ids[there, :] ^ (r * local)
        own_spots = spots[there, :]
        for i in range(TOPK):
            hit = lane == own_ids[:, i : i + 1]
            named = jnp.where(hit, 1.0, named)
            spot = jnp.where(hit, own_spots[:, i : i + 1].astype(F32), spot)
        chosen[at, :] = named
        slot = jnp.where((named > 0.0) & (spot < capacity), spot, -1.0)
        slot_cols[at, :] = slot
        slot_rows[:, at] = slot.T[: slot_rows.shape[0], :]

    ms.forward(1)

    @pl.loop(0, nblk)
    def _(b):
        at = pl.ds(pl.multiple_of(b * tokens, tokens), tokens)
        found = jnp.zeros((tokens, LANES), F32)
        for j in range(nblk):
            part = slice(j * tokens, (j + 1) * tokens)
            match = iota((tokens, tokens), 0) + b * tokens == src_row[:, part]
            match = jnp.where(match, 1.0, 0.0).astype(BF)
            value = slot_cols[part, :] + 1.0
            high = jnp.floor(value * 0.0625)
            low = value - 16.0 * high
            found = found + 16.0 * mm(match, high.astype(BF)) + mm(match, low.astype(BF))
        slot_given[at, :] = found - 1.0
        given_rows[:, at] = (found - 1.0).T[: given_rows.shape[0], :]

    ms.wait((1, 0), (2, 1), (3, 0), (3, 1))
    place.wait()
    for gather in (xs, ws, ms):
        gather.drain()
    for copy in share:
        copy.wait_send()


def front(xin, w_half, src, starts, cos, sin, gain_a, gain_m, ids, spots, src_row, nblk, pairs):
    tokens, width = xin.shape
    shard, both = w_half.shape[1], w_half.shape[2] - LANES
    total = nblk * tokens
    qkv_width = nblk * both * 2 // 3
    head_width = nblk * both // 3
    shape = jax.ShapeDtypeStruct
    count = 3 * RowGather.count + nblk + 1
    local = EXPERT_COUNT // nblk
    return pl.pallas_call(
        front_kernel,
        out_shape=(
            shape((tokens, width), BF),
            shape((tokens, width), BF),
            shape((tokens, qkv_width), BF),
            shape((tokens, head_width), BF),
            shape((tokens, width), F32),
            shape((nblk, tokens, width), BF),
            shape((total, LANES), F32),
            shape((local, total), F32),
            shape((total, LANES), F32),
            shape((nblk, pairs, 2, shard, both), BF),
            shape((tokens, width), BF),
            shape((total, LANES), F32),
            shape((local, total), F32),
            shape((tokens, width), BF),
            shape((pairs, 2, shard, LANES), BF),
        ),
        in_specs=[ANY] * 2 + [FULL] * 9,
        out_specs=[FULL] * 5 + [ANY] + [FULL] * 9,
        scratch_shapes=[
            pltpu.VMEM((nblk, tokens, width), BF),
            pltpu.VMEM((tokens // 2, tokens), F32),
            pltpu.SemaphoreType.DMA((2, count)),
            pltpu.SemaphoreType.DMA((2 + 2 * pairs,)),
        ],
        compiler_params=pltpu.CompilerParams(
            vmem_limit_bytes=58 * MIB, collective_id=1, has_side_effects=True
        ),
        cost_estimate=cost(20e9, 60 * MIB),
        name="attention_forward",
    )(xin, w_half, src, starts, cos, sin, gain_a, gain_m, ids, spots, src_row)


def router_kernel(moe, w_router, chosen, gates, packed):
    nblk, tokens, _ = moe.shape
    local = EXPERT_COUNT // nblk
    for j in range(nblk):
        at = slice(j * tokens, (j + 1) * tokens)
        logits = mm(moe[j], w_router[...])
        named = chosen[at, :] > 0.0
        logits = jnp.where(named, logits, MASKED)
        top = jnp.max(logits, axis=-1, keepdims=True)
        raised = jnp.where(named, jnp.exp(logits - top), 0.0)
        gate = raised / jnp.sum(raised, axis=-1, keepdims=True)
        gates[at, :] = gate
        lane = iota((tokens, LANES), 1)
        own = jnp.where(lane < local, gate, 0.0)
        high = own.astype(BF).astype(F32)
        rest = own - high
        mid = rest.astype(BF).astype(F32)
        low = rest - mid
        packed[at, :] = (high + pltpu.roll(mid, local, 1) + pltpu.roll(low, 2 * local, 1)).astype(BF)


def router(moe, w_router, chosen):
    nblk, tokens, _ = moe.shape
    total = nblk * tokens
    shape = jax.ShapeDtypeStruct
    return pl.pallas_call(
        router_kernel,
        out_shape=(shape((total, LANES), F32), shape((total, LANES), BF)),
        in_specs=[FULL] * 3,
        out_specs=[FULL] * 2,
        compiler_params=params(24),
        cost_estimate=cost(1e9, 7 * MIB),
        name="router",
    )(moe, w_router, chosen)


class RowScatter:
    count = 6

    def __init__(self, block, mixed_in, across, landed, sems, base, r, c):
        near, far = (r ^ 1, c), (r ^ 2, c)
        self.copies = {
            "diag0": link(block(3, 0), across(0), sems, base, near),
            "diag1": link(block(3, 1), across(1), sems, base + 1, far),
            "near0": link(block(1, 0), landed(1, 0), sems, base + 2, near),
            "far1": link(block(2, 1), landed(2, 1), sems, base + 3, far),
        }
        if mixed_in is not None:
            self.copies["far0"] = link(mixed_in(0), landed(2, 0), sems, base + 4, far)
            self.copies["near1"] = link(mixed_in(1), landed(1, 1), sems, base + 5, near)

    def start(self):
        for key in ("diag0", "diag1", "near0", "far1"):
            self.copies[key].start()

    def arrived(self, half):
        self.copies["diag0" if half == 0 else "diag1"].wait_recv()

    def send(self, half):
        self.copies["far0" if half == 0 else "near1"].start()

    def finish(self):
        for key in self.copies:
            if not key.startswith("diag"):
                self.copies[key].wait_recv()

    def drain(self):
        for copy in self.copies.values():
            copy.wait_send()


def tree_sum(parts):
    while len(parts) > 1:
        parts = [parts[i] + parts[i + 1] for i in range(0, len(parts), 2)]
    return parts[0]


def plus(a, b):
    return (a.astype(F32) + b.astype(F32)).astype(BF)


def one_hot(hit):
    return jnp.where(hit, 1.0, 0.0).astype(BF)


def lane_column(table, index):
    return jnp.sum(jnp.where(iota(table.shape, 1) == index, table, 0.0), axis=1, keepdims=True)


def split_three(value):
    high = value.astype(BF).astype(F32)
    rest = value - high
    mid = rest.astype(BF).astype(F32)
    return high, mid, rest - mid


def forward_kernel(base, first, last, gathers, local, capacity, *refs):
    moe_hbm, slot_rows, slot_given, packed, w = refs[:5]
    refs = refs[5:]
    if not first:
        acc_in, refs = refs[0], refs[1:]
    if gathers:
        own_hbm, refs = refs[0], refs[1:]
    routed_out, gate_out, up_out, weight_out, acc_out = refs[:5]
    refs = refs[5:]
    if gathers:
        all_hbm, refs = refs[0], refs[1:]
    moe, acc, sel, given, y1, sems = refs[:6]
    step = pl.program_id(0)
    steps = pl.num_programs(0)
    e = base + step
    ne = y1.shape[0] // capacity
    nblk, tokens, width = moe_hbm.shape
    fe = w.shape[3] // 3
    copies = [
        pltpu.make_async_copy(moe_hbm.at[j], moe.at[pl.ds(j * tokens, tokens)], sems.at[j])
        for j in range(nblk)
    ]
    if not first:
        load = pltpu.make_async_copy(acc_in, acc, sems.at[nblk])
    if gathers:
        link_sems = refs[6]
        r = lax.axis_index("row")
        c = lax.axis_index("col")
        half = tokens // 2
        gather = RowGather(
            lambda h: own_hbm.at[pl.ds(h * half, half)],
            lambda j, h: all_hbm.at[j, pl.ds(h * half, half)],
            link_sems,
            0,
            r,
            c,
        )
        keep = pltpu.make_async_copy(own_hbm, all_hbm.at[0], sems.at[nblk + 1])

    @pl.when(step == 0)
    def _():
        for copy in copies:
            copy.start()
        if not first:
            load.start()
        if gathers:
            keep.start()
            greet([(r ^ 1, c), (r ^ 2, c)])
            gather.start(0)
            gather.start(1)

    row = slot_rows[pl.ds(e, 1), :]
    for j in range(nblk):
        at = slice(j * tokens, (j + 1) * tokens)
        sel[:, at] = one_hot(iota((capacity, tokens), 0).astype(F32) == row[:, at])

    @pl.when(step == 0)
    def _():
        for copy in copies:
            copy.wait()

    if gathers:

        @pl.when(step == steps - 1)
        def _():
            gather.forward(0)
            gather.forward(1)

    routed_out[0] = mm(sel[...], moe[...]).astype(BF)
    lane = iota((capacity, LANES), 1)
    picked = mm(sel[...], packed[...])
    mine = (lane == e) | (lane == e + local) | (lane == e + 2 * local)
    gate = jnp.sum(jnp.where(mine, picked, 0.0), axis=1, keepdims=True)
    weight_out[0] = jnp.broadcast_to(gate, (capacity, LANES))
    gate_up = mm(routed_out[0], w[:, 0, :, : 2 * fe].reshape(width, 2 * fe))
    gate_in = gate_up[:, :fe]
    up_in = gate_up[:, fe:]
    gate_out[0] = gate_in
    up_out[0] = up_in
    hidden = (gate_in * jax.nn.sigmoid(gate_in) * up_in).astype(BF)
    out = mm_nt(hidden, w[:, 0, :, 2 * fe :].reshape(width, fe))
    y1[pl.ds(pl.multiple_of(step * capacity, capacity), capacity), :] = (gate * out).astype(BF)

    @pl.when(step == steps - 1)
    def _():
        if not first:
            load.wait()

        def put(b):
            at = pl.ds(pl.multiple_of(b * tokens, tokens), tokens)
            if last:
                return pltpu.make_async_copy(moe.at[at], acc_out.at[b], sems.at[b])
            return pltpu.make_async_copy(acc.at[at], acc_out.at[at], sems.at[b])

        @pl.loop(0, nblk)
        def _(b):
            at = pl.ds(pl.multiple_of(b * tokens, tokens), tokens)
            slots = iota((tokens, capacity), 1).astype(F32)
            for i in range(ne):
                given[:, i * capacity : (i + 1) * capacity] = one_hot(
                    lane_column(slot_given[at, :], base + i) == slots
                )
            part = mm(given[...], y1[...])
            if not first:
                part = part + acc[at, :]
            if last:
                moe[at, :] = part.astype(BF)
            else:
                acc[at, :] = part
            put(b).start()

        if gathers:
            gather.wait((1, 0), (2, 1), (3, 0), (3, 1))
            keep.wait()
            gather.drain()
        for b in range(nblk):
            put(b).wait()


def experts_forward(moe, slot_rows, slot_given, packed, w, acc, own, base, last, capacity, key):
    nblk, tokens, width = moe.shape
    total = nblk * tokens
    cols, ne, shard, fe3 = w.shape
    fe = fe3 // 3
    local = EXPERT_COUNT // nblk
    first = acc is None
    gathers = own is not None
    shape = jax.ShapeDtypeStruct
    wspec = pl.BlockSpec((cols, 1, shard, fe3), lambda s: (0, s, 0, 0))

    def each(*dims):
        return pl.BlockSpec((1, *dims), lambda s: (s, 0, 0))

    ins = [moe, slot_rows, slot_given, packed, w]
    in_specs = [ANY, FULL, FULL, FULL, wspec]
    aliases = {}
    if not first:
        ins.append(acc)
        in_specs.append(ANY)
        if not last:
            aliases = {len(ins) - 1: 4}
    outs = [
        shape((ne, capacity, width), BF),
        shape((ne, capacity, fe), F32),
        shape((ne, capacity, fe), F32),
        shape((ne, capacity, LANES), F32),
        shape((nblk, tokens, width), BF) if last else shape((total, width), F32),
    ]
    out_specs = [each(capacity, width), each(capacity, fe), each(capacity, fe), each(capacity, LANES), ANY]
    scratch = [
        pltpu.VMEM((total, width), BF),
        pltpu.VMEM((total, width), F32),
        pltpu.VMEM((capacity, total), BF),
        pltpu.VMEM((tokens, ne * capacity), BF),
        pltpu.VMEM((ne * capacity, width), BF),
        pltpu.SemaphoreType.DMA((nblk + 2,)),
    ]
    options = dict(vmem_limit_bytes=58 * MIB)
    if gathers:
        ins.append(own)
        in_specs.append(ANY)
        outs.append(shape((nblk, tokens, width), BF))
        out_specs.append(ANY)
        scratch.append(pltpu.SemaphoreType.DMA((2, RowGather.count)))
        options.update(collective_id=key, has_side_effects=True)
    return pl.pallas_call(
        functools.partial(forward_kernel, base, first, last, gathers, local, capacity),
        grid=(ne,),
        out_shape=outs,
        in_specs=in_specs,
        out_specs=out_specs,
        scratch_shapes=scratch,
        input_output_aliases=aliases,
        compiler_params=pltpu.CompilerParams(**options),
        cost_estimate=cost(7e9 * ne, 30 * MIB),
        name="experts_forward",
    )(*ins)


def reverse_kernel(base, first, last, local, capacity, *refs):
    cot_hbm, given_rows, slot_cols, routed, gate_in_ref, up_in_ref, weight_ref, w = refs[:8]
    refs = refs[8:]
    if not first:
        acc_in, accg_in = refs[:2]
        refs = refs[2:]
    if last:
        es, refs = refs[0], refs[1:]
    grads, acc_out, accg_out = refs[:3]
    refs = refs[3:]
    if last:
        e_mix, e_across, e_landed = refs[:3]
        refs = refs[3:]
    cot, acc, accg, sel, chosen, spread, dsl, dslot, y2, sems = refs[:10]
    step = pl.program_id(0)
    steps = pl.num_programs(0)
    e = base + step
    nblk, tokens, width = cot_hbm.shape
    half = tokens // 2
    cols, _, shard, fe = w.shape
    fe = fe // 3
    ne = y2.shape[0] // capacity
    copies = [
        pltpu.make_async_copy(cot_hbm.at[j], cot.at[pl.ds(j * tokens, tokens)], sems.at[j])
        for j in range(nblk)
    ]
    if not first:
        loads = [
            pltpu.make_async_copy(acc_in, acc, sems.at[nblk]),
            pltpu.make_async_copy(accg_in, accg, sems.at[nblk + 1]),
        ]
    if last:
        e_vmem, link_sems = refs[10:]
        r = lax.axis_index("row")
        c = lax.axis_index("col")
        scatter = RowScatter(
            lambda j, h: es.at[j, pl.ds(h * half, half)],
            None,
            lambda h: e_across.at[h],
            lambda j, h: e_landed.at[h],
            link_sems,
            0,
            r,
            c,
        )

    @pl.when(step == 0)
    def _():
        for copy in copies:
            copy.start()
        if not first:
            for copy in loads:
                copy.start()
        if last:
            greet([(r ^ 1, c), (r ^ 2, c)])
            scatter.start()

    row = given_rows[pl.ds(e, 1), :]
    for j in range(nblk):
        at = slice(j * tokens, (j + 1) * tokens)
        sel[:, at] = one_hot(iota((capacity, tokens), 0).astype(F32) == row[:, at])

    @pl.when(step == 0)
    def _():
        for copy in copies:
            copy.wait()

    gate = weight_ref[0, :, :1]

    rows = (RESIDUAL_SCALE * mm(sel[...], cot[...])).astype(BF)
    dsl[...] = rows
    dslot[...] = (gate * rows.astype(F32)).astype(BF)
    gate_in = gate_in_ref[0]
    up_in = up_in_ref[0]
    sig = jax.nn.sigmoid(gate_in)
    silu = gate_in * sig
    hidden = (silu * up_in).astype(BF)
    dhidden = mm(dslot[...], w[:, 0, :, 2 * fe :].reshape(width, fe))
    dgate = (dhidden * up_in * sig * (1.0 + gate_in * (1.0 - sig))).astype(BF)
    dup = (dhidden * silu).astype(BF)
    both = jnp.concatenate([dgate, dup], axis=1)
    out = mm_nt(hidden, w[:, 0, :, 2 * fe :].reshape(width, fe))
    inner = jnp.sum(dsl[...].astype(F32) * out, axis=1, keepdims=True)
    grads[:, 0, :, 2 * fe :] = mm_tn(dslot[...], hidden).astype(BF).reshape(cols, shard, fe)
    grads[:, 0, :, : 2 * fe] = mm_tn(routed[0], both).astype(BF).reshape(cols, shard, 2 * fe)
    mine = pl.ds(pl.multiple_of(step * capacity, capacity), capacity)
    y2[mine, :] = mm_nt(both, w[:, 0, :, : 2 * fe].reshape(width, 2 * fe)).astype(BF)
    high, mid, low = split_three(inner)
    lane = iota((capacity, LANES), 1)
    spread[mine, :] = jnp.where(
        lane == e,
        high,
        jnp.where(lane == e + local, mid, jnp.where(lane == e + 2 * local, low, 0.0)),
    ).astype(BF)

    @pl.when(step == steps - 1)
    def _():
        if not first:
            for copy in loads:
                copy.wait()

        def put(b):
            at = pl.ds(pl.multiple_of(b * tokens, tokens), tokens)
            if last:
                return pltpu.make_async_copy(cot.at[at], acc_out.at[b], sems.at[b])
            return pltpu.make_async_copy(acc.at[at], acc_out.at[at], sems.at[b])

        @pl.loop(0, nblk)
        def _(b):
            at = pl.ds(pl.multiple_of(b * tokens, tokens), tokens)
            slots = iota((tokens, capacity), 1).astype(F32)
            for i in range(ne):
                chosen[:, i * capacity : (i + 1) * capacity] = one_hot(
                    lane_column(slot_cols[at, :], base + i) == slots
                )
            part = mm(chosen[...], y2[...])
            partg = mm(chosen[...], spread[...])
            if not first:
                part = part + acc[at, :]
                partg = partg + accg[at, :]
            if last:
                cot[at, :] = part.astype(BF)
            else:
                acc[at, :] = part
            accg[at, :] = partg
            put(b).start()

        if last:
            summed = accg[...]
            summed = (
                summed
                + pltpu.roll(summed, LANES - local, 1)
                + pltpu.roll(summed, LANES - 2 * local, 1)
            )
            accg_out[...] = summed.T[:local, :]
            for h in range(2):
                scatter.arrived(h)
                gets = [
                    pltpu.make_async_copy(
                        es.at[2 - h, pl.ds(h * half, half)], e_vmem.at[0], sems.at[nblk]
                    ),
                    pltpu.make_async_copy(e_across.at[h], e_vmem.at[1], sems.at[nblk + 1]),
                ]
                for copy in gets:
                    copy.start()
                for copy in gets:
                    copy.wait()
                e_vmem[0] = plus(e_vmem[0], e_vmem[1])
                back = pltpu.make_async_copy(e_vmem.at[0], e_mix.at[h], sems.at[nblk])
                back.start()
                back.wait()
            scatter.finish()
            scatter.drain()
        else:
            out_g = pltpu.make_async_copy(accg, accg_out, sems.at[nblk])
            out_g.start()
            out_g.wait()
        for b in range(nblk):
            put(b).wait()


def experts_reverse(cot, given_rows, slot_cols, kept, w, carried, es, base, last, capacity, key):
    nblk, tokens, width = cot.shape
    half = tokens // 2
    total = nblk * tokens
    cols, ne, shard, fe3 = w.shape
    fe = fe3 // 3
    local = EXPERT_COUNT // nblk
    first = carried is None
    shape = jax.ShapeDtypeStruct
    wspec = pl.BlockSpec((cols, 1, shard, fe3), lambda s: (0, s, 0, 0))

    def each(*dims):
        return pl.BlockSpec((1, *dims), lambda s: (s, 0, 0))

    ins = [cot, given_rows, slot_cols, *kept, w]
    in_specs = [
        ANY,
        FULL,
        FULL,
        each(capacity, width),
        each(capacity, fe),
        each(capacity, fe),
        each(capacity, LANES),
        wspec,
    ]
    aliases = {}
    if not first:
        ins += list(carried)
        in_specs += [ANY, ANY]
        if not last:
            aliases = {len(ins) - 2: 1, len(ins) - 1: 2}
    if last:
        outs = [
            shape(w.shape, BF),
            shape((nblk, tokens, width), BF),
            shape((local, total), F32),
            shape((2, half, width), BF),
            shape((2, half, width), BF),
            shape((2, half, width), BF),
        ]
        out_specs = [wspec, ANY, FULL, ANY, ANY, ANY]
        ins.append(es)
        in_specs.append(ANY)
    else:
        outs = [shape(w.shape, BF), shape((total, width), F32), shape((total, LANES), F32)]
        out_specs = [wspec, ANY, ANY]
    scratch = [
        pltpu.VMEM((total, width), BF),
        pltpu.VMEM((total, width), F32),
        pltpu.VMEM((total, LANES), F32),
        pltpu.VMEM((capacity, total), BF),
        pltpu.VMEM((tokens, ne * capacity), BF),
        pltpu.VMEM((ne * capacity, LANES), BF),
        pltpu.VMEM((capacity, width), BF),
        pltpu.VMEM((capacity, width), BF),
        pltpu.VMEM((ne * capacity, width), BF),
        pltpu.SemaphoreType.DMA((nblk + 2,)),
    ]
    options = dict(vmem_limit_bytes=58 * MIB)
    if last:
        scratch += [
            pltpu.VMEM((2, half, width), BF),
            pltpu.SemaphoreType.DMA((2, RowScatter.count)),
        ]
        options.update(collective_id=key, has_side_effects=True)
    return pl.pallas_call(
        functools.partial(reverse_kernel, base, first, last, local, capacity),
        grid=(ne,),
        out_shape=outs,
        in_specs=in_specs,
        out_specs=out_specs,
        scratch_shapes=scratch,
        input_output_aliases=aliases,
        compiler_params=pltpu.CompilerParams(**options),
        cost_estimate=cost(9e9 * ne, 40 * MIB),
        name="experts_reverse",
    )(*ins)


def back_kernel(nblk, *refs):
    dm, es, e_mix, e_half, dgates, mids, cot = refs[:7]
    refs = refs[7:]
    (gates, middle, moe, src_col, mixed, qkv, attn, xd, w_att, w_router) = refs[:10]
    (starts, cos, sin, gain_a, gain_m, src_row) = refs[10:16]
    (block_out, input_grad, att_grad, small, e_rest) = refs[16:21]
    (own, d_across, d_landed, dg_land, igb, dmid, dmix, dproj, dkv, bias, wg, wg_sib) = refs[21:33]
    (w_across, w_landed, w_z, rowsum, s_own, s_sib, s_sum, s_row, s_chip, s_z, sems, lsems) = refs[33:]
    tokens, width = xd.shape
    half = tokens // 2
    local = EXPERT_COUNT // nblk
    pairs = w_att.shape[1]
    shard = w_att.shape[3]
    qw = w_att.shape[4] * 2 // 3
    ow = w_att.shape[4] - qw
    hw = HEAD_WIDTH
    r = lax.axis_index("row")
    c = lax.axis_index("col")
    z = c // 2
    k = c % 2
    row_peers = [(r ^ j, c) for j in range(1, nblk)]
    z_peers = [(r, 2 * (z ^ i) + k) for i in range(1, pairs)]
    sibling = (r, c ^ 1)
    greet(row_peers + z_peers + [sibling])

    def part(h):
        return pl.ds(h * half, half)

    zhalf = pairs // 2

    def zpart(h):
        return pl.ds(h * zhalf, zhalf)

    n = RowScatter.count
    dms = RowScatter(
        lambda j, h: dm.at[j, part(h)],
        lambda h: own.at[2 - h, part(h)],
        lambda h: d_across.at[h],
        lambda j, h: d_landed.at[j - 1, part(h)],
        sems,
        0,
        r,
        c,
    )
    ess = [
        link(e_mix.at[0], e_rest.at[0], sems, n, (r ^ 2, c)),
        link(e_mix.at[1], e_rest.at[1], sems, n + 1, (r ^ 1, c)),
    ]
    wgs = RowScatter(
        lambda j, h: wg.at[j, zpart(h), k],
        lambda h: wg.at[2 - h, zpart(h), k],
        lambda h: w_across.at[h],
        lambda j, h: w_landed.at[j - 1, zpart(h)],
        sems,
        2 * n,
        r,
        c,
    )
    igs = RowGather(
        lambda h: igb.at[0, part(h)], lambda j, h: igb.at[j, part(h)], sems, 3 * n, r, c
    )
    at = 3 * n + RowGather.count
    dgs = [
        link(dgates.at[:, pl.ds(j * tokens, tokens)], dg_land.at[j - 1], sems, at + j - 1, (r ^ j, c))
        for j in range(1, nblk)
    ]
    at += nblk - 1
    wg_share = [
        link(wg.at[j, :, 1 - k], wg_sib.at[j], sems, at + j, sibling) for j in range(nblk)
    ]
    at += nblk
    wg_z = [
        link(rowsum.at[z ^ i], w_z.at[i - 1], sems, at + i - 1, z_peers[i - 1])
        for i in range(1, pairs)
    ]
    at += pairs - 1
    s_share = link(s_own, s_sib, sems, at, sibling)
    s_rows = [link(s_sum, s_row.at[j], sems, at + 1 + j, row_peers[j]) for j in range(nblk - 1)]
    at += nblk
    s_zs = [link(s_chip, s_z.at[i], sems, at + i, z_peers[i]) for i in range(pairs - 1)]

    dms.start()
    for copy in dgs:
        copy.start()
    loads = [
        pltpu.make_async_copy(dm.at[0], own.at[0], lsems.at[0]),
        pltpu.make_async_copy(dm.at[1, part(1)], own.at[1, part(1)], lsems.at[1]),
        pltpu.make_async_copy(dm.at[2, part(0)], own.at[2, part(0)], lsems.at[2]),
        pltpu.make_async_copy(middle, dmid, lsems.at[3]),
    ]
    for copy in loads:
        copy.start()

    def match(j):
        hit = iota((tokens, tokens), 0) == src_row[:, j * tokens : (j + 1) * tokens]
        return jnp.where(hit, 1.0, 0.0).astype(BF)

    total = jnp.zeros((tokens, width), F32)
    for j in range(nblk):
        get = pltpu.make_async_copy(mids.at[j], dmix, lsems.at[4])
        get.start()
        hit = match(j)
        get.wait()
        total = total + mm(hit, dmix[...])
    input_grad[...] = total
    dy = jnp.zeros((tokens, width), F32)
    for j in range(nblk):
        get = pltpu.make_async_copy(cot.at[j], dmix, lsems.at[4])
        get.start()
        hit = one_hot(src_col[...] == iota((tokens, tokens), 1) + j * tokens)
        get.wait()
        dy = dy + mm(hit, dmix[...])
    dproj[:, :width] = dy.astype(BF)
    for copy in loads:
        copy.wait()
    for h in range(2):
        dms.arrived(h)
        rows = part(h)
        own[2 - h, rows, :] = plus(own[2 - h, rows, :], d_across[h])
        dms.send(h)

    for copy in dgs:
        copy.wait_recv()
    parts = [dgates[:, :tokens]] + [dg_land[j] for j in range(nblk - 1)]
    pad = jnp.zeros((LANES - EXPERT_COUNT, tokens), F32)
    dgate = jnp.concatenate(parts + [pad], axis=0).T
    gate = gates[...]
    dchosen = gate * (dgate - jnp.sum(gate * dgate, axis=1, keepdims=True))
    dlogits = dchosen.astype(BF)
    router_t = mm_tn(dlogits, moe[...])
    for j in range(nblk):
        s_own[pl.ds(pl.multiple_of((r ^ j) * local, local), local), :] = router_t[
            j * local : (j + 1) * local, :
        ]
    dmoe = mm_nt(dlogits, w_router[...]) + own[0].astype(F32)
    dms.finish()
    for copy in ess:
        copy.start()
    dmoe = dmoe + (d_landed[0].astype(F32) + d_landed[1].astype(F32))
    mid = dmid[...]
    rr = row_scale(mid)
    scaled = dmoe * gain_m[...]
    inner = jnp.mean(scaled * mid, axis=-1, keepdims=True)
    gain_m_part = jnp.sum(dmoe * mid * rr, axis=0, keepdims=True)
    dmid[...] = dproj[:, :width].astype(F32) + (rr * scaled - mid * (rr * rr * rr) * inner)
    dattn = (RESIDUAL_SCALE * dmid[...]).astype(BF)
    for j in range(nblk):
        cols = slice(j * ow, (j + 1) * ow)
        dmix[:, cols] = mm(dattn, w_att[j, :, :, :, qw:].reshape(width, ow)).astype(BF)
        wg[j, :, :, :, qw:] = (
            mm_tn(dattn, mixed[:, cols]).astype(BF).reshape(pairs, 2, shard, ow)
        )

    quad = 4 * hw
    groups = nblk * qw // quad
    gain_a_part = jnp.zeros((1, width), F32)
    for b in (1, 0):
        span = (b + 1) * half
        rows = slice(b * half, (b + 1) * half)
        bias[:, :span] = attention_bias(b * half, half, span, starts[rows, :])

        @pl.loop(0, groups)
        def _(g):
            chunk = qkv[:span, pl.ds(pl.multiple_of(g * quad, quad), quad)]
            dm_chunk = dmix[rows, pl.ds(pl.multiple_of(g * 2 * hw, 2 * hw), 2 * hw)]
            k_rows = chunk[:, 2 * hw : 3 * hw]
            v_rows = chunk[:, 3 * hw :]
            dk = jnp.zeros((span, hw), F32)
            dv = jnp.zeros((span, hw), F32)
            dqs = []
            for h in range(2):
                q = chunk[b * half :, h * hw : (h + 1) * hw]
                dmh = dm_chunk[:, h * hw : (h + 1) * hw]
                probs = masked_probs(q, k_rows, bias[:, :span])
                dprobs = mm_nt(dmh, v_rows)
                total = jnp.sum(probs * dprobs, axis=-1, keepdims=True)
                dscores = (probs * (dprobs - total)).astype(BF)
                dqs.append(mm(dscores, k_rows))
                dk = dk + mm_tn(dscores, q)
                dv = dv + mm_tn(probs.astype(BF), dmh)
            dkv_new = jnp.concatenate([dk, dv], axis=1)
            pair = pl.ds(pl.multiple_of(g * 2 * hw, 2 * hw), 2 * hw)
            if b == 1:
                dkv[:, pair] = dkv_new[:half]
                dkv_own = dkv_new[half:]
            else:
                dkv_own = dkv_new + dkv[:, pair]
            d = jnp.concatenate(dqs + [dkv_own], axis=1)
            d = d * cos[rows, :] - swap_halves(d) * sin[rows, :]
            dproj[rows, pl.ds(pl.multiple_of(g * quad, quad), quad)] = d.astype(BF)

        dattn_in = jnp.zeros((half, width), F32)
        for j in range(nblk):
            dattn_in = dattn_in + mm_nt(
                dproj[rows, j * qw : (j + 1) * qw],
                w_att[j, :, :, :, :qw].reshape(width, qw),
            )
        x = xd[rows, :].astype(F32)
        rx = row_scale(x)
        scaled = dattn_in * gain_a[...]
        inner = jnp.mean(scaled * x, axis=-1, keepdims=True)
        igb[0, rows, :] = (dmid[rows, :] + (rx * scaled - x * (rx * rx * rx) * inner)).astype(BF)
        gain_a_part = gain_a_part + jnp.sum(dattn_in * x * rx, axis=0, keepdims=True)
        igs.start(b)

    s_own[EXPERT_COUNT : EXPERT_COUNT + 8, :] = jnp.concatenate(
        [gain_a_part, gain_m_part, jnp.zeros((6, width), F32)], axis=0
    )
    s_share.start()
    for j in range(nblk):
        wg[j, :, :, :, :qw] = (
            mm_tn(attn[...], dproj[:, j * qw : (j + 1) * qw])
            .astype(BF)
            .reshape(pairs, 2, shard, qw)
        )
        wg_share[j].start()
    igs.forward(1)
    igs.forward(0)
    s_share.wait_recv()
    s_sum[...] = s_own[...] + s_sib[...]
    for copy in s_rows:
        copy.start()
    for j in (3, 1, 2, 0):
        wg_share[j].wait_recv()
        wg[j, :, pl.ds(k, 1)] = plus(wg[j, :, pl.ds(k, 1)], wg_sib[j][:, None])
    wgs.start()

    for copy in ess:
        copy.wait_recv()
    e_gets = [
        pltpu.make_async_copy(es.at[0], own.at[0], lsems.at[0]),
        pltpu.make_async_copy(e_half.at[0], own.at[1, part(0)], lsems.at[1]),
        pltpu.make_async_copy(e_half.at[1], own.at[1, part(1)], lsems.at[2]),
        pltpu.make_async_copy(e_rest.at[0], own.at[2, part(0)], lsems.at[3]),
        pltpu.make_async_copy(e_rest.at[1], own.at[2, part(1)], lsems.at[4]),
    ]
    dms.drain()
    for copy in e_gets:
        copy.start()
    for copy in e_gets:
        copy.wait()
    rest = own[2].astype(F32)
    summed = own[0].astype(F32) + (own[1].astype(F32) + rest)
    block_out[...] = (input_grad[...] + RESIDUAL_SCALE * summed).astype(BF)

    for h in range(2):
        wgs.arrived(h)
        hz = zpart(h)
        wg[2 - h, hz, pl.ds(k, 1)] = plus(wg[2 - h, hz, pl.ds(k, 1)], w_across[h][:, None])
        wgs.send(h)
    for copy in s_rows:
        copy.wait_recv()
    s_chip[...] = tree_sum([s_sum[...]] + [s_row[j] for j in range(nblk - 1)])
    for copy in s_zs:
        copy.start()
    igs.wait((1, 0), (2, 1))
    total = mm(match(0), igb[0])
    for j in (1, 2):
        total = total + mm(match(j), igb[j])
    igs.wait((3, 0), (3, 1))
    total = total + mm(match(3), igb[3])
    input_grad[...] = total
    wgs.finish()
    rowsum[...] = (
        wg[0, :, pl.ds(k, 1)].reshape(rowsum.shape).astype(F32)
        + (w_landed[0].astype(F32) + w_landed[1].astype(F32))
    ).astype(BF)
    for copy in wg_z:
        copy.start()
    for copy in s_zs:
        copy.wait_recv()
    small[...] = tree_sum([s_chip[...]] + [s_z[i] for i in range(pairs - 1)])
    for copy in wg_z:
        copy.wait_recv()
    att_grad[...] = tree_sum(
        [rowsum[pl.ds(z, 1)].reshape(att_grad.shape).astype(F32)]
        + [w_z[i].astype(F32) for i in range(pairs - 1)]
    )
    for group in (wgs, igs):
        group.drain()
    for copy in ess + dgs + wg_share + wg_z + [s_share] + s_rows + s_zs:
        copy.wait_send()


def backward(dm, es, e_mix, e_half, dgates, mids, cot, *rest):
    nblk, tokens, width = dm.shape
    w_att = rest[8]
    pairs, shard, both = w_att.shape[1], w_att.shape[3], w_att.shape[4]
    half = tokens // 2
    local = EXPERT_COUNT // nblk
    shape = jax.ShapeDtypeStruct
    count = (
        3 * RowScatter.count
        + RowGather.count
        + (nblk - 1)
        + nblk
        + (pairs - 1)
        + 1
        + (nblk - 1)
        + (pairs - 1)
    )
    small = (EXPERT_COUNT + 8, width)
    outs = pl.pallas_call(
        functools.partial(back_kernel, nblk),
        out_shape=(
            shape((tokens, width), BF),
            shape((tokens, width), F32),
            shape((shard, both), F32),
            shape(small, F32),
            shape((2, half, width), BF),
        ),
        in_specs=[ANY] * 4 + [FULL] + [ANY] * 2 + [FULL, ANY] + [FULL] * 14,
        out_specs=[FULL] * 4 + [ANY],
        scratch_shapes=[
            pltpu.VMEM((3, tokens, width), BF),
            pltpu.VMEM((2, half, width), BF),
            pltpu.VMEM((2, tokens, width), BF),
            pltpu.VMEM((nblk - 1, local, tokens), F32),
            pltpu.VMEM((nblk, tokens, width), BF),
            pltpu.VMEM((tokens, width), F32),
            pltpu.VMEM((tokens, width), BF),
            pltpu.VMEM((tokens, 2 * width), BF),
            pltpu.VMEM((half, width), F32),
            pltpu.VMEM((half, tokens), F32),
            pltpu.VMEM(w_att.shape, BF),
            pltpu.VMEM((nblk, pairs, shard, both), BF),
            pltpu.VMEM((2, pairs // 2, shard, both), BF),
            pltpu.VMEM((2, pairs, shard, both), BF),
            pltpu.VMEM((pairs - 1, shard, both), BF),
            pltpu.VMEM((pairs, shard, both), BF),
            pltpu.VMEM(small, F32),
            pltpu.VMEM(small, F32),
            pltpu.VMEM(small, F32),
            pltpu.VMEM((nblk - 1, *small), F32),
            pltpu.VMEM(small, F32),
            pltpu.VMEM((pairs - 1, *small), F32),
            pltpu.SemaphoreType.DMA((2, count)),
            pltpu.SemaphoreType.DMA((8,)),
        ],
        compiler_params=pltpu.CompilerParams(
            vmem_limit_bytes=62 * MIB, collective_id=2, has_side_effects=True
        ),
        cost_estimate=cost(60e9, 100 * MIB),
        name="attention_backward",
    )(dm, es, e_mix, e_half, dgates, mids, cot, *rest)
    return outs[:4]


def swap_over(value, axis, size, step):
    return lax.ppermute(value, axis, [(i, i ^ step) for i in range(size)])


def spread_rows(value, axis, size, step=1):
    return [value] + [swap_over(value, axis, size, j) for j in range(step, size, step)]


def body(
    block_in,
    cotangent,
    seq_lengths,
    seq_order,
    expert_ids,
    places,
    attn_gain,
    w_qkv,
    w_out,
    moe_gain,
    w_router,
    w_gate,
    w_up,
    w_down,
):
    tokens = block_in.shape[1]
    width = block_in.shape[2]
    rows = lax.axis_size("row")
    cols = lax.axis_size("col")
    total = tokens * rows
    r = lax.axis_index("row")
    c = lax.axis_index("col")
    local = w_gate.shape[1]
    shard = w_gate.shape[0]
    fe = w_gate.shape[2]
    capacity = total * TOPK // EXPERT_COUNT
    pairs = cols // 2
    qw = w_qkv.shape[1]
    ow = w_out.shape[1]

    router_own = jnp.concatenate(
        [lax.dynamic_slice_in_dim(w_router, (r ^ j) * local, local, 1) for j in range(rows)], axis=1
    )
    router_own = jnp.pad(router_own, ((0, 0), (0, LANES - EXPERT_COUNT)))
    w_half = jnp.stack(
        spread_rows(jnp.concatenate([w_qkv, w_out, router_own], axis=1), "col", cols, 2)
    )

    stacked = jnp.concatenate([w_gate, w_up, w_down], axis=2).transpose(1, 0, 2)
    sizes = [local - 2 * (local * 3 // 8), local * 3 // 8, local * 3 // 8][::-1]
    bases = [sum(sizes[:i]) for i in range(len(sizes))]
    gathered = [
        lax.all_gather(stacked[i : i + n], "col", axis=0) for i, n in zip(bases, sizes)
    ]

    lengths = seq_lengths[0]
    perm = seq_order[0]
    seq_ids = jnp.arange(lengths.shape[0], dtype=jnp.int32)
    picked = perm[:, None] == seq_ids[None, :]
    dealt_len = jnp.sum(jnp.where(picked, lengths[None, :], 0), axis=1)
    before = seq_ids[None, :] < perm[:, None]
    source_base = jnp.sum(jnp.where(before, lengths[None, :], 0), axis=1)
    upto = seq_ids[None, :] <= seq_ids[:, None]
    seq_ends = jnp.sum(jnp.where(upto, dealt_len[None, :], 0), axis=1)
    dealt_start = seq_ends - dealt_len
    turn = r * tokens
    pos = jnp.arange(total, dtype=jnp.int32) ^ turn
    inside = (pos[:, None] >= dealt_start[None, :]) & (pos[:, None] < seq_ends[None, :])
    seq_starts = jnp.sum(jnp.where(inside, dealt_start[None, :], 0), axis=1)
    offset = pos - seq_starts
    source = jnp.sum(jnp.where(inside, source_base[None, :], 0), axis=1) + offset
    source = source ^ turn
    src_col = source[:, None]
    src_row = source[None, :]
    own_offset = offset[:tokens]
    own_starts = (seq_starts[:tokens] - turn)[:, None]

    half = HEAD_WIDTH // 2
    frequency = ROPE_BASE ** (-jnp.arange(half, dtype=F32) * 2.0 / HEAD_WIDTH)
    turned = own_offset.astype(F32)[:, None] * frequency[None, :]
    cosine, sine = jnp.cos(turned), jnp.sin(turned)
    ones, zeros = jnp.ones_like(cosine), jnp.zeros_like(cosine)
    cos_q, sin_q = cosine * SCORE_SCALE, sine * SCORE_SCALE
    cos_w = jnp.concatenate([cos_q] * 4 + [cosine] * 2 + [ones] * 2, axis=1)
    sin_w = jnp.concatenate([-sin_q, sin_q] * 2 + [-sine, sine] + [zeros] * 2, axis=1)

    gain_a = attn_gain[None, :]
    gain_m = moe_gain[None, :]
    (
        xd,
        attn,
        qkv,
        mixed,
        middle,
        moe,
        slot_cols,
        slot_rows,
        chosen,
        w_att,
        moe_own,
        slot_given,
        given_rows,
        mid16,
        router_x,
    ) = front(
        block_in[0],
        w_half,
        src_col,
        own_starts,
        cos_w,
        sin_w,
        gain_a,
        gain_m,
        expert_ids[0],
        places[0],
        src_row,
        rows,
        pairs,
    )

    router_x = router_x.reshape(width, LANES)
    gates, packed = router(moe, router_x, chosen)

    acc = carried = None
    summed = []
    final = len(gathered) - 1
    spare = [cotangent[0], mid16]
    full = []
    for i, w in enumerate(gathered):
        own = spare[i] if i < 2 else None
        if i > 0:
            w, *carried = lax.optimization_barrier((w, *carried))
        parts = experts_forward(
            moe, slot_rows, slot_given, packed, w, acc, own, bases[i], i == final, capacity, 3 + i
        )
        kept, acc = parts[:4], parts[4]
        full += parts[5:]
        rows_in = given_rows
        if i == final:
            rows_in = lax.optimization_barrier((given_rows, summed[0]))[0]
        grads, *carried = experts_reverse(
            full[0], rows_in, slot_cols, kept, w, carried, acc, bases[i], i == final, capacity, 7
        )
        summed.append(lax.psum_scatter(grads, "col", scatter_dimension=0, tiled=False))
    es = acc
    dm, dgates, e_mix, e_across, e_half = carried
    block_out, input_grad, att_grad, small = backward(
        dm,
        es,
        e_mix,
        e_half,
        dgates,
        full[1],
        full[0],
        gates[:tokens],
        middle,
        moe_own,
        src_col[:tokens],
        mixed,
        qkv,
        attn,
        xd,
        w_att,
        router_x,
        own_starts,
        cos_w,
        sin_w,
        gain_a,
        gain_m,
        src_row,
    )
    router_all = small[:EXPERT_COUNT].T
    router_grad = lax.dynamic_slice_in_dim(router_all, c * shard, shard, 0)
    def collect(i):
        parts = [g[:, :, i * fe : (i + 1) * fe] for g in summed]
        return jnp.concatenate(parts, axis=0).astype(F32).transpose(1, 0, 2)

    return (
        block_out[None],
        input_grad[None],
        small[EXPERT_COUNT],
        att_grad[:, :qw],
        att_grad[:, qw:],
        small[EXPERT_COUNT + 1],
        router_grad,
        collect(0),
        collect(1),
        collect(2),
    )


def solution(mesh):
    tokens = P("col", "row", None)
    weight = P("col", "row")
    expert = P("col", "row", None)
    return jax.shard_map(
        body,
        mesh=mesh,
        in_specs=(
            tokens,
            tokens,
            P("col", None),
            P("col", None),
            P("col", None, None),
            P("col", None, None),
            P(),
            weight,
            weight,
            P(),
            P("col", None),
            expert,
            expert,
            expert,
        ),
        out_specs=(
            tokens,
            tokens,
            P(),
            weight,
            weight,
            P(),
            P("col", None),
            expert,
            expert,
            expert,
        ),
        check_vma=False,
    )
```

time: 680 us -> 633 us (0.931)
  Pallas kernels: 559 us -> 522 us
  waiting for transfers between devices: 45.8 us -> 32.5 us
    pallas_call x1, Pallas kernels: 173 us -> 139 us  [front(): pl.pallas_call(front_kernel, out_shape=(shape((tokens, width), BF), shape...]
    ppermute x7 -> x3, waiting for transfers between devices: 43.1 us -> 31.7 us  [swap_over(): return lax.ppermute(value, axis, [(i, i ^ step) for i in range(size)])]
    pallas_call x1, Pallas kernels: 171 us -> 163 us  [backward(): pl.pallas_call(functools.partial(back_kernel, nblk), out_shape=(shape((to...]
    pallas_call x4 -> x6, Pallas kernels: 212 us -> 217 us  [the longest x3 113 us: experts_reverse(): pl.pallas_call(functools.partial(reverse_kernel, base, first, last, local...]
    unnamed x46 -> x44, local copies, waits for them, and re-layouts: 17.4 us -> 21.8 us
  transfers between devices with their start and end apart: 15 -> 9, of which waited for: 3 -> 2; matrix products, arithmetic and copies ran while one was open for 3% -> 4% of each run, Pallas kernels for 83% -> 84%
where the time goes in v3:
time: 633 us; the launch traced here: 621 us
  Pallas kernels  522 us (82%)
  local copies, waits for them, and re-layouts  40.1 us (6%)
  waiting for transfers between devices  32.5 us (5%)
  between operations  14.9 us (2%)
  other arithmetic  8.55 us (1%)
    pallas_call x1, Pallas kernels, backward(): pl.pallas_call(functools.partial(back_kernel, nblk), out_shape=(shape((to...  163 us
    pallas_call x1, Pallas kernels, front(): pl.pallas_call(front_kernel, out_shape=(shape((tokens, width), BF), shape...  139 us
    pallas_call x3, Pallas kernels, experts_reverse(): pl.pallas_call(functools.partial(reverse_kernel, base, first, last, local...  113 us
    pallas_call x3, Pallas kernels, experts_forward(): pl.pallas_call(functools.partial(forward_kernel, base, first, last, gathe...  105 us
    ppermute x3, waiting for transfers between devices, swap_over(): return lax.ppermute(value, axis, [(i, i ^ step) for i in range(size)])  31.7 us
    unnamed x44, local copies, waits for them, and re-layouts  21.8 us
  transfers between devices with their start and end apart: 9, of which 2 were waited for; matrix products, arithmetic and copies ran while one was open for 4% of the time, Pallas kernels for 84%

profile of v3, /device:TPU:9, one launch (start us, length us, event | category | flops | bytes accessed | tf_op | source)
XLA Modules:
  0.0 620.6 jit_solution(9580722781440375270)
XLA Ops:
  7.2 1.6 copy.93
  8.9 1.5 copy.94
  11.0 1.6 fusion.8
  15.5 2.3 collective-permute-start.1
  20.8 1.3 copy.90
  22.2 1.3 copy.91
  23.5 1.8 multiply_sine_fusion
  25.3 1.3 concatenate.33.cos.refs_18_
  26.7 2.2 concatenate.35.sin.refs_19_
  30.7 11.6 %collective-permute-done.1 = bf16[128,896]{1,0:T(8,128)(2,1)} collective-permute-done((bf16[128,896]{1,0:T(8,128)(2,1)}, bf16[128,896]{1,0:T(8,128)(2,1)}, u32[]{:S(2)}, u32[]{:S(2)}) %collective-permute-start.1) | collective-permute-done | bytes 229408 | tf_op jit(solution)/shard_map/ppermute | solution.py:1239
  42.3 20.1 %collective-permute-done.2 = bf16[128,896]{1,0:T(8,128)(2,1)} collective-permute-done((bf16[128,896]{1,0:T(8,128)(2,1)}, bf16[128,896]{1,0:T(8,128)(2,1)}, u32[]{:S(2)}, u32[]{:S(2)}) %collective-permute-start.2) | collective-permute-done | bytes 229408 | tf_op jit(solution)/shard_map/ppermute | solution.py:1239
  62.4 2.3 pad_maximum_fusion.w_half
  64.7 138.9 %attention_forward.1 = (bf16[512,1024]{1,0:T(8,128)(2,1)}, bf16[512,1024]{1,0:T(8,128)(2,1)}, bf16[512,2048]{1,0:T(8,128)(2,1)}, bf16[512,1024]{1,0:T(8,128)(2,1...) custom-call(bf16[512,1024]{1,0:T(8,128)(2,1)} %bitcast.65, ...), custom_call_target="tpu_custom_call" | custom-call | flops 20000000000 | bytes 62914560 | tf_op jit(solution)/shard_map/attention_forward/pallas_call | solution.py:340
  203.6 2.2 copy-done
  205.7 1.2 copy-done.1
  207.9 2.6 router.1
  211.3 42.0 %experts_forward.3 = (bf16[3,512,1024]{2,1,0:T(8,128)(2,1)}, f32[3,512,512]{2,1,0:T(8,128)}, f32[3,512,512]{2,1,0:T(8,128)}, f32[3,512,128]{2,1,0:T(8,128)}, f32...) custom-call(bf16[4,512,1024]{2,1,0:T(8,128)(2,1)} %get-tuple-element.66.moe.refs_0_, ...), custom_call_target="tpu_custom_call" | custom-call | flops 20999999488 | bytes 31457280 | tf_op jit(solution)/shard_map/experts_forward/pallas_call | solution.py:636
  253.3 39.5 %experts_reverse.3 = (bf16[8,3,128,1536]{3,2,1,0:T(8,128)(2,1)}, f32[2048,1024]{1,0:T(8,128)}, f32[2048,128]{1,0:T(8,128)}) custom-call(bf16[4,512,1024]{2,1,0:T(8,128)(2,1)} %get-tuple-element.72.refs_0_.refs_6_, f32[8,2048]{1,0:T(8,128)} %get-tuple-element.80.refs_1_, f32[2048,128]{1,0:T(8,128)} %get-tuple-element.74.refs_2_, ...), custom_call_target="tpu_custom_call" | custom-call | flops 27000000512 | bytes 41943040 | tf_op jit(solution)/shard_map/experts_reverse/pallas_call | solution.py:876
  292.9 40.2 %experts_forward.4 = (bf16[3,512,1024]{2,1,0:T(8,128)(2,1)}, f32[3,512,512]{2,1,0:T(8,128)}, f32[3,512,512]{2,1,0:T(8,128)}, f32[3,512,128]{2,1,0:T(8,128)}, f32...) custom-call(bf16[4,512,1024]{2,1,0:T(8,128)(2,1)} %get-tuple-element.66.moe.refs_0_, ...), custom_call_target="tpu_custom_call", output_to_operand_aliasing={{4}: (5, {})} | custom-call | flops 20999999488 | bytes 31457280 | tf_op jit(solution)/shard_map/experts_forward/pallas_call | solution.py:636
  333.1 39.6 %experts_reverse.4 = (bf16[8,3,128,1536]{3,2,1,0:T(8,128)(2,1)}, f32[2048,1024]{1,0:T(8,128)}, f32[2048,128]{1,0:T(8,128)}) custom-call(bf16[4,512,1024]{2,1,0:T(8,128)(2,1)} %get-tuple-element.72.refs_0_.refs_6_, f32[8,2048]{1,0:T(8,128)} %get-tuple-element.80.refs_1_, ...), custom_call_target="tpu_custom_call", output_to_operand_aliasing={{1}: (8, {}), {2}: (9, {})} | custom-call | flops 27000000512 | bytes 41943040 | tf_op jit(solution)/shard_map/experts_reverse/pallas_call | solution.py:876
  372.8 22.7 %experts_forward.5 = (bf16[2,512,1024]{2,1,0:T(8,128)(2,1)}, f32[2,512,512]{2,1,0:T(8,128)}, f32[2,512,512]{2,1,0:T(8,128)}, f32[2,512,128]{2,1,0:T(8,128)}, bf16[4,512,1024]{2,1,0:T(8,128)(2,1)}) custom-call(bf16[4,512,1024]{2,1,0:T(8,128)(2,1)} %get-tuple-element.66.moe.refs_0_, f32[8,2048]{1,0:T(8,128)} %get-tuple-element.67.refs_1_, ...), custom_call_target="tpu_custom_call" | custom-call | flops 14000000000 | bytes 31457280 | tf_op jit(solution)/shard_map/experts_forward/pallas_call | solution.py:636
  395.5 33.6 %experts_reverse.5 = (bf16[8,2,128,1536]{3,2,1,0:T(8,128)(2,1)}, bf16[4,512,1024]{2,1,0:T(8,128)(2,1)}, f32[8,2048]{1,0:T(8,128)}, bf16[2,256,1024]{2,1,0:T(8,12...) custom-call(bf16[4,512,1024]{2,1,0:T(8,128)(2,1)} %get-tuple-element.72.refs_0_.refs_6_, ...), custom_call_target="tpu_custom_call" | custom-call | flops 17999998976 | bytes 41943040 | tf_op jit(solution)/shard_map/experts_reverse/pallas_call | solution.py:876
  431.4 162.6 %attention_backward.1 = (bf16[512,1024]{1,0:T(8,128)(2,1)}, f32[512,1024]{1,0:T(8,128)}, f32[128,768]{1,0:T(8,128)}, f32[40,1024]{1,0:T(8,128)}, bf16[2,256,1024]{2,1,0:T(8,128)(2,1)}) custom-call(bf16[4,512,1024]{2,1,0:T(8,128)(2,1)} %get-tuple-element.103.refs_0_, bf16[4,512,1024]{2,1,0:T(8,128)(2,1)} %get-tuple-element.102.refs_10_.refs_1_, ...), custom_call_target="tpu_custom_call" | custom-call | flops 60000002048 | bytes 104857600 | tf_op jit(solution)/shard_map/attention_backward/pallas_call | solution.py:1192
  594.0 1.6 slice.76
  595.6 1.7 slice.75
  598.8 1.4 fusion.12
  600.4 1.4 fusion.10
  601.8 1.2 fusion.11
  603.1 2.5 copy.100
  605.8 2.5 copy.99
  608.5 2.5 copy.98
  612.0 1.3 copy.107
  (84 shorter events, 15.5 us)
Async XLA Ops:
  7.2 3.2 copy-start.6
  7.2 204.2 %all-gather.7.cloned.1.call-start = ((), (), s32[]{:S(2)}) async-start(), calls=%async_computation.6 | async-start | bytes 10616832 | tf_op jit(solution)/shard_map/all_gather | solution.py:1289
  12.6 1.9 copy-start.14
  12.6 2.1 copy-start.9
  12.6 2.1 copy-start.12
  12.6 5.6 copy-start.15
  12.6 5.6 copy-start.16
  12.6 280.3 %all-gather.11.cloned.1.call-start = ((), (), s32[]{:S(2)}) async-start(), calls=%async_computation.8 | async-start | bytes 10616832 | tf_op jit(solution)/shard_map/all_gather | solution.py:1289
  12.7 8.1 %copy-start.10 = (s32[1,2048,8]{1,2,0:T(8,128)S(1)}, s32[1,2048,8]{1,2,0:T(8,128)}, u32[]{:S(2)}) copy-start(s32[1,2048,8]{1,2,0:T(8,128)} %param.18) | copy-start | bytes 196612
  13.4 8.8 %copy-start.11 = (s32[1,2048,8]{1,2,0:T(8,128)S(1)}, s32[1,2048,8]{1,2,0:T(8,128)}, u32[]{:S(2)}) copy-start(s32[1,2048,8]{1,2,0:T(8,128)} %param.19) | copy-start | bytes 196612
  13.4 359.4 %all-gather.9.cloned.1.call-start = ((), (), s32[]{:S(2)}) async-start(), calls=%async_computation.7 | async-start | bytes 7077888 | tf_op jit(solution)/shard_map/all_gather | solution.py:1289
  14.4 381.1 %reduce-scatter.4.cloned.1.call-start = ((), (), s32[]{:S(2)}) async-start(), calls=%async_computation.3 | async-start | bytes 10616832 | tf_op jit(solution)/shard_map/reduce_scatter | solution.py:1380
  15.5 26.7 %collective-permute-start.1 = (bf16[128,896]{1,0:T(8,128)(2,1)}, bf16[128,896]{1,0:T(8,128)(2,1)}, u32[]{:S(2)}, u32[]{:S(2)}) collective-permute-start(bf16[128,896]{1,0:T(8,128)(2,1)} %get-tuple-element.188), channel_id=1, source_target_pairs={{0,4},{1,5},{2,6},{3,7},{4,0},{5,1},{6,2},{7,3},{8,12},{9,13},{10,... | collective-permute-start | bytes 688136 | tf_op jit(solution)/shard_map/ppermute | solution.py:1239
  17.8 24.4 %collective-permute-start = (bf16[128,896]{1,0:T(8,128)(2,1)}, bf16[128,896]{1,0:T(8,128)(2,1)}, u32[]{:S(2)}, u32[]{:S(2)}) collective-permute-start(bf16[128,896]{1,0:T(8,128)(2,1)} %get-tuple-element.188), channel_id=1, source_target_pairs={{0,2},{1,3},{2,0},{3,1},{4,6},{5,7},{6,4},{7,5},{8,10},{9,11},{10,... | collective-permute-start | bytes 688136 | tf_op jit(solution)/shard_map/ppermute | solution.py:1239
  18.0 44.4 %collective-permute-start.2 = (bf16[128,896]{1,0:T(8,128)(2,1)}, bf16[128,896]{1,0:T(8,128)(2,1)}, u32[]{:S(2)}, u32[]{:S(2)}) collective-permute-start(bf16[128,896]{1,0:T(8,128)(2,1)} %get-tuple-element.188), channel_id=1, source_target_pairs={{0,6},{1,7},{2,4},{3,5},{4,2},{5,3},{6,0},{7,1},{8,14},{9,15},{10,... | collective-permute-start | bytes 688136 | tf_op jit(solution)/shard_map/ppermute | solution.py:1239
  26.7 35.7 %copy-start.8 = (bf16[1,128,896]{2,1,0:T(8,128)(2,1)S(1)}, bf16[1,128,896]{2,1,0:T(8,128)(2,1)}, u32[]{:S(2)}) copy-start(bf16[1,128,896]{2,1,0:T(8,128)(2,1)} %get-tuple-element.187) | copy-start | bytes 688132
  203.5 2.2 copy-start
  205.7 1.2 copy-start.1
  207.0 0.9 copy-start.2
  210.5 0.8 copy-start.3
  292.8 307.6 %reduce-scatter.6.cloned.1.call-start = ((), (), s32[]{:S(2)}) async-start(), calls=%async_computation.4 | async-start | bytes 10616832 | tf_op jit(solution)/shard_map/reduce_scatter | solution.py:1380
  372.8 229.0 %reduce-scatter.8.cloned.1.call-start = ((), (), s32[]{:S(2)}) async-start(), calls=%async_computation.5 | async-start | bytes 7077888 | tf_op jit(solution)/shard_map/reduce_scatter | solution.py:1380
  429.1 0.7 copy-start.13
  431.4 168.9 %copy-start.5 = (bf16[1,3,128,1536]{3,2,1,0:T(8,128)(2,1)S(1)}, bf16[1,3,128,1536]{3,2,1,0:T(8,128)(2,1)}, u32[]{:S(2)}) copy-start(bf16[1,3,128,1536]{3,2,1,0:T(8,128)(2,1)} %reduce-scatter.4.cloned.1.call-done) | copy-start | bytes 3538948
  608.4 2.7 copy-start.7
  608.5 3.5 copy-start.4
Sparse Core Ops, SparseCore 0:
  12.8 101.4 all-gather.6
  116.5 91.6 all-gather.10
  209.8 63.7 all-gather.8
  292.9 100.1 reduce-scatter.3
  395.3 97.9 reduce-scatter.5
  495.5 93.7 reduce-scatter.7

commit v4 on v3

--- a/solution.py
+++ b/solution.py
@@ -124,42 +124,17 @@
             copy.wait_send()
 
 
-def front_kernel(
-    xin,
-    w_half,
-    src,
-    starts,
-    cos,
-    sin,
-    gain_a,
-    gain_m,
-    ids,
-    spots,
-    src_row,
-    xd,
-    attn,
-    qkv,
-    mixed,
-    middle,
-    moe_all,
-    slot_cols,
-    slot_rows,
-    chosen,
-    w_att,
-    moe,
-    slot_given,
-    given_rows,
-    mid16,
-    w_router,
-    xb,
-    bias,
-    sems,
-    local_sems,
-):
+def front_kernel(pairs, *refs):
+    xin, cot, w_last = refs[:3]
+    w_parts = refs[3 : 3 + pairs]
+    refs = refs[3 + pairs :]
+    src, starts, cos, sin, gain_a, gain_m, ids, spots, src_row = refs[:9]
+    xd, attn, qkv, mixed, middle, moe_all, cot_first, slot_cols, slot_rows, gates, packed = refs[9:20]
+    w_att, moe, slot_given, given_rows, mid16, w_router, w_next = refs[20:27]
+    xb, bias, chosen, sems, local_sems = refs[27:]
     nblk, tokens, width = xb.shape
     half = tokens // 2
     capacity = nblk * tokens * TOPK // EXPERT_COUNT
-    pairs = w_att.shape[1]
     qw = w_att.shape[4] * 2 // 3
     rank = w_att.shape[1] * 2 * w_att.shape[3]
     r = lax.axis_index("row")
@@ -186,6 +161,10 @@
     ms = RowGather(cut(moe), cut_slot(moe_all), sems, 2 * n, r, c)
     base = 3 * n
     share = [link(w_att.at[j, :, k], w_att.at[j, :, k], sems, base + j, sibling) for j in range(nblk)]
+    early = [
+        link(cot.at[pl.ds(0, half)], cot_first.at[i], sems, base + nblk + 1 + i, (r ^ (1 + i), c))
+        for i in range(2)
+    ]
     share.append(link(w_router.at[:, k], w_router.at[:, k], sems, base + nblk, sibling))
     xs.start(1)
     xs.start(0)
@@ -193,16 +172,18 @@
     for i in range(pairs):
         keep.append(
             pltpu.make_async_copy(
-                w_half.at[i, :, pl.ds(0, both)], w_att.at[0, z ^ i, k], local_sems.at[2 + 2 * i]
+                w_parts[i].at[:, pl.ds(0, both)], w_att.at[0, z ^ i, k], local_sems.at[2 + 2 * i]
             )
         )
         keep.append(
             pltpu.make_async_copy(
-                w_half.at[i, :, pl.ds(both, LANES)], w_router.at[z ^ i, k], local_sems.at[3 + 2 * i]
+                w_parts[i].at[:, pl.ds(both, LANES)], w_router.at[z ^ i, k], local_sems.at[3 + 2 * i]
             )
         )
     for copy in keep:
         copy.start()
+    seat = pltpu.make_async_copy(w_last, w_next.at[c], local_sems.at[2 + 2 * pairs])
+    seat.start()
     for copy in keep:
         copy.wait()
     ws.start(1)
@@ -242,6 +223,8 @@
 
     ws.wait((3, 0), (3, 1))
     share[3].start()
+    for copy in early:
+        copy.start()
     for copy in share:
         copy.wait_recv()
 
@@ -288,20 +271,21 @@
     @pl.loop(0, nblk)
     def _(b):
         at = pl.ds(pl.multiple_of(b * tokens, tokens), tokens)
-        lane = iota((tokens, LANES), 1)
-        spot = jnp.zeros((tokens, LANES), F32)
-        named = jnp.zeros((tokens, LANES), F32)
         there = pl.ds(pl.multiple_of((b ^ r) * tokens, tokens), tokens)
-        own_ids = ids[there, :] ^ (r * local)
-        own_spots = spots[there, :]
+        expert = iota((EXPERT_COUNT, tokens), 0)
+        spot = jnp.zeros((EXPERT_COUNT, tokens), F32)
+        named = jnp.zeros((EXPERT_COUNT, tokens), F32)
+        own_ids = ids[:, there] ^ (r * local)
+        own_spots = spots[:, there].astype(F32)
         for i in range(TOPK):
-            hit = lane == own_ids[:, i : i + 1]
+            hit = expert == own_ids[i : i + 1, :]
             named = jnp.where(hit, 1.0, named)
-            spot = jnp.where(hit, own_spots[:, i : i + 1].astype(F32), spot)
-        chosen[at, :] = named
+            spot = jnp.where(hit, own_spots[i : i + 1, :], spot)
         slot = jnp.where((named > 0.0) & (spot < capacity), spot, -1.0)
-        slot_cols[at, :] = slot
-        slot_rows[:, at] = slot.T[: slot_rows.shape[0], :]
+        slot_rows[:, at] = slot[:local, :]
+        rest = jnp.zeros((LANES - EXPERT_COUNT, tokens), F32)
+        chosen[at, :] = jnp.concatenate([named, rest], axis=0).T
+        slot_cols[at, :] = jnp.concatenate([slot, rest - 1.0], axis=0).T
 
     ms.forward(1)
 
@@ -320,25 +304,50 @@
         slot_given[at, :] = found - 1.0
         given_rows[:, at] = (found - 1.0).T[: given_rows.shape[0], :]
 
-    ms.wait((1, 0), (2, 1), (3, 0), (3, 1))
+    def gate_block(j, rows):
+        at = slice(j * tokens, (j + 1) * tokens)
+        logits = mm(rows, w_router[...].reshape(width, LANES))
+        named = chosen[at, :] > 0.0
+        logits = jnp.where(named, logits, MASKED)
+        top = jnp.max(logits, axis=-1, keepdims=True)
+        raised = jnp.where(named, jnp.exp(logits - top), 0.0)
+        gate = raised / jnp.sum(raised, axis=-1, keepdims=True)
+        if j == 0:
+            gates[...] = gate
+        own = jnp.where(iota((tokens, LANES), 1) < local, gate, 0.0)
+        high, mid, low = split_three(own)
+        packed[at, :] = (high + pltpu.roll(mid, local, 1) + pltpu.roll(low, 2 * local, 1)).astype(BF)
+
+    gate_block(0, moe[...])
     place.wait()
-    for gather in (xs, ws, ms):
+    xs.drain()
+    for j, keys in ((1, ((1, 0),)), (2, ((2, 1),)), (3, ((3, 0), (3, 1)))):
+        ms.wait(*keys)
+        get = pltpu.make_async_copy(moe_all.at[j], xb.at[j], local_sems.at[0])
+        get.start()
+        get.wait()
+        gate_block(j, xb[j])
+    seat.wait()
+    for copy in early:
+        copy.wait_recv()
+    for gather in (ws, ms):
         gather.drain()
-    for copy in share:
+    for copy in share + early:
         copy.wait_send()
 
 
-def front(xin, w_half, src, starts, cos, sin, gain_a, gain_m, ids, spots, src_row, nblk, pairs):
+def front(xin, cot, w_last, w_parts, tables, nblk):
     tokens, width = xin.shape
-    shard, both = w_half.shape[1], w_half.shape[2] - LANES
+    pairs = len(w_parts)
+    shard, both = w_parts[0].shape[0], w_parts[0].shape[1] - LANES
     total = nblk * tokens
     qkv_width = nblk * both * 2 // 3
     head_width = nblk * both // 3
     shape = jax.ShapeDtypeStruct
-    count = 3 * RowGather.count + nblk + 1
+    count = 3 * RowGather.count + nblk + 3
     local = EXPERT_COUNT // nblk
     return pl.pallas_call(
-        front_kernel,
+        functools.partial(front_kernel, pairs),
         out_shape=(
             shape((tokens, width), BF),
             shape((tokens, width), BF),
@@ -346,66 +355,34 @@
             shape((tokens, head_width), BF),
             shape((tokens, width), F32),
             shape((nblk, tokens, width), BF),
+            shape((2, tokens // 2, width), BF),
             shape((total, LANES), F32),
             shape((local, total), F32),
-            shape((total, LANES), F32),
+            shape((tokens, LANES), F32),
+            shape((total, LANES), BF),
             shape((nblk, pairs, 2, shard, both), BF),
             shape((tokens, width), BF),
             shape((total, LANES), F32),
             shape((local, total), F32),
             shape((tokens, width), BF),
             shape((pairs, 2, shard, LANES), BF),
+            shape((2 * pairs, *w_last.shape), BF),
         ),
-        in_specs=[ANY] * 2 + [FULL] * 9,
-        out_specs=[FULL] * 5 + [ANY] + [FULL] * 9,
+        in_specs=[ANY] * (3 + pairs) + [FULL] * 9,
+        out_specs=[FULL] * 5 + [ANY] * 2 + [FULL] * 10 + [ANY],
         scratch_shapes=[
             pltpu.VMEM((nblk, tokens, width), BF),
             pltpu.VMEM((tokens // 2, tokens), F32),
+            pltpu.VMEM((total, LANES), F32),
             pltpu.SemaphoreType.DMA((2, count)),
-            pltpu.SemaphoreType.DMA((2 + 2 * pairs,)),
+            pltpu.SemaphoreType.DMA((3 + 2 * pairs,)),
         ],
         compiler_params=pltpu.CompilerParams(
             vmem_limit_bytes=58 * MIB, collective_id=1, has_side_effects=True
         ),
         cost_estimate=cost(20e9, 60 * MIB),
         name="attention_forward",
-    )(xin, w_half, src, starts, cos, sin, gain_a, gain_m, ids, spots, src_row)
-
-
-def router_kernel(moe, w_router, chosen, gates, packed):
-    nblk, tokens, _ = moe.shape
-    local = EXPERT_COUNT // nblk
-    for j in range(nblk):
-        at = slice(j * tokens, (j + 1) * tokens)
-        logits = mm(moe[j], w_router[...])
-        named = chosen[at, :] > 0.0
-        logits = jnp.where(named, logits, MASKED)
-        top = jnp.max(logits, axis=-1, keepdims=True)
-        raised = jnp.where(named, jnp.exp(logits - top), 0.0)
-        gate = raised / jnp.sum(raised, axis=-1, keepdims=True)
-        gates[at, :] = gate
-        lane = iota((tokens, LANES), 1)
-        own = jnp.where(lane < local, gate, 0.0)
-        high = own.astype(BF).astype(F32)
-        rest = own - high
-        mid = rest.astype(BF).astype(F32)
-        low = rest - mid
-        packed[at, :] = (high + pltpu.roll(mid, local, 1) + pltpu.roll(low, 2 * local, 1)).astype(BF)
-
-
-def router(moe, w_router, chosen):
-    nblk, tokens, _ = moe.shape
-    total = nblk * tokens
-    shape = jax.ShapeDtypeStruct
-    return pl.pallas_call(
-        router_kernel,
-        out_shape=(shape((total, LANES), F32), shape((total, LANES), BF)),
-        in_specs=[FULL] * 3,
-        out_specs=[FULL] * 2,
-        compiler_params=params(24),
-        cost_estimate=cost(1e9, 7 * MIB),
-        name="router",
-    )(moe, w_router, chosen)
+    )(xin, cot, w_last, *w_parts, *tables)
 
 
 class RowScatter:
@@ -468,17 +445,24 @@
     return high, mid, rest - mid
 
 
-def forward_kernel(base, first, last, gathers, local, capacity, *refs):
+def forward_kernel(base, first, last, gathers, stage, local, capacity, *refs):
     moe_hbm, slot_rows, slot_given, packed, w = refs[:5]
     refs = refs[5:]
     if not first:
         acc_in, refs = refs[0], refs[1:]
+    early = gathers == "rest"
     if gathers:
         own_hbm, refs = refs[0], refs[1:]
+    if early:
+        first_hbm, refs = refs[0], refs[1:]
+    if stage:
+        next_in, refs = refs[0], refs[1:]
     routed_out, gate_out, up_out, weight_out, acc_out = refs[:5]
     refs = refs[5:]
     if gathers:
         all_hbm, refs = refs[0], refs[1:]
+    if stage:
+        next_out, refs = refs[0], refs[1:]
     moe, acc, sel, given, y1, sems = refs[:6]
     step = pl.program_id(0)
     steps = pl.num_programs(0)
@@ -497,15 +481,30 @@
         r = lax.axis_index("row")
         c = lax.axis_index("col")
         half = tokens // 2
-        gather = RowGather(
-            lambda h: own_hbm.at[pl.ds(h * half, half)],
-            lambda j, h: all_hbm.at[j, pl.ds(h * half, half)],
-            link_sems,
-            0,
-            r,
-            c,
-        )
-        keep = pltpu.make_async_copy(own_hbm, all_hbm.at[0], sems.at[nblk + 1])
+        near, far = (r ^ 1, c), (r ^ 2, c)
+        top, bottom = pl.ds(0, half), pl.ds(half, half)
+        later = []
+        greeted = [near, far]
+        if stage:
+            line = LineGather(stage, next_in, next_out, refs[7], r, c)
+            greeted = greeted + line.devices
+        if gathers == "rest":
+            begin = [
+                link(own_hbm.at[bottom], all_hbm.at[0], link_sems, 0, near),
+                link(first_hbm.at[1], all_hbm.at[2], link_sems, 1, near),
+                link(own_hbm.at[bottom], all_hbm.at[1], link_sems, 2, far),
+            ]
+            later = [link(all_hbm.at[0], all_hbm.at[3], link_sems, 3, far)]
+        elif gathers == "sides":
+            begin = [
+                link(own_hbm, all_hbm.at[0], link_sems, 0, near),
+                link(own_hbm, all_hbm.at[1], link_sems, 1, far),
+            ]
+        else:
+            begin = [
+                link(own_hbm.at[1, top], all_hbm.at[top], link_sems, 0, near),
+                link(own_hbm.at[0, bottom], all_hbm.at[bottom], link_sems, 1, far),
+            ]
 
     @pl.when(step == 0)
     def _():
@@ -514,10 +513,11 @@
         if not first:
             load.start()
         if gathers:
-            keep.start()
-            greet([(r ^ 1, c), (r ^ 2, c)])
-            gather.start(0)
-            gather.start(1)
+            greet(greeted)
+            for copy in begin:
+                copy.start()
+            if stage:
+                line.start()
 
     row = slot_rows[pl.ds(e, 1), :]
     for j in range(nblk):
@@ -529,12 +529,12 @@
         for copy in copies:
             copy.wait()
 
-    if gathers:
+    if early:
 
         @pl.when(step == steps - 1)
         def _():
-            gather.forward(0)
-            gather.forward(1)
+            begin[0].wait_recv()
+            later[0].start()
 
     routed_out[0] = mm(sel[...], moe[...]).astype(BF)
     lane = iota((capacity, LANES), 1)
@@ -579,22 +579,28 @@
                 acc[at, :] = part
             put(b).start()
 
+        if stage:
+            line.finish()
         if gathers:
-            gather.wait((1, 0), (2, 1), (3, 0), (3, 1))
-            keep.wait()
-            gather.drain()
+            for copy in begin[1:] if early else begin:
+                copy.wait_recv()
+            for copy in later:
+                copy.wait_recv()
+            for copy in begin + later:
+                copy.wait_send()
         for b in range(nblk):
             put(b).wait()
 
 
-def experts_forward(moe, slot_rows, slot_given, packed, w, acc, own, base, last, capacity, key):
+def experts_forward(moe, slot_rows, slot_given, packed, w, acc, moved, later, base, last, capacity, key):
     nblk, tokens, width = moe.shape
     total = nblk * tokens
     cols, ne, shard, fe3 = w.shape
     fe = fe3 // 3
     local = EXPERT_COUNT // nblk
     first = acc is None
-    gathers = own is not None
+    gathers, *sent = moved
+    landing = {"rest": (4, tokens // 2), "sides": (2, tokens), "corner": (tokens,)}[gathers]
     shape = jax.ShapeDtypeStruct
     wspec = pl.BlockSpec((cols, 1, shard, fe3), lambda s: (0, s, 0, 0))
 
@@ -623,18 +629,25 @@
         pltpu.VMEM((capacity, total), BF),
         pltpu.VMEM((tokens, ne * capacity), BF),
         pltpu.VMEM((ne * capacity, width), BF),
-        pltpu.SemaphoreType.DMA((nblk + 2,)),
+        pltpu.SemaphoreType.DMA((nblk + 1,)),
     ]
     options = dict(vmem_limit_bytes=58 * MIB)
-    if gathers:
-        ins.append(own)
+    ins += sent
+    in_specs += [ANY] * len(sent)
+    outs.append(shape((*landing, width), BF))
+    out_specs.append(ANY)
+    scratch.append(pltpu.SemaphoreType.DMA((2, 4)))
+    stage, following = later
+    if stage:
+        aliases = {**aliases, len(ins): len(outs)}
+        ins.append(following)
         in_specs.append(ANY)
-        outs.append(shape((nblk, tokens, width), BF))
+        outs.append(shape(following.shape, BF))
         out_specs.append(ANY)
-        scratch.append(pltpu.SemaphoreType.DMA((2, RowGather.count)))
-        options.update(collective_id=key, has_side_effects=True)
+        scratch.append(LineGather.scratch(cols // 2))
+    options.update(collective_id=key, has_side_effects=True)
     return pl.pallas_call(
-        functools.partial(forward_kernel, base, first, last, gathers, local, capacity),
+        functools.partial(forward_kernel, base, first, last, gathers, stage, local, capacity),
         grid=(ne,),
         out_shape=outs,
         in_specs=in_specs,
@@ -647,41 +660,133 @@
     )(*ins)
 
 
-def reverse_kernel(base, first, last, local, capacity, *refs):
-    cot_hbm, given_rows, slot_cols, routed, gate_in_ref, up_in_ref, weight_ref, w = refs[:8]
-    refs = refs[8:]
+class LineGather:
+    def __init__(self, stage, src, dst, sems, r, c):
+        self.pairs = src.shape[0] // 2
+        self.stage, self.src, self.dst, self.sems = stage, src, dst, sems
+        self.z, self.k = c // 2, c % 2
+        count = 2 * self.pairs
+        hops = list(range(1, self.pairs))
+        cut = [(len(hops) * i) // 3 for i in range(4)]
+        self.hops = hops[cut[stage - 1] : cut[stage]] if stage < 4 else []
+        self.swaps = []
+        if stage == 4:
+            self.devices = [(r, c ^ 1)]
+            for i in range(self.pairs):
+                slot = 2 * i + self.k
+                self.swaps.append(link(src.at[slot], dst.at[slot], sems, i, (r, c ^ 1)))
+        else:
+            self.devices = [(r, (c + 2) % count), (r, (c - 2) % count)]
+
+    def place(self, side):
+        return self.z if side == 0 else self.pairs - 1 - self.z
+
+    def copy(self, side, hop):
+        at = jnp.maximum(self.place(side) - hop + 1, 0)
+        slot = 2 * (at if side == 0 else self.pairs - 1 - at) + self.k
+        src = self.src if hop == self.hops[0] else self.dst
+        index = side * (self.pairs - 1) + hop - 1
+        return link(src.at[slot], self.dst.at[slot], self.sems, index, self.devices[side])
+
+    def sends(self, side, hop):
+        return (self.place(side) >= hop - 1) & (self.place(side) <= self.pairs - 2)
+
+    def hop(self, hop):
+        for side in range(2):
+
+            @pl.when(self.sends(side, hop))
+            def _():
+                self.copy(side, hop).start()
+
+    def start(self):
+        for copy in self.swaps:
+            copy.start()
+        if self.hops:
+            self.hop(self.hops[0])
+
+    def finish(self):
+        for copy in self.swaps:
+            copy.wait_recv()
+        for hop in self.hops:
+            for side in range(2):
+
+                @pl.when(self.place(side) >= hop)
+                def _():
+                    self.copy(side, hop).wait_recv()
+
+            if hop != self.hops[-1]:
+                self.hop(hop + 1)
+        for hop in self.hops:
+            for side in range(2):
+
+                @pl.when(self.sends(side, hop))
+                def _():
+                    self.copy(side, hop).wait_send()
+
+        for copy in self.swaps:
+            copy.wait_send()
+
+    @staticmethod
+    def scratch(pairs):
+        return pltpu.SemaphoreType.DMA((2, 2 * pairs))
+
+
+def cot_pieces(own, first, rest):
+    half = own.shape[0] // 2
+    return [
+        own.at[pl.ds(0, half)],
+        own.at[pl.ds(half, half)],
+        first.at[0],
+        rest.at[0],
+        first.at[1],
+        rest.at[1],
+        rest.at[2],
+        rest.at[3],
+    ]
+
+
+def reverse_kernel(base, first, last, stage, local, capacity, *refs):
+    cot_own, cot_first, cot_rest, given_rows, slot_cols, routed, gate_in_ref, up_in_ref, weight_ref, w = refs[:10]
+    refs = refs[10:]
     if not first:
         acc_in, accg_in = refs[:2]
         refs = refs[2:]
     if last:
         es, refs = refs[0], refs[1:]
+    if stage:
+        next_in, refs = refs[0], refs[1:]
     grads, acc_out, accg_out = refs[:3]
     refs = refs[3:]
     if last:
         e_mix, e_across, e_landed = refs[:3]
         refs = refs[3:]
+    if stage:
+        next_out, refs = refs[0], refs[1:]
     cot, acc, accg, sel, chosen, spread, dsl, dslot, y2, sems = refs[:10]
     step = pl.program_id(0)
     steps = pl.num_programs(0)
     e = base + step
-    nblk, tokens, width = cot_hbm.shape
+    tokens, width = cot_own.shape
+    nblk = cot.shape[0] // tokens
     half = tokens // 2
     cols, _, shard, fe = w.shape
     fe = fe // 3
     ne = y2.shape[0] // capacity
     copies = [
-        pltpu.make_async_copy(cot_hbm.at[j], cot.at[pl.ds(j * tokens, tokens)], sems.at[j])
-        for j in range(nblk)
+        pltpu.make_async_copy(piece, cot.at[pl.ds(j * half, half)], sems.at[j])
+        for j, piece in enumerate(cot_pieces(cot_own, cot_first, cot_rest))
     ]
     if not first:
         loads = [
-            pltpu.make_async_copy(acc_in, acc, sems.at[nblk]),
-            pltpu.make_async_copy(accg_in, accg, sems.at[nblk + 1]),
+            pltpu.make_async_copy(acc_in, acc, sems.at[2 * nblk]),
+            pltpu.make_async_copy(accg_in, accg, sems.at[2 * nblk + 1]),
         ]
+    r = lax.axis_index("row")
+    c = lax.axis_index("col")
+    if stage:
+        line = LineGather(stage, next_in, next_out, refs[10], r, c)
     if last:
         e_vmem, link_sems = refs[10:]
-        r = lax.axis_index("row")
-        c = lax.axis_index("col")
         scatter = RowScatter(
             lambda j, h: es.at[j, pl.ds(h * half, half)],
             None,
@@ -703,6 +808,9 @@
         if last:
             greet([(r ^ 1, c), (r ^ 2, c)])
             scatter.start()
+        if stage:
+            greet(line.devices)
+            line.start()
 
     row = given_rows[pl.ds(e, 1), :]
     for j in range(nblk):
@@ -803,13 +911,16 @@
         else:
             out_g = pltpu.make_async_copy(accg, accg_out, sems.at[nblk])
             out_g.start()
+            if stage:
+                line.finish()
             out_g.wait()
         for b in range(nblk):
             put(b).wait()
 
 
-def experts_reverse(cot, given_rows, slot_cols, kept, w, carried, es, base, last, capacity, key):
-    nblk, tokens, width = cot.shape
+def experts_reverse(cots, given_rows, slot_cols, kept, w, carried, es, later, base, last, capacity, key):
+    tokens, width = cots[0].shape
+    nblk = EXPERT_COUNT // given_rows.shape[0]
     half = tokens // 2
     total = nblk * tokens
     cols, ne, shard, fe3 = w.shape
@@ -822,8 +933,10 @@
     def each(*dims):
         return pl.BlockSpec((1, *dims), lambda s: (s, 0, 0))
 
-    ins = [cot, given_rows, slot_cols, *kept, w]
+    ins = [*cots, given_rows, slot_cols, *kept, w]
     in_specs = [
+        ANY,
+        ANY,
         ANY,
         FULL,
         FULL,
@@ -864,17 +977,26 @@
         pltpu.VMEM((capacity, width), BF),
         pltpu.VMEM((capacity, width), BF),
         pltpu.VMEM((ne * capacity, width), BF),
-        pltpu.SemaphoreType.DMA((nblk + 2,)),
+        pltpu.SemaphoreType.DMA((2 * nblk + 2,)),
     ]
-    options = dict(vmem_limit_bytes=58 * MIB)
+    options = dict(vmem_limit_bytes=61 * MIB)
     if last:
         scratch += [
             pltpu.VMEM((2, half, width), BF),
             pltpu.SemaphoreType.DMA((2, RowScatter.count)),
         ]
         options.update(collective_id=key, has_side_effects=True)
+    stage, following = later
+    if stage:
+        aliases = {**aliases, len(ins): len(outs)}
+        ins.append(following)
+        in_specs.append(ANY)
+        outs.append(shape(following.shape, BF))
+        out_specs.append(ANY)
+        scratch.append(LineGather.scratch(cols // 2))
+        options.update(collective_id=key, has_side_effects=True)
     return pl.pallas_call(
-        functools.partial(reverse_kernel, base, first, last, local, capacity),
+        functools.partial(reverse_kernel, base, first, last, stage, local, capacity),
         grid=(ne,),
         out_shape=outs,
         in_specs=in_specs,
@@ -887,14 +1009,167 @@
     )(*ins)
 
 
+class WeightScatter:
+    def __init__(self, full, mate, across, landed, own, others, sems, base, r, c):
+        nblk, self.pairs = full.shape[0], full.shape[1]
+        self.full, self.mate, self.across, self.landed = full, mate, across, landed
+        self.own, self.others = own, others
+        self.z, self.k = c // 2, c % 2
+        z, k, step = self.z, self.k, self.pairs // 2
+        self.part = lambda h: pl.ds(h * step, step)
+        self.shares = [
+            link(full.at[j, :, 1 - k], mate.at[j], sems, base + j, (r, c ^ 1)) for j in range(nblk)
+        ]
+        self.rows = RowScatter(
+            lambda j, h: full.at[j, self.part(h), k],
+            lambda h: full.at[2 - h, self.part(h), k],
+            lambda h: across.at[h],
+            lambda j, h: landed.at[j - 1, self.part(h)],
+            sems,
+            base + nblk,
+            r,
+            c,
+        )
+        self.line = [
+            link(
+                own.at[z ^ i],
+                others.at[i - 1],
+                sems,
+                base + nblk + RowScatter.count + i - 1,
+                (r, 2 * (z ^ i) + k),
+            )
+            for i in range(1, self.pairs)
+        ]
+
+    def share(self, j):
+        self.shares[j].start()
+
+    def join(self):
+        mine = pl.ds(self.k, 1)
+        for j in (3, 1, 2, 0):
+            self.shares[j].wait_recv()
+            self.full[j, :, mine] = plus(self.full[j, :, mine], self.mate[j][:, None])
+        self.rows.start()
+
+    def middle(self):
+        mine = pl.ds(self.k, 1)
+        for h in range(2):
+            self.rows.arrived(h)
+            at = self.part(h)
+            self.full[2 - h, at, mine] = plus(self.full[2 - h, at, mine], self.across[h][:, None])
+            self.rows.send(h)
+
+    def settle(self):
+        self.rows.finish()
+        self.own[...] = (
+            self.full[0, :, pl.ds(self.k, 1)].reshape(self.own.shape).astype(F32)
+            + (self.landed[0].astype(F32) + self.landed[1].astype(F32))
+        ).astype(BF)
+        for copy in self.line:
+            copy.start()
+
+    def result(self):
+        for copy in self.line:
+            copy.wait_recv()
+        shape = self.own.shape[1:]
+        return tree_sum(
+            [self.own[pl.ds(self.z, 1)].reshape(shape).astype(F32)]
+            + [self.others[i].astype(F32) for i in range(self.pairs - 1)]
+        )
+
+    def drain(self):
+        self.rows.drain()
+        for copy in self.shares + self.line:
+            copy.wait_send()
+
+    @staticmethod
+    def count(nblk, pairs):
+        return nblk + RowScatter.count + pairs - 1
+
+    @staticmethod
+    def scratch(nblk, pairs, shard, width):
+        return [
+            pltpu.VMEM((nblk, pairs, 2, shard, width), BF),
+            pltpu.VMEM((nblk, pairs, shard, width), BF),
+            pltpu.VMEM((2, pairs // 2, shard, width), BF),
+            pltpu.VMEM((2, pairs, shard, width), BF),
+            pltpu.VMEM((pairs, shard, width), BF),
+            pltpu.VMEM((pairs - 1, shard, width), BF),
+        ]
+
+
+class SmallSum:
+    def __init__(self, own, mate, chip, row_in, row, line_in, sems, base, sliced, r, c):
+        pairs = line_in.shape[0] + 1
+        self.refs = (own, mate, chip, row_in, row, line_in)
+        self.z, self.sliced = c // 2, sliced
+        z, k = c // 2, c % 2
+        self.share = link(own, mate, sems, base, (r, c ^ 1))
+        count = row_in.shape[0]
+        self.rows = [
+            link(chip, row_in.at[j], sems, base + 1 + j, (r ^ (j + 1), c)) for j in range(count)
+        ]
+        self.line = [
+            link(
+                row.at[z ^ i] if sliced else row,
+                line_in.at[i - 1],
+                sems,
+                base + count + i,
+                (r, 2 * (z ^ i) + k),
+            )
+            for i in range(1, pairs)
+        ]
+
+    def over_row(self):
+        own, mate, chip = self.refs[:3]
+        self.share.wait_recv()
+        chip[...] = own[...] + mate[...]
+        for copy in self.rows:
+            copy.start()
+
+    def over_line(self):
+        chip, row_in, row = self.refs[2:5]
+        for copy in self.rows:
+            copy.wait_recv()
+        row[...] = tree_sum([chip[...]] + [row_in[j] for j in range(row_in.shape[0])])
+        for copy in self.line:
+            copy.start()
+
+    def result(self):
+        row, line_in = self.refs[4:]
+        for copy in self.line:
+            copy.wait_recv()
+        own = row[pl.ds(self.z, 1)].reshape(row.shape[1:]) if self.sliced else row[...]
+        return tree_sum([own] + [line_in[i] for i in range(line_in.shape[0])])
+
+    def drain(self):
+        for copy in [self.share] + self.rows + self.line:
+            copy.wait_send()
+
+    @staticmethod
+    def scratch(nblk, pairs, shape, sliced):
+        whole = (pairs, *shape) if sliced else shape
+        return [
+            pltpu.VMEM(whole, F32),
+            pltpu.VMEM(whole, F32),
+            pltpu.VMEM(whole, F32),
+            pltpu.VMEM((nblk - 1, *whole), F32),
+            pltpu.VMEM(whole, F32),
+            pltpu.VMEM((pairs - 1, *shape), F32),
+        ]
+
+
 def back_kernel(nblk, *refs):
-    dm, es, e_mix, e_half, dgates, mids, cot = refs[:7]
-    refs = refs[7:]
+    dm, es, e_mix, e_half, dgates, mid_own, mid_sides, mid_corner = refs[:8]
+    cots = cot_pieces(*refs[8:11])
+    refs = refs[11:]
+    mids = [mid_own, mid_sides.at[0], mid_sides.at[1], mid_corner]
     (gates, middle, moe, src_col, mixed, qkv, attn, xd, w_att, w_router) = refs[:10]
     (starts, cos, sin, gain_a, gain_m, src_row) = refs[10:16]
-    (block_out, input_grad, att_grad, small, e_rest) = refs[16:21]
-    (own, d_across, d_landed, dg_land, igb, dmid, dmix, dproj, dkv, bias, wg, wg_sib) = refs[21:33]
-    (w_across, w_landed, w_z, rowsum, s_own, s_sib, s_sum, s_row, s_chip, s_z, sems, lsems) = refs[33:]
+    (block_out, input_grad, qkv_grad, out_grad, router_out, gains_out, e_rest) = refs[16:23]
+    (own, d_across, d_landed, dg_land, igb, dmid, dmix, dproj, dkv, bias) = refs[23:33]
+    refs = refs[33:]
+    sems, lsems = refs[24:]
     tokens, width = xd.shape
     half = tokens // 2
     local = EXPERT_COUNT // nblk
@@ -915,11 +1190,6 @@
     def part(h):
         return pl.ds(h * half, half)
 
-    zhalf = pairs // 2
-
-    def zpart(h):
-        return pl.ds(h * zhalf, zhalf)
-
     n = RowScatter.count
     dms = RowScatter(
         lambda j, h: dm.at[j, part(h)],
@@ -935,16 +1205,6 @@
         link(e_mix.at[0], e_rest.at[0], sems, n, (r ^ 2, c)),
         link(e_mix.at[1], e_rest.at[1], sems, n + 1, (r ^ 1, c)),
     ]
-    wgs = RowScatter(
-        lambda j, h: wg.at[j, zpart(h), k],
-        lambda h: wg.at[2 - h, zpart(h), k],
-        lambda h: w_across.at[h],
-        lambda j, h: w_landed.at[j - 1, zpart(h)],
-        sems,
-        2 * n,
-        r,
-        c,
-    )
     igs = RowGather(
         lambda h: igb.at[0, part(h)], lambda j, h: igb.at[j, part(h)], sems, 3 * n, r, c
     )
@@ -954,19 +1214,14 @@
         for j in range(1, nblk)
     ]
     at += nblk - 1
-    wg_share = [
-        link(wg.at[j, :, 1 - k], wg_sib.at[j], sems, at + j, sibling) for j in range(nblk)
-    ]
-    at += nblk
-    wg_z = [
-        link(rowsum.at[z ^ i], w_z.at[i - 1], sems, at + i - 1, z_peers[i - 1])
-        for i in range(1, pairs)
-    ]
-    at += pairs - 1
-    s_share = link(s_own, s_sib, sems, at, sibling)
-    s_rows = [link(s_sum, s_row.at[j], sems, at + 1 + j, row_peers[j]) for j in range(nblk - 1)]
-    at += nblk
-    s_zs = [link(s_chip, s_z.at[i], sems, at + i, z_peers[i]) for i in range(pairs - 1)]
+    wos = WeightScatter(*refs[:6], sems, at, r, c)
+    at += WeightScatter.count(nblk, pairs)
+    wqs = WeightScatter(*refs[6:12], sems, at, r, c)
+    at += WeightScatter.count(nblk, pairs)
+    wo, wq = refs[0], refs[6]
+    routers = SmallSum(*refs[12:18], sems, at, True, r, c)
+    at += nblk + pairs - 1
+    gains = SmallSum(*refs[18:24], sems, at, False, r, c)
 
     dms.start()
     for copy in dgs:
@@ -986,7 +1241,7 @@
 
     total = jnp.zeros((tokens, width), F32)
     for j in range(nblk):
-        get = pltpu.make_async_copy(mids.at[j], dmix, lsems.at[4])
+        get = pltpu.make_async_copy(mids[j], dmix, lsems.at[4])
         get.start()
         hit = match(j)
         get.wait()
@@ -994,10 +1249,15 @@
     input_grad[...] = total
     dy = jnp.zeros((tokens, width), F32)
     for j in range(nblk):
-        get = pltpu.make_async_copy(cot.at[j], dmix, lsems.at[4])
-        get.start()
+        gets = [
+            pltpu.make_async_copy(cots[2 * j], dmix.at[pl.ds(0, half)], lsems.at[4]),
+            pltpu.make_async_copy(cots[2 * j + 1], dmix.at[pl.ds(half, half)], lsems.at[5]),
+        ]
+        for copy in gets:
+            copy.start()
         hit = one_hot(src_col[...] == iota((tokens, tokens), 1) + j * tokens)
-        get.wait()
+        for copy in gets:
+            copy.wait()
         dy = dy + mm(hit, dmix[...])
     dproj[:, :width] = dy.astype(BF)
     for copy in loads:
@@ -1017,10 +1277,12 @@
     dchosen = gate * (dgate - jnp.sum(gate * dgate, axis=1, keepdims=True))
     dlogits = dchosen.astype(BF)
     router_t = mm_tn(dlogits, moe[...])
-    for j in range(nblk):
-        s_own[pl.ds(pl.multiple_of((r ^ j) * local, local), local), :] = router_t[
-            j * local : (j + 1) * local, :
-        ]
+    for i in range(pairs):
+        for j in range(nblk):
+            refs[12][i, pl.ds(pl.multiple_of((r ^ j) * local, local), local), :] = router_t[
+                j * local : (j + 1) * local, i * 2 * shard : (i + 1) * 2 * shard
+            ]
+    routers.share.start()
     dmoe = mm_nt(dlogits, w_router[...]) + own[0].astype(F32)
     dms.finish()
     for copy in ess:
@@ -1036,9 +1298,9 @@
     for j in range(nblk):
         cols = slice(j * ow, (j + 1) * ow)
         dmix[:, cols] = mm(dattn, w_att[j, :, :, :, qw:].reshape(width, ow)).astype(BF)
-        wg[j, :, :, :, qw:] = (
-            mm_tn(dattn, mixed[:, cols]).astype(BF).reshape(pairs, 2, shard, ow)
-        )
+        wo[j] = mm_tn(dattn, mixed[:, cols]).astype(BF).reshape(pairs, 2, shard, ow)
+        wos.share(j)
+    routers.over_row()
 
     quad = 4 * hw
     groups = nblk * qw // quad
@@ -1091,28 +1353,26 @@
         igb[0, rows, :] = (dmid[rows, :] + (rx * scaled - x * (rx * rx * rx) * inner)).astype(BF)
         gain_a_part = gain_a_part + jnp.sum(dattn_in * x * rx, axis=0, keepdims=True)
         igs.start(b)
-
-    s_own[EXPERT_COUNT : EXPERT_COUNT + 8, :] = jnp.concatenate(
+        if b == 1:
+            wos.join()
+            routers.over_line()
+
+    refs[18][...] = jnp.concatenate(
         [gain_a_part, gain_m_part, jnp.zeros((6, width), F32)], axis=0
     )
-    s_share.start()
+    gains.share.start()
+    wos.middle()
     for j in range(nblk):
-        wg[j, :, :, :, :qw] = (
+        wq[j] = (
             mm_tn(attn[...], dproj[:, j * qw : (j + 1) * qw])
             .astype(BF)
             .reshape(pairs, 2, shard, qw)
         )
-        wg_share[j].start()
+        wqs.share(j)
     igs.forward(1)
     igs.forward(0)
-    s_share.wait_recv()
-    s_sum[...] = s_own[...] + s_sib[...]
-    for copy in s_rows:
-        copy.start()
-    for j in (3, 1, 2, 0):
-        wg_share[j].wait_recv()
-        wg[j, :, pl.ds(k, 1)] = plus(wg[j, :, pl.ds(k, 1)], wg_sib[j][:, None])
-    wgs.start()
+    gains.over_row()
+    wqs.join()
 
     for copy in ess:
         copy.wait_recv()
@@ -1132,46 +1392,27 @@
     summed = own[0].astype(F32) + (own[1].astype(F32) + rest)
     block_out[...] = (input_grad[...] + RESIDUAL_SCALE * summed).astype(BF)
 
-    for h in range(2):
-        wgs.arrived(h)
-        hz = zpart(h)
-        wg[2 - h, hz, pl.ds(k, 1)] = plus(wg[2 - h, hz, pl.ds(k, 1)], w_across[h][:, None])
-        wgs.send(h)
-    for copy in s_rows:
-        copy.wait_recv()
-    s_chip[...] = tree_sum([s_sum[...]] + [s_row[j] for j in range(nblk - 1)])
-    for copy in s_zs:
-        copy.start()
+    wos.settle()
+    wqs.middle()
+    gains.over_line()
     igs.wait((1, 0), (2, 1))
     total = mm(match(0), igb[0])
     for j in (1, 2):
         total = total + mm(match(j), igb[j])
+    router_out[...] = routers.result()
+    out_grad[...] = wos.result()
+    wqs.settle()
     igs.wait((3, 0), (3, 1))
-    total = total + mm(match(3), igb[3])
-    input_grad[...] = total
-    wgs.finish()
-    rowsum[...] = (
-        wg[0, :, pl.ds(k, 1)].reshape(rowsum.shape).astype(F32)
-        + (w_landed[0].astype(F32) + w_landed[1].astype(F32))
-    ).astype(BF)
-    for copy in wg_z:
-        copy.start()
-    for copy in s_zs:
-        copy.wait_recv()
-    small[...] = tree_sum([s_chip[...]] + [s_z[i] for i in range(pairs - 1)])
-    for copy in wg_z:
-        copy.wait_recv()
-    att_grad[...] = tree_sum(
-        [rowsum[pl.ds(z, 1)].reshape(att_grad.shape).astype(F32)]
-        + [w_z[i].astype(F32) for i in range(pairs - 1)]
-    )
-    for group in (wgs, igs):
+    input_grad[...] = total + mm(match(3), igb[3])
+    gains_out[...] = gains.result()
+    qkv_grad[...] = wqs.result()
+    for group in (wos, wqs, igs, routers, gains):
         group.drain()
-    for copy in ess + dgs + wg_share + wg_z + [s_share] + s_rows + s_zs:
+    for copy in ess + dgs:
         copy.wait_send()
 
 
-def backward(dm, es, e_mix, e_half, dgates, mids, cot, *rest):
+def backward(dm, es, e_mix, e_half, dgates, mids, cots, *rest):
     nblk, tokens, width = dm.shape
     w_att = rest[8]
     pairs, shard, both = w_att.shape[1], w_att.shape[3], w_att.shape[4]
@@ -1182,24 +1423,23 @@
         3 * RowScatter.count
         + RowGather.count
         + (nblk - 1)
-        + nblk
-        + (pairs - 1)
-        + 1
-        + (nblk - 1)
-        + (pairs - 1)
+        + 2 * WeightScatter.count(nblk, pairs)
+        + 2 * (nblk + pairs - 1)
     )
-    small = (EXPERT_COUNT + 8, width)
+    router_part = (EXPERT_COUNT, 2 * shard)
     outs = pl.pallas_call(
         functools.partial(back_kernel, nblk),
         out_shape=(
             shape((tokens, width), BF),
             shape((tokens, width), F32),
-            shape((shard, both), F32),
-            shape(small, F32),
+            shape((shard, both * 2 // 3), F32),
+            shape((shard, both // 3), F32),
+            shape(router_part, F32),
+            shape((8, width), F32),
             shape((2, half, width), BF),
         ),
-        in_specs=[ANY] * 4 + [FULL] + [ANY] * 2 + [FULL, ANY] + [FULL] * 14,
-        out_specs=[FULL] * 4 + [ANY],
+        in_specs=[ANY] * 4 + [FULL] + [ANY] * 6 + [FULL, ANY] + [FULL] * 14,
+        out_specs=[FULL] * 6 + [ANY],
         scratch_shapes=[
             pltpu.VMEM((3, tokens, width), BF),
             pltpu.VMEM((2, half, width), BF),
@@ -1211,18 +1451,10 @@
             pltpu.VMEM((tokens, 2 * width), BF),
             pltpu.VMEM((half, width), F32),
             pltpu.VMEM((half, tokens), F32),
-            pltpu.VMEM(w_att.shape, BF),
-            pltpu.VMEM((nblk, pairs, shard, both), BF),
-            pltpu.VMEM((2, pairs // 2, shard, both), BF),
-            pltpu.VMEM((2, pairs, shard, both), BF),
-            pltpu.VMEM((pairs - 1, shard, both), BF),
-            pltpu.VMEM((pairs, shard, both), BF),
-            pltpu.VMEM(small, F32),
-            pltpu.VMEM(small, F32),
-            pltpu.VMEM(small, F32),
-            pltpu.VMEM((nblk - 1, *small), F32),
-            pltpu.VMEM(small, F32),
-            pltpu.VMEM((pairs - 1, *small), F32),
+            *WeightScatter.scratch(nblk, pairs, shard, both // 3),
+            *WeightScatter.scratch(nblk, pairs, shard, both * 2 // 3),
+            *SmallSum.scratch(nblk, pairs, router_part, True),
+            *SmallSum.scratch(nblk, pairs, (8, width), False),
             pltpu.SemaphoreType.DMA((2, count)),
             pltpu.SemaphoreType.DMA((8,)),
         ],
@@ -1231,8 +1463,33 @@
         ),
         cost_estimate=cost(60e9, 100 * MIB),
         name="attention_backward",
-    )(dm, es, e_mix, e_half, dgates, mids, cot, *rest)
-    return outs[:4]
+    )(dm, es, e_mix, e_half, dgates, *mids, *cots, *rest)
+    return outs[:6]
+
+
+def collect_kernel(*refs):
+    parts, outs = refs[:-3], refs[-3:]
+    rows = jnp.concatenate([part[...].astype(F32) for part in parts], axis=0)
+    fe = outs[0].shape[2]
+    for i in range(3):
+        outs[i][...] = jnp.swapaxes(rows[:, :, i * fe : (i + 1) * fe], 0, 1)
+
+
+def collect(parts):
+    count = sum(part.shape[0] for part in parts)
+    _, shard, fe3 = parts[0].shape
+    step = min(16, shard)
+    out = jax.ShapeDtypeStruct((shard, count, fe3 // 3), F32)
+    return pl.pallas_call(
+        collect_kernel,
+        grid=(shard // step,),
+        out_shape=[out] * 3,
+        in_specs=[pl.BlockSpec((part.shape[0], step, fe3), lambda i: (0, i, 0)) for part in parts],
+        out_specs=[pl.BlockSpec((step, count, fe3 // 3), lambda i: (i, 0, 0))] * 3,
+        compiler_params=params(32),
+        cost_estimate=cost(1e6, 9 * MIB),
+        name="collect",
+    )(*parts)
 
 
 def swap_over(value, axis, size, step):
@@ -1278,16 +1535,14 @@
         [lax.dynamic_slice_in_dim(w_router, (r ^ j) * local, local, 1) for j in range(rows)], axis=1
     )
     router_own = jnp.pad(router_own, ((0, 0), (0, LANES - EXPERT_COUNT)))
-    w_half = jnp.stack(
-        spread_rows(jnp.concatenate([w_qkv, w_out, router_own], axis=1), "col", cols, 2)
-    )
+    w_parts = spread_rows(jnp.concatenate([w_qkv, w_out, router_own], axis=1), "col", cols, 2)
 
     stacked = jnp.concatenate([w_gate, w_up, w_down], axis=2).transpose(1, 0, 2)
-    sizes = [local - 2 * (local * 3 // 8), local * 3 // 8, local * 3 // 8][::-1]
+    sizes = [local // 4, local - 5 * local // 8, 3 * local // 8]
     bases = [sum(sizes[:i]) for i in range(len(sizes))]
-    gathered = [
-        lax.all_gather(stacked[i : i + n], "col", axis=0) for i, n in zip(bases, sizes)
-    ]
+    pieces = [stacked[i : i + n] for i, n in zip(bases, sizes)]
+    pieces[0], pieces[1], *w_parts = lax.optimization_barrier((pieces[0], pieces[1], *w_parts))
+    gathered = [lax.all_gather(piece, "col", axis=0) for piece in pieces[:-1]]
 
     lengths = seq_lengths[0]
     perm = seq_order[0]
@@ -1329,66 +1584,83 @@
         mixed,
         middle,
         moe,
+        cot_first,
         slot_cols,
         slot_rows,
-        chosen,
+        gates,
+        packed,
         w_att,
         moe_own,
         slot_given,
         given_rows,
         mid16,
         router_x,
+        following,
     ) = front(
         block_in[0],
-        w_half,
-        src_col,
-        own_starts,
-        cos_w,
-        sin_w,
-        gain_a,
-        gain_m,
-        expert_ids[0],
-        places[0],
-        src_row,
+        cotangent[0],
+        pieces[-1],
+        w_parts,
+        [
+            src_col,
+            own_starts,
+            cos_w,
+            sin_w,
+            gain_a,
+            gain_m,
+            expert_ids[0].T,
+            places[0].T,
+            src_row,
+        ],
         rows,
-        pairs,
     )
-
     router_x = router_x.reshape(width, LANES)
-    gates, packed = router(moe, router_x, chosen)
 
     acc = carried = None
     summed = []
-    final = len(gathered) - 1
-    spare = [cotangent[0], mid16]
+    final = len(sizes) - 1
     full = []
-    for i, w in enumerate(gathered):
-        own = spare[i] if i < 2 else None
+    for i in range(len(sizes)):
+        w = gathered[i] if i < final else following
+        moved = [("rest", cotangent[0], cot_first), ("sides", mid16)]
+        moved = moved[i] if i < 2 else ("corner", full[1])
         if i > 0:
             w, *carried = lax.optimization_barrier((w, *carried))
+        stage = 2 * i + 1 if i < final else 0
         parts = experts_forward(
-            moe, slot_rows, slot_given, packed, w, acc, own, bases[i], i == final, capacity, 3 + i
+            moe, slot_rows, slot_given, packed, w, acc, moved, (stage, following), bases[i], i == final, capacity, 3 + i
         )
         kept, acc = parts[:4], parts[4]
-        full += parts[5:]
+        full.append(parts[5])
+        if i == 1:
+            held, acc = lax.optimization_barrier((held, acc))
+            summed.append(lax.psum_scatter(held, "col", scatter_dimension=0, tiled=False))
+        if stage:
+            following = parts[6]
+            stage += 1
         rows_in = given_rows
         if i == final:
             rows_in = lax.optimization_barrier((given_rows, summed[0]))[0]
         grads, *carried = experts_reverse(
-            full[0], rows_in, slot_cols, kept, w, carried, acc, bases[i], i == final, capacity, 7
+            (cotangent[0], cot_first, full[0]), rows_in, slot_cols, kept, w, carried, acc, (stage, following), bases[i], i == final, capacity, 6 + i
         )
-        summed.append(lax.psum_scatter(grads, "col", scatter_dimension=0, tiled=False))
+        if stage:
+            following = carried.pop()
+        if i == 0:
+            held = grads
+        else:
+            summed.append(lax.psum_scatter(grads, "col", scatter_dimension=0, tiled=False))
     es = acc
     dm, dgates, e_mix, e_across, e_half = carried
-    block_out, input_grad, att_grad, small = backward(
+    block_out, input_grad, qkv_grad, out_grad, router_part, gains = backward(
         dm,
         es,
         e_mix,
         e_half,
         dgates,
-        full[1],
-        full[0],
-        gates[:tokens],
+        [mid16, full[1], full[2]],
+        (cotangent[0], cot_first, full[0]),
+        gates,
         middle,
         moe_own,
         src_col[:tokens],
@@ -1405,23 +1677,20 @@
         gain_m,
         src_row,
     )
-    router_all = small[:EXPERT_COUNT].T
-    router_grad = lax.dynamic_slice_in_dim(router_all, c * shard, shard, 0)
-    def collect(i):
-        parts = [g[:, :, i * fe : (i + 1) * fe] for g in summed]
-        return jnp.concatenate(parts, axis=0).astype(F32).transpose(1, 0, 2)
-
+    router_grad = lax.dynamic_slice_in_dim(router_part, c % 2 * shard, shard, 1).T
+
+    gate_grad, up_grad, down_grad = collect(summed)
     return (
         block_out[None],
         input_grad[None],
-        small[EXPERT_COUNT],
-        att_grad[:, :qw],
-        att_grad[:, qw:],
-        small[EXPERT_COUNT + 1],
+        gains[0],
+        qkv_grad,
+        out_grad,
+        gains[1],
         router_grad,
-        collect(0),
-        collect(1),
-        collect(2),
+        gate_grad,
+        up_grad,
+        down_grad,
     )
 
 

time: 633 us -> 589 us (0.930); the launches traced: 621 us -> 586 us
  Pallas kernels: 522 us -> 494 us
  local copies, waits for them, and re-layouts: 40.1 us -> 21.4 us
  waiting for transfers between devices: 32.5 us -> 46.4 us
    reduce_scatter x3 -> x2, waiting for transfers between devices: 0.06 us -> 30.9 us  [body(): lax.psum_scatter(grads, 'col', scatter_dimension=0, tiled=False)]
    pallas_call x1, Pallas kernels: 163 us -> 143 us  [backward(): pl.pallas_call(functools.partial(back_kernel, nblk), out_shape=(shape((to...]
    ppermute x3, waiting for transfers between devices: 31.7 us -> 14.4 us  [swap_over(): return lax.ppermute(value, axis, [(i, i ^ step) for i in range(size)])]
    pallas_call x3, Pallas kernels: 105 us -> 91.3 us  [experts_forward(): pl.pallas_call(functools.partial(forward_kernel, base, first, last, gathe...]
    unnamed x44 -> x39, local copies, waits for them, and re-layouts: 21.8 us -> 9.05 us
    slice x10 -> x3, local copies, waits for them, and re-layouts: 11.4 us -> 4.02 us  [the longest x2 2.59 us: body(): pieces = [stacked[i:i + n] for i, n in zip(bases, sizes)]]
  transfers between devices with their start and end apart: 9 -> 8, of which waited for: 2 -> 5; matrix products, arithmetic and copies ran while one was open for 4% -> 3% of each run, Pallas kernels for 84% -> 79%
where the time goes in v4:
time: 589 us; the launch traced here: 586 us
  Pallas kernels  494 us (84%)
  waiting for transfers between devices  46.4 us (8%)
  local copies, waits for them, and re-layouts  21.4 us (4%)
  between operations  14.3 us (2%)
  other arithmetic  6.45 us (1%)
    pallas_call x1, Pallas kernels, backward(): pl.pallas_call(functools.partial(back_kernel, nblk), out_shape=(shape((to...  143 us
    pallas_call x1, Pallas kernels, front(): pl.pallas_call(functools.partial(front_kernel, pairs), out_shape=(shape((...  141 us
    pallas_call x3, Pallas kernels, experts_reverse(): pl.pallas_call(functools.partial(reverse_kernel, base, first, last, stage...  114 us
    pallas_call x3, Pallas kernels, experts_forward(): pl.pallas_call(functools.partial(forward_kernel, base, first, last, gathe...  91.3 us
    reduce_scatter x2, waiting for transfers between devices, body(): lax.psum_scatter(grads, 'col', scatter_dimension=0, tiled=False)  30.9 us
    ppermute x3, waiting for transfers between devices, swap_over(): return lax.ppermute(value, axis, [(i, i ^ step) for i in range(size)])  14.4 us
  transfers between devices with their start and end apart: 8, of which 5 were waited for; matrix products, arithmetic and copies ran while one was open for 3% of the time, Pallas kernels for 79%

profile of v4, /device:TPU:9, one launch (start us, length us, event | category | flops | bytes accessed | tf_op | source)
XLA Modules:
  0.0 585.8 jit_solution(13506577323215366867)
XLA Ops:
  7.3 0.9 constant_dynamic-slice_fusion.3
  8.3 1.0 fusion.1.refs_3_
  9.3 2.5 collective-permute-start.1
  12.0 1.5 copy.70
  14.5 1.7 fusion.7
  16.2 0.9 slice.37
  17.7 4.0 collective-permute-done.1.refs_5_
  21.8 9.7 %collective-permute-done.2.refs_6_ = bf16[128,896]{1,0:T(8,128)(2,1)S(1)} collective-permute-done((bf16[128,896]{1,0:T(8,128)(2,1)S(1)}, bf16[128,896]{1,0:T(8,128)(2,1)S(1)}, u32[]{:S(2)}, u32[]{:S(2)}) %collective-permute-start.2) | collective-permute-done | bytes 229408 | tf_op jit(solution)/shard_map/ppermute | solution.py:1496
  31.6 0.7 all-gather.7.cloned.1.call-update
  34.1 0.9 copy.77.refs_8_.refs_21_
  35.0 2.4 multiply_sine_fusion
  37.4 1.3 concatenate.25.refs_9_.refs_22_
  38.8 2.2 concatenate.27.refs_10_.refs_23_
  41.6 1.1 add_xor_fusion.refs_7_
  42.7 141.5 %attention_forward.1 = (bf16[512,1024]{1,0:T(8,128)(2,1)}, bf16[512,1024]{1,0:T(8,128)(2,1)}, bf16[512,2048]{1,0:T(8,128)(2,1)}, bf16[512,1024]{1,0:T(8,128)(2,1...) custom-call(bf16[512,1024]{1,0:T(8,128)(2,1)} %bitcast.51, ...), custom_call_target="tpu_custom_call" | custom-call | flops 20000000000 | bytes 62914560 | tf_op jit(solution)/shard_map/attention_forward/pallas_call | solution.py:349
  184.3 31.2 %experts_forward.3 = (bf16[2,512,1024]{2,1,0:T(8,128)(2,1)}, f32[2,512,512]{2,1,0:T(8,128)}, f32[2,512,512]{2,1,0:T(8,128)}, f32[2,512,128]{2,1,0:T(8,128)}, f32...) custom-call(bf16[4,512,1024]{2,1,0:T(8,128)(2,1)} %get-tuple-element, ...), custom_call_target="tpu_custom_call", output_to_operand_aliasing={{6}: (7, {})} | custom-call | flops 14000000000 | bytes 31457280 | tf_op jit(solution)/shard_map/experts_forward/pallas_call | solution.py:649
  215.5 30.8 %experts_reverse.3 = (bf16[8,2,128,1536]{3,2,1,0:T(8,128)(2,1)}, f32[2048,1024]{1,0:T(8,128)}, f32[2048,128]{1,0:T(8,128)}, bf16[8,3,128,1536]{3,2,1,0:T(8,128)(2,1)}) custom-call(bf16[512,1024]{1,0:T(8,128)(2,1)} %bitcast.54, bf16[2,256,1024]{2,1,0:T(8,128)(2,1)} %get-tuple-element.89.refs_6_.refs_1_.refs_9_, ...), custom_call_target="tpu_custom_call", output_to_operand_aliasing={{3}: (10, {})} | custom-call | flops 17999998976 | bytes 41943040 | tf_op jit(solution)/shard_map/experts_reverse/pallas_call | solution.py:998
  246.3 30.1 %experts_forward.4 = (bf16[3,512,1024]{2,1,0:T(8,128)(2,1)}, f32[3,512,512]{2,1,0:T(8,128)}, f32[3,512,512]{2,1,0:T(8,128)}, f32[3,512,128]{2,1,0:T(8,128)}, f32...) custom-call(bf16[4,512,1024]{2,1,0:T(8,128)(2,1)} %get-tuple-element, ...), custom_call_target="tpu_custom_call", output_to_operand_aliasing={{4}: (5, {}), {6}: (7, {})} | custom-call | flops 20999999488 | bytes 31457280 | tf_op jit(solution)/shard_map/experts_forward/pallas_call | solution.py:649
  276.5 39.9 %experts_reverse.4 = (bf16[8,3,128,1536]{3,2,1,0:T(8,128)(2,1)}, f32[2048,1024]{1,0:T(8,128)}, f32[2048,128]{1,0:T(8,128)}, bf16[8,3,128,1536]{3,2,1,0:T(8,128)(2,1)}) custom-call(bf16[512,1024]{1,0:T(8,128)(2,1)} %bitcast.55, ...), custom_call_target="tpu_custom_call", output_to_operand_aliasing={{1}: (10, {}), {2}: (11, {}), {3}: (12, {})} | custom-call | flops 27000000512 | bytes 41943040 | tf_op jit(solution)/shard_map/experts_reverse/pallas_call | solution.py:998
  316.5 29.9 %experts_forward.5 = (bf16[3,512,1024]{2,1,0:T(8,128)(2,1)}, f32[3,512,512]{2,1,0:T(8,128)}, f32[3,512,512]{2,1,0:T(8,128)}, f32[3,512,128]{2,1,0:T(8,128)}, bf1...) custom-call(bf16[4,512,1024]{2,1,0:T(8,128)(2,1)} %get-tuple-element.90.refs_0_, ...), custom_call_target="tpu_custom_call" | custom-call | flops 20999999488 | bytes 31457280 | tf_op jit(solution)/shard_map/experts_forward/pallas_call | solution.py:649
  346.8 43.2 %experts_reverse.5 = (bf16[8,3,128,1536]{3,2,1,0:T(8,128)(2,1)}, bf16[4,512,1024]{2,1,0:T(8,128)(2,1)}, f32[8,2048]{1,0:T(8,128)}, bf16[2,256,1024]{2,1,0:T(8,12...) custom-call(bf16[512,1024]{1,0:T(8,128)(2,1)} %bitcast.56, ...), custom_call_target="tpu_custom_call" | custom-call | flops 27000000512 | bytes 41943040 | tf_op jit(solution)/shard_map/experts_reverse/pallas_call | solution.py:998
  390.7 0.9 copy.78.refs_14_
  391.6 143.5 %attention_backward.1 = (bf16[512,1024]{1,0:T(8,128)(2,1)}, f32[512,1024]{1,0:T(8,128)}, f32[128,512]{1,0:T(8,128)}, f32[128,256]{1,0:T(8,128)}, f32[32,256]{1,0...) custom-call(bf16[4,512,1024]{2,1,0:T(8,128)(2,1)} %get-tuple-element.135.refs_0_, ...), custom_call_target="tpu_custom_call" | custom-call | flops 60000002048 | bytes 104857600 | tf_op jit(solution)/shard_map/attention_backward/pallas_call | solution.py:1430
  535.1 1.3 dynamic-slice_bitcast_fusion
  536.4 1.4 fusion.8
  537.8 30.9 %reduce-scatter.8.cloned.1.call-done = bf16[1,3,128,1536]{3,2,1,0:T(8,128)(2,1)} async-done(((bf16[8,3,128,1536]{3,2,1,0:T(8,128)(2,1)}), bf16[1,3,128,1536]{3,2,1,0:T(8,128)(2,1)}) %reduce-scatter.8.cloned.1.call-update) | async-done | bytes 1179664 | tf_op jit(solution)/shard_map/reduce_scatter | solution.py:1652
  568.7 1.3 copy-done
  570.0 1.3 copy-done.1
  571.3 4.1 collect.1
  575.4 1.0 copy.91
  576.4 1.3 copy.92
  577.7 0.7 copy.93
  (65 shorter events, 6.3 us)
Async XLA Ops:
  7.2 6.3 %copy-start.4 = (bf16[128,8,512]{2,1,0:T(8,128)(2,1)S(1)}, bf16[128,8,512]{2,1,0:T(8,128)(2,1)}, u32[]{:S(2)}) copy-start(bf16[128,8,512]{2,1,0:T(8,128)(2,1)} %param.26) | copy-start | bytes 3145732
  7.2 6.6 %copy-start.5 = (bf16[128,8,512]{2,1,0:T(8,128)(2,1)S(1)}, bf16[128,8,512]{2,1,0:T(8,128)(2,1)}, u32[]{:S(2)}) copy-start(bf16[128,8,512]{2,1,0:T(8,128)(2,1)} %param.25) | copy-start | bytes 3145732
  7.2 177.1 %all-gather.5.cloned.1.call-start = ((), (), s32[]{:S(2)}) async-start(), calls=%async_computation.6 | async-start | bytes 7077888 | tf_op jit(solution)/shard_map/all_gather | solution.py:1545
  9.2 5.2 copy-start.8
  9.2 8.5 %collective-permute-start = (bf16[128,896]{1,0:T(8,128)(2,1)S(1)}, bf16[128,896]{1,0:T(8,128)(2,1)S(1)}, u32[]{:S(2)}, u32[]{:S(2)}) collective-permute-start(bf16[128,896]{1,0:T(8,128)(2,1)S(1)} %fusion.1.refs_3_), channel_id=1, source_target_pairs={{0,2},{1,3},{2,0},{3,1},{4,6},{5,7},{6,4},{7,5},{8,10},{9,11},{10,... | collective-permute-start | bytes 688136 | tf_op jit(solution)/shard_map/ppermute | solution.py:1496
  9.3 12.4 %collective-permute-start.1 = (bf16[128,896]{1,0:T(8,128)(2,1)S(1)}, bf16[128,896]{1,0:T(8,128)(2,1)S(1)}, u32[]{:S(2)}, u32[]{:S(2)}) collective-permute-start(bf16[128,896]{1,0:T(8,128)(2,1)S(1)} %fusion.1.refs_3_), channel_id=1, source_target_pairs={{0,4},{1,5},{2,6},{3,7},{4,0},{5,1},{6,2},{7,3},{8,12},{9,13},{10,... | collective-permute-start | bytes 688136 | tf_op jit(solution)/shard_map/ppermute | solution.py:1496
  11.8 19.7 %collective-permute-start.2 = (bf16[128,896]{1,0:T(8,128)(2,1)S(1)}, bf16[128,896]{1,0:T(8,128)(2,1)S(1)}, u32[]{:S(2)}, u32[]{:S(2)}) collective-permute-start(bf16[128,896]{1,0:T(8,128)(2,1)S(1)} %fusion.1.refs_3_), channel_id=1, source_target_pairs={{0,6},{1,7},{2,4},{3,5},{4,2},{5,3},{6,0},{7,1},{8,14},{9,15},{10,... | collective-permute-start | bytes 688136 | tf_op jit(solution)/shard_map/ppermute | solution.py:1496
  14.5 17.8 %copy-start.11 = (s32[1,12]{1,0:T(1,128)S(1)}, s32[1,12]{1,0:T(1,128)}, u32[]{:S(2)}) copy-start(s32[1,12]{1,0:T(1,128)} %param.16) | copy-start | bytes 148
  14.5 17.8 %copy-start.12 = (s32[1,12]{1,0:T(1,128)S(1)}, s32[1,12]{1,0:T(1,128)}, u32[]{:S(2)}) copy-start(s32[1,12]{1,0:T(1,128)} %param.17) | copy-start | bytes 148
  17.7 17.3 %copy-start.13 = (bf16[128,896]{1,0:T(8,128)(2,1)}, bf16[128,896]{1,0:T(8,128)(2,1)S(1)}, u32[]{:S(2)}) copy-start(bf16[128,896]{1,0:T(8,128)(2,1)S(1)} %collective-permute-done.refs_4_) | copy-start | bytes 688132
  21.8 13.3 %copy-start.14 = (bf16[128,896]{1,0:T(8,128)(2,1)}, bf16[128,896]{1,0:T(8,128)(2,1)S(1)}, u32[]{:S(2)}) copy-start(bf16[128,896]{1,0:T(8,128)(2,1)S(1)} %collective-permute-done.1.refs_5_) | copy-start | bytes 688132
  31.5 3.5 copy-start.15
  31.5 214.8 %all-gather.7.cloned.1.call-start = ((), (), s32[]{:S(2)}) async-start(), calls=%async_computation.7 | async-start | bytes 10616832 | tf_op jit(solution)/shard_map/all_gather | solution.py:1545
  32.3 314.5 %reduce-scatter.4.cloned.1.call-start = ((), (), s32[]{:S(2)}) async-start(), calls=%async_computation.3 | async-start | bytes 7077888 | tf_op jit(solution)/shard_map/reduce_scatter | solution.py:1637
  276.5 261.3 %reduce-scatter.6.cloned.1.call-start = ((), (), s32[]{:S(2)}) async-start(), calls=%async_computation.4 | async-start | bytes 10616832 | tf_op jit(solution)/shard_map/reduce_scatter | solution.py:1652
  316.5 252.2 %reduce-scatter.8.cloned.1.call-start = ((), (), s32[]{:S(2)}) async-start(), calls=%async_computation.5 | async-start | bytes 10616832 | tf_op jit(solution)/shard_map/reduce_scatter | solution.py:1652
  390.0 0.7 copy-start.10
  391.6 177.2 %copy-start.2 = (bf16[1,2,128,1536]{3,2,1,0:T(8,128)(2,1)S(1)}, bf16[1,2,128,1536]{3,2,1,0:T(8,128)(2,1)}, u32[]{:S(2)}) copy-start(bf16[1,2,128,1536]{3,2,1,0:T(8,128)(2,1)} %reduce-scatter.4.cloned.1.call-done) | copy-start | bytes 2359300
  568.7 1.3 copy-start
  570.0 1.3 copy-start.1
  571.3 4.1 copy-start.6
  571.3 5.1 copy-start.3
  575.4 2.3 copy-start.7
  575.4 3.0 copy-start.9
Sparse Core Ops, SparseCore 0:
  31.6 64.2 all-gather.4
  98.1 88.8 all-gather.6
  276.6 70.1 reduce-scatter.3
  348.9 98.1 reduce-scatter.5
  449.3 119.3 reduce-scatter.7

commit v5 on v4

--- a/solution.py
+++ b/solution.py
@@ -529,6 +529,12 @@
         for copy in copies:
             copy.wait()
 
+    if stage:
+
+        @pl.when(step == steps - 1)
+        def _():
+            line.advance()
+
     if early:
 
         @pl.when(step == steps - 1)
@@ -644,7 +650,7 @@
         in_specs.append(ANY)
         outs.append(shape(following.shape, BF))
         out_specs.append(ANY)
-        scratch.append(LineGather.scratch(cols // 2))
+        scratch.append(LineGather.scratch(cols // 2, following.shape[1]))
     options.update(collective_id=key, has_side_effects=True)
     return pl.pallas_call(
         functools.partial(forward_kernel, base, first, last, gathers, stage, local, capacity),
@@ -662,13 +668,14 @@
 
 class LineGather:
     def __init__(self, stage, src, dst, sems, r, c):
-        self.pairs = src.shape[0] // 2
+        self.pairs, self.count = src.shape[0] // 2, src.shape[1]
         self.stage, self.src, self.dst, self.sems = stage, src, dst, sems
         self.z, self.k = c // 2, c % 2
-        count = 2 * self.pairs
-        hops = list(range(1, self.pairs))
-        cut = [(len(hops) * i) // 3 for i in range(4)]
-        self.hops = hops[cut[stage - 1] : cut[stage]] if stage < 4 else []
+        slots = []
+        for slot in range(self.pairs + self.count - 2):
+            moves = [(slot - e + 1, e) for e in range(self.count)]
+            slots.append([(hop, e) for hop, e in moves if 1 <= hop < self.pairs])
+        self.slots = [slots[:1], slots[1:-1], slots[-1:], []][stage - 1]
         self.swaps = []
         if stage == 4:
             self.devices = [(r, c ^ 1)]
@@ -676,59 +683,73 @@
                 slot = 2 * i + self.k
                 self.swaps.append(link(src.at[slot], dst.at[slot], sems, i, (r, c ^ 1)))
         else:
-            self.devices = [(r, (c + 2) % count), (r, (c - 2) % count)]
+            devices = 2 * self.pairs
+            self.devices = [(r, (c + 2) % devices), (r, (c - 2) % devices)]
 
     def place(self, side):
         return self.z if side == 0 else self.pairs - 1 - self.z
 
-    def copy(self, side, hop):
+    def copy(self, side, hop, e):
         at = jnp.maximum(self.place(side) - hop + 1, 0)
         slot = 2 * (at if side == 0 else self.pairs - 1 - at) + self.k
-        src = self.src if hop == self.hops[0] else self.dst
-        index = side * (self.pairs - 1) + hop - 1
-        return link(src.at[slot], self.dst.at[slot], self.sems, index, self.devices[side])
+        here = any((hop - 1, e) in moves for moves in self.slots)
+        src = self.dst if here else self.src
+        index = (side * (self.pairs - 1) + hop - 1) * self.count + e
+        return link(
+            src.at[slot, e], self.dst.at[slot, e], self.sems, index, self.devices[side]
+        )
 
     def sends(self, side, hop):
         return (self.place(side) >= hop - 1) & (self.place(side) <= self.pairs - 2)
 
-    def hop(self, hop):
-        for side in range(2):
-
-            @pl.when(self.sends(side, hop))
-            def _():
-                self.copy(side, hop).start()
+    def send(self, moves):
+        for hop, e in moves:
+            for side in range(2):
+
+                @pl.when(self.sends(side, hop))
+                def _():
+                    self.copy(side, hop, e).start()
 
     def start(self):
         for copy in self.swaps:
             copy.start()
-        if self.hops:
-            self.hop(self.hops[0])
+        if self.slots:
+            self.send(self.slots[0])
+
+    def land(self, number):
+        for hop, e in self.slots[number]:
+            for side in range(2):
+
+                @pl.when(self.place(side) >= hop)
+                def _():
+                    self.copy(side, hop, e).wait_recv()
+
+        if number + 1 < len(self.slots):
+            self.send(self.slots[number + 1])
+
+    def advance(self):
+        if len(self.slots) > 1:
+            self.land(0)
 
     def finish(self):
         for copy in self.swaps:
             copy.wait_recv()
-        for hop in self.hops:
-            for side in range(2):
-
-                @pl.when(self.place(side) >= hop)
-                def _():
-                    self.copy(side, hop).wait_recv()
-
-            if hop != self.hops[-1]:
-                self.hop(hop + 1)
-        for hop in self.hops:
-            for side in range(2):
-
-                @pl.when(self.sends(side, hop))
-                def _():
-                    self.copy(side, hop).wait_send()
+        for number in range(1 if len(self.slots) > 1 else 0, len(self.slots)):
+            self.land(number)
+        for moves in self.slots:
+            for hop, e in moves:
+                for side in range(2):
+
+                    @pl.when(self.sends(side, hop))
+                    def _():
+                        self.copy(side, hop, e).wait_send()
 
         for copy in self.swaps:
             copy.wait_send()
 
     @staticmethod
-    def scratch(pairs):
-        return pltpu.SemaphoreType.DMA((2, 2 * pairs))
+    def scratch(pairs, count):
+        return pltpu.SemaphoreType.DMA((2, max(2 * (pairs - 1) * count, pairs)))
 
 
 def cot_pieces(own, first, rest):
@@ -832,6 +853,12 @@
     sig = jax.nn.sigmoid(gate_in)
     silu = gate_in * sig
     hidden = (silu * up_in).astype(BF)
+    if stage:
+
+        @pl.when(step == (steps - 1) // 2)
+        def _():
+            line.advance()
+
     dhidden = mm(dslot[...], w[:, 0, :, 2 * fe :].reshape(width, fe))
     dgate = (dhidden * up_in * sig * (1.0 + gate_in * (1.0 - sig))).astype(BF)
     dup = (dhidden * silu).astype(BF)
@@ -993,7 +1020,7 @@
         in_specs.append(ANY)
         outs.append(shape(following.shape, BF))
         out_specs.append(ANY)
-        scratch.append(LineGather.scratch(cols // 2))
+        scratch.append(LineGather.scratch(cols // 2, following.shape[1]))
         options.update(collective_id=key, has_side_effects=True)
     return pl.pallas_call(
         functools.partial(reverse_kernel, base, first, last, stage, local, capacity),
@@ -1538,7 +1565,7 @@
     w_parts = spread_rows(jnp.concatenate([w_qkv, w_out, router_own], axis=1), "col", cols, 2)
 
     stacked = jnp.concatenate([w_gate, w_up, w_down], axis=2).transpose(1, 0, 2)
-    sizes = [local // 4, local - 5 * local // 8, 3 * local // 8]
+    sizes = [3 * local // 8, 3 * local // 8, local // 4]
     bases = [sum(sizes[:i]) for i in range(len(sizes))]
     pieces = [stacked[i : i + n] for i, n in zip(bases, sizes)]
     pieces[0], pieces[1], *w_parts = lax.optimization_barrier((pieces[0], pieces[1], *w_parts))
@@ -1626,18 +1653,15 @@
         moved = moved[i] if i < 2 else ("corner", full[1])
         if i > 0:
             w, *carried = lax.optimization_barrier((w, *carried))
-        stage = 2 * i + 1 if i < final else 0
+        stage = (1, 3, 0)[i]
         parts = experts_forward(
             moe, slot_rows, slot_given, packed, w, acc, moved, (stage, following), bases[i], i == final, capacity, 3 + i
         )
         kept, acc = parts[:4], parts[4]
         full.append(parts[5])
-        if i == 1:
-            held, acc = lax.optimization_barrier((held, acc))
-            summed.append(lax.psum_scatter(held, "col", scatter_dimension=0, tiled=False))
         if stage:
             following = parts[6]
-            stage += 1
+        stage = (2, 4, 0)[i]
         rows_in = given_rows
         if i == final:
             rows_in = lax.optimization_barrier((given_rows, summed[0]))[0]
@@ -1646,10 +1670,7 @@
         )
         if stage:
             following = carried.pop()
-        if i == 0:
-            held = grads
-        else:
-            summed.append(lax.psum_scatter(grads, "col", scatter_dimension=0, tiled=False))
+        summed.append(lax.psum_scatter(grads, "col", scatter_dimension=0, tiled=False))
     es = acc
     dm, dgates, e_mix, e_across, e_half = carried
     block_out, input_grad, qkv_grad, out_grad, router_part, gains = backward(

time: 589 us -> 580 us (0.985)
  waiting for transfers between devices: 46.4 us -> 27 us
  Pallas kernels: 494 us -> 504 us
    reduce_scatter x2 -> x3, waiting for transfers between devices: 30.9 us -> 10.8 us  [body(): lax.psum_scatter(grads, 'col', scatter_dimension=0, tiled=False)]
    pallas_call x1, Pallas kernels: 143 us -> 152 us  [backward(): pl.pallas_call(functools.partial(back_kernel, nblk), out_shape=(shape((to...]
    pallas_call x3, Pallas kernels: 114 us -> 121 us  [experts_reverse(): pl.pallas_call(functools.partial(reverse_kernel, base, first, last, stage...]
  transfers between devices with their start and end apart: 8 -> 8, of which waited for: 5 -> 5; matrix products, arithmetic and copies ran while one was open for 3% -> 3% of each run, Pallas kernels for 79% -> 87%
where the time goes in v5:
time: 580 us; the launch traced here: 576 us
  Pallas kernels  504 us (87%)
  waiting for transfers between devices  27 us (5%)
  local copies, waits for them, and re-layouts  21.9 us (4%)
  between operations  14.2 us (2%)
  other arithmetic  6.1 us (1%)
    pallas_call x1, Pallas kernels, backward(): pl.pallas_call(functools.partial(back_kernel, nblk), out_shape=(shape((to...  152 us
    pallas_call x1, Pallas kernels, front(): pl.pallas_call(functools.partial(front_kernel, pairs), out_shape=(shape((...  141 us
    pallas_call x3, Pallas kernels, experts_reverse(): pl.pallas_call(functools.partial(reverse_kernel, base, first, last, stage...  121 us
    pallas_call x3, Pallas kernels, experts_forward(): pl.pallas_call(functools.partial(forward_kernel, base, first, last, gathe...  86 us
    ppermute x3, waiting for transfers between devices, swap_over(): return lax.ppermute(value, axis, [(i, i ^ step) for i in range(size)])  15.4 us
  transfers between devices with their start and end apart: 8, of which 5 were waited for; matrix products, arithmetic and copies ran while one was open for 3% of the time, Pallas kernels for 87%

profile of v5, /device:TPU:9, one launch (start us, length us, event | category | flops | bytes accessed | tf_op | source)
XLA Modules:
  0.0 576.0 jit_solution(2782918052679568132)
XLA Ops:
  7.3 0.9 constant_dynamic-slice_fusion.3
  8.3 1.0 fusion.1.refs_3_
  9.3 2.5 collective-permute-start.1
  12.0 1.5 copy.70
  14.5 1.6 fusion.7
  16.1 1.7 collective-permute-done.refs_4_
  17.7 4.0 collective-permute-done.1.refs_5_
  21.8 9.7 %collective-permute-done.2.refs_6_ = bf16[128,896]{1,0:T(8,128)(2,1)S(1)} collective-permute-done((bf16[128,896]{1,0:T(8,128)(2,1)S(1)}, bf16[128,896]{1,0:T(8,128)(2,1)S(1)}, u32[]{:S(2)}, u32[]{:S(2)}) %collective-permute-start.2) | collective-permute-done | bytes 229408 | tf_op jit(solution)/shard_map/ppermute | solution.py:1523
  33.0 0.9 slice.36.refs_2_
  35.7 0.9 copy.77.refs_8_.refs_21_
  36.6 2.0 multiply_sine_fusion
  38.6 1.3 concatenate.25.refs_9_.refs_22_
  40.0 2.2 concatenate.27.refs_10_.refs_23_
  42.9 1.1 add_xor_fusion.refs_7_
  44.0 140.7 %attention_forward.1 = (bf16[512,1024]{1,0:T(8,128)(2,1)}, bf16[512,1024]{1,0:T(8,128)(2,1)}, bf16[512,2048]{1,0:T(8,128)(2,1)}, bf16[512,1024]{1,0:T(8,128)(2,1...) custom-call(bf16[512,1024]{1,0:T(8,128)(2,1)} %bitcast.51, ...), custom_call_target="tpu_custom_call" | custom-call | flops 20000000000 | bytes 62914560 | tf_op jit(solution)/shard_map/attention_forward/pallas_call | solution.py:349
  184.8 33.2 %experts_forward.3 = (bf16[3,512,1024]{2,1,0:T(8,128)(2,1)}, f32[3,512,512]{2,1,0:T(8,128)}, f32[3,512,512]{2,1,0:T(8,128)}, f32[3,512,128]{2,1,0:T(8,128)}, f32...) custom-call(bf16[4,512,1024]{2,1,0:T(8,128)(2,1)} %get-tuple-element, ...), custom_call_target="tpu_custom_call", output_to_operand_aliasing={{6}: (7, {})} | custom-call | flops 20999999488 | bytes 31457280 | tf_op jit(solution)/shard_map/experts_forward/pallas_call | solution.py:655
  218.0 47.5 %experts_reverse.3 = (bf16[8,3,128,1536]{3,2,1,0:T(8,128)(2,1)}, f32[2048,1024]{1,0:T(8,128)}, f32[2048,128]{1,0:T(8,128)}, bf16[8,2,128,1536]{3,2,1,0:T(8,128)(2,1)}) custom-call(bf16[512,1024]{1,0:T(8,128)(2,1)} %bitcast.54, bf16[2,256,1024]{2,1,0:T(8,128)(2,1)} %get-tuple-element.87.refs_6_.refs_1_.refs_9_, ...), custom_call_target="tpu_custom_call", output_to_operand_aliasing={{3}: (10, {})} | custom-call | flops 27000000512 | bytes 41943040 | tf_op jit(solution)/shard_map/experts_reverse/pallas_call | solution.py:1025
  265.6 30.1 %experts_forward.4 = (bf16[3,512,1024]{2,1,0:T(8,128)(2,1)}, f32[3,512,512]{2,1,0:T(8,128)}, f32[3,512,512]{2,1,0:T(8,128)}, f32[3,512,128]{2,1,0:T(8,128)}, f32...) custom-call(bf16[4,512,1024]{2,1,0:T(8,128)(2,1)} %get-tuple-element, ...), custom_call_target="tpu_custom_call", output_to_operand_aliasing={{4}: (5, {}), {6}: (7, {})} | custom-call | flops 20999999488 | bytes 31457280 | tf_op jit(solution)/shard_map/experts_forward/pallas_call | solution.py:655
  295.7 39.8 %experts_reverse.4 = (bf16[8,3,128,1536]{3,2,1,0:T(8,128)(2,1)}, f32[2048,1024]{1,0:T(8,128)}, f32[2048,128]{1,0:T(8,128)}, bf16[8,2,128,1536]{3,2,1,0:T(8,128)(2,1)}) custom-call(bf16[512,1024]{1,0:T(8,128)(2,1)} %bitcast.55, ...), custom_call_target="tpu_custom_call", output_to_operand_aliasing={{1}: (10, {}), {2}: (11, {}), {3}: (12, {})} | custom-call | flops 27000000512 | bytes 41943040 | tf_op jit(solution)/shard_map/experts_reverse/pallas_call | solution.py:1025
  335.6 22.7 %experts_forward.5 = (bf16[2,512,1024]{2,1,0:T(8,128)(2,1)}, f32[2,512,512]{2,1,0:T(8,128)}, f32[2,512,512]{2,1,0:T(8,128)}, f32[2,512,128]{2,1,0:T(8,128)}, bf1...) custom-call(bf16[4,512,1024]{2,1,0:T(8,128)(2,1)} %get-tuple-element.88.refs_0_, ...), custom_call_target="tpu_custom_call" | custom-call | flops 14000000000 | bytes 31457280 | tf_op jit(solution)/shard_map/experts_forward/pallas_call | solution.py:655
  358.3 6.7 %reduce-scatter.4.cloned.1.call-done = bf16[1,3,128,1536]{3,2,1,0:T(8,128)(2,1)} async-done(((bf16[8,3,128,1536]{3,2,1,0:T(8,128)(2,1)}), bf16[1,3,128,1536]{3,2,1,0:T(8,128)(2,1)}) %reduce-scatter.4.cloned.1.call-update) | async-done | bytes 1179664 | tf_op jit(solution)/shard_map/reduce_scatter | solution.py:1673
  365.0 33.6 %experts_reverse.5 = (bf16[8,2,128,1536]{3,2,1,0:T(8,128)(2,1)}, bf16[4,512,1024]{2,1,0:T(8,128)(2,1)}, f32[8,2048]{1,0:T(8,128)}, bf16[2,256,1024]{2,1,0:T(8,12...) custom-call(bf16[512,1024]{1,0:T(8,128)(2,1)} %bitcast.56, ...), custom_call_target="tpu_custom_call" | custom-call | flops 17999998976 | bytes 41943040 | tf_op jit(solution)/shard_map/experts_reverse/pallas_call | solution.py:1025
  399.3 0.9 copy.78.refs_14_
  400.2 152.0 %attention_backward.1 = (bf16[512,1024]{1,0:T(8,128)(2,1)}, f32[512,1024]{1,0:T(8,128)}, f32[128,512]{1,0:T(8,128)}, f32[128,256]{1,0:T(8,128)}, f32[32,256]{1,0...) custom-call(bf16[4,512,1024]{2,1,0:T(8,128)(2,1)} %get-tuple-element.131.refs_0_, ...), custom_call_target="tpu_custom_call" | custom-call | flops 60000002048 | bytes 104857600 | tf_op jit(solution)/shard_map/attention_backward/pallas_call | solution.py:1457
  552.2 1.3 dynamic-slice_bitcast_fusion
  553.6 1.4 fusion.8
  555.0 4.1 reduce-scatter.8.cloned.1.call-done
  559.1 1.3 copy-done.1
  560.4 1.1 copy-done.2
  561.5 4.1 collect.1
  565.6 1.0 copy.91
  566.6 1.3 copy.92
  (65 shorter events, 7.5 us)
Async XLA Ops:
  7.2 6.3 %copy-start.4 = (bf16[128,8,512]{2,1,0:T(8,128)(2,1)S(1)}, bf16[128,8,512]{2,1,0:T(8,128)(2,1)}, u32[]{:S(2)}) copy-start(bf16[128,8,512]{2,1,0:T(8,128)(2,1)} %param.26) | copy-start | bytes 3145732
  7.2 6.6 %copy-start.5 = (bf16[128,8,512]{2,1,0:T(8,128)(2,1)S(1)}, bf16[128,8,512]{2,1,0:T(8,128)(2,1)}, u32[]{:S(2)}) copy-start(bf16[128,8,512]{2,1,0:T(8,128)(2,1)} %param.25) | copy-start | bytes 3145732
  7.2 177.6 %all-gather.5.cloned.1.call-start = ((), (), s32[]{:S(2)}) async-start(), calls=%async_computation.6 | async-start | bytes 10616832 | tf_op jit(solution)/shard_map/all_gather | solution.py:1572
  9.2 5.2 copy-start.8
  9.2 8.5 %collective-permute-start = (bf16[128,896]{1,0:T(8,128)(2,1)S(1)}, bf16[128,896]{1,0:T(8,128)(2,1)S(1)}, u32[]{:S(2)}, u32[]{:S(2)}) collective-permute-start(bf16[128,896]{1,0:T(8,128)(2,1)S(1)} %fusion.1.refs_3_), channel_id=1, source_target_pairs={{0,2},{1,3},{2,0},{3,1},{4,6},{5,7},{6,4},{7,5},{8,10},{9,11},{10,... | collective-permute-start | bytes 688136 | tf_op jit(solution)/shard_map/ppermute | solution.py:1523
  9.3 12.4 %collective-permute-start.1 = (bf16[128,896]{1,0:T(8,128)(2,1)S(1)}, bf16[128,896]{1,0:T(8,128)(2,1)S(1)}, u32[]{:S(2)}, u32[]{:S(2)}) collective-permute-start(bf16[128,896]{1,0:T(8,128)(2,1)S(1)} %fusion.1.refs_3_), channel_id=1, source_target_pairs={{0,4},{1,5},{2,6},{3,7},{4,0},{5,1},{6,2},{7,3},{8,12},{9,13},{10,... | collective-permute-start | bytes 688136 | tf_op jit(solution)/shard_map/ppermute | solution.py:1523
  11.8 19.7 %collective-permute-start.2 = (bf16[128,896]{1,0:T(8,128)(2,1)S(1)}, bf16[128,896]{1,0:T(8,128)(2,1)S(1)}, u32[]{:S(2)}, u32[]{:S(2)}) collective-permute-start(bf16[128,896]{1,0:T(8,128)(2,1)S(1)} %fusion.1.refs_3_), channel_id=1, source_target_pairs={{0,6},{1,7},{2,4},{3,5},{4,2},{5,3},{6,0},{7,1},{8,14},{9,15},{10,... | collective-permute-start | bytes 688136 | tf_op jit(solution)/shard_map/ppermute | solution.py:1523
  16.0 17.9 %copy-start.11 = (s32[1,12]{1,0:T(1,128)S(1)}, s32[1,12]{1,0:T(1,128)}, u32[]{:S(2)}) copy-start(s32[1,12]{1,0:T(1,128)} %param.16) | copy-start | bytes 148
  16.1 17.9 %copy-start.12 = (s32[1,12]{1,0:T(1,128)S(1)}, s32[1,12]{1,0:T(1,128)}, u32[]{:S(2)}) copy-start(s32[1,12]{1,0:T(1,128)} %param.17) | copy-start | bytes 148
  17.7 13.8 %copy-start.13 = (bf16[128,896]{1,0:T(8,128)(2,1)}, bf16[128,896]{1,0:T(8,128)(2,1)S(1)}, u32[]{:S(2)}) copy-start(bf16[128,896]{1,0:T(8,128)(2,1)S(1)} %collective-permute-done.refs_4_) | copy-start | bytes 688132
  21.8 9.7 %copy-start.14 = (bf16[128,896]{1,0:T(8,128)(2,1)}, bf16[128,896]{1,0:T(8,128)(2,1)S(1)}, u32[]{:S(2)}) copy-start(bf16[128,896]{1,0:T(8,128)(2,1)S(1)} %collective-permute-done.1.refs_5_) | copy-start | bytes 688132
  31.5 0.7 copy-start.15
  32.2 233.4 %all-gather.7.cloned.1.call-start = ((), (), s32[]{:S(2)}) async-start(), calls=%async_computation.7 | async-start | bytes 10616832 | tf_op jit(solution)/shard_map/all_gather | solution.py:1572
  33.0 332.0 %reduce-scatter.4.cloned.1.call-start = ((), (), s32[]{:S(2)}) async-start(), calls=%async_computation.3 | async-start | bytes 10616832 | tf_op jit(solution)/shard_map/reduce_scatter | solution.py:1673
  265.5 289.5 %reduce-scatter.6.cloned.1.call-start = ((), (), s32[]{:S(2)}) async-start(), calls=%async_computation.4 | async-start | bytes 10616832 | tf_op jit(solution)/shard_map/reduce_scatter | solution.py:1673
  335.5 223.6 %reduce-scatter.8.cloned.1.call-start = ((), (), s32[]{:S(2)}) async-start(), calls=%async_computation.5 | async-start | bytes 7077888 | tf_op jit(solution)/shard_map/reduce_scatter | solution.py:1673
  398.6 0.7 copy-start.10
  400.2 158.9 %copy-start = (bf16[1,3,128,1536]{3,2,1,0:T(8,128)(2,1)S(1)}, bf16[1,3,128,1536]{3,2,1,0:T(8,128)(2,1)}, u32[]{:S(2)}) copy-start(bf16[1,3,128,1536]{3,2,1,0:T(8,128)(2,1)} %reduce-scatter.4.cloned.1.call-done) | copy-start | bytes 3538948
  559.1 1.3 copy-start.1
  560.4 1.1 copy-start.2
  561.5 4.1 copy-start.6
  561.5 5.1 copy-start.3
  565.6 2.3 copy-start.7
  565.6 3.0 copy-start.9
Sparse Core Ops, SparseCore 0:
  32.3 89.6 all-gather.4
  124.2 97.5 all-gather.6
  265.7 99.2 reduce-scatter.3
  367.1 101.6 reduce-scatter.5
  471.0 88.1 reduce-scatter.7

commit v6 on v5

--- a/solution.py
+++ b/solution.py
@@ -1568,8 +1568,6 @@
     sizes = [3 * local // 8, 3 * local // 8, local // 4]
     bases = [sum(sizes[:i]) for i in range(len(sizes))]
     pieces = [stacked[i : i + n] for i, n in zip(bases, sizes)]
-    pieces[0], pieces[1], *w_parts = lax.optimization_barrier((pieces[0], pieces[1], *w_parts))
-    gathered = [lax.all_gather(piece, "col", axis=0) for piece in pieces[:-1]]
 
     lengths = seq_lengths[0]
     perm = seq_order[0]
@@ -1601,6 +1599,13 @@
     cos_q, sin_q = cosine * SCORE_SCALE, sine * SCORE_SCALE
     cos_w = jnp.concatenate([cos_q] * 4 + [cosine] * 2 + [ones] * 2, axis=1)
     sin_w = jnp.concatenate([-sin_q, sin_q] * 2 + [-sine, sine] + [zeros] * 2, axis=1)
+
+    tables = (src_col, src_row, own_starts, cos_w, sin_w)
+    count = len(w_parts)
+    ready = lax.optimization_barrier((pieces[0], pieces[1], *w_parts, *tables))
+    pieces[:2], w_parts, tables = ready[:2], ready[2 : 2 + count], ready[2 + count :]
+    src_col, src_row, own_starts, cos_w, sin_w = tables
+    gathered = [lax.all_gather(piece, "col", axis=0) for piece in pieces[:-1]]
 
     gain_a = attn_gain[None, :]
     gain_m = moe_gain[None, :]

time: 580 us -> 578 us (level)
  waiting for transfers between devices: 27 us -> 8.37 us
  Pallas kernels: 504 us -> 516 us
    ppermute x3, waiting for transfers between devices: 15.4 us -> 0.48 us  [swap_over(): return lax.ppermute(value, axis, [(i, i ^ step) for i in range(size)])]
  transfers between devices with their start and end apart: 8 -> 8, of which waited for: 5 -> 3; matrix products, arithmetic and copies ran while one was open for 3% -> 4% of each run, Pallas kernels for 87% -> 89%
where the time goes in v6:
time: 578 us; the launch traced here: 574 us
  Pallas kernels  516 us (89%)
  local copies, waits for them, and re-layouts  24.7 us (4%)
  between operations  14.2 us (2%)
  waiting for transfers between devices  8.37 us (1%)
  other arithmetic  6.82 us (1%)
    pallas_call x1, Pallas kernels, backward(): pl.pallas_call(functools.partial(back_kernel, nblk), out_shape=(shape((to...  155 us
    pallas_call x1, Pallas kernels, front(): pl.pallas_call(functools.partial(front_kernel, pairs), out_shape=(shape((...  141 us
    pallas_call x3, Pallas kernels, experts_reverse(): pl.pallas_call(functools.partial(reverse_kernel, base, first, last, stage...  126 us
    pallas_call x3, Pallas kernels, experts_forward(): pl.pallas_call(functools.partial(forward_kernel, base, first, last, gathe...  88.5 us
  transfers between devices with their start and end apart: 8, of which 3 were waited for; matrix products, arithmetic and copies ran while one was open for 4% of the time, Pallas kernels for 89%

profile of v6, /device:TPU:9, one launch (start us, length us, event | category | flops | bytes accessed | tf_op | source)
XLA Modules:
  0.0 573.8 jit_solution(12480400813123007456)
XLA Ops:
  7.3 0.9 constant_dynamic-slice_fusion.3
  8.3 1.7 fusion.1.refs_3_
  9.9 1.3 collective-permute-start.2
  11.2 1.0 collective-permute-start.1
  12.2 1.2 collective-permute-start
  14.6 1.3 copy.69
  15.9 1.3 copy.70
  18.6 1.6 fusion.6
  21.0 1.1 add_xor_fusion.refs_7_
  22.1 1.9 multiply_sine_fusion
  24.8 2.2 concatenate.25.refs_9_.refs_22_
  27.1 2.4 concatenate.27.refs_10_.refs_23_
  31.6 0.9 slice.32.refs_2_
  32.5 0.9 copy.72.refs_8_.refs_21_
  33.4 141.3 %attention_forward.1 = (bf16[512,1024]{1,0:T(8,128)(2,1)}, bf16[512,1024]{1,0:T(8,128)(2,1)}, bf16[512,2048]{1,0:T(8,128)(2,1)}, bf16[512,1024]{1,0:T(8,128)(2,1...) custom-call(bf16[512,1024]{1,0:T(8,128)(2,1)} %bitcast.49, ...), custom_call_target="tpu_custom_call" | custom-call | flops 20000000000 | bytes 62914560 | tf_op jit(solution)/shard_map/attention_forward/pallas_call | solution.py:349
  174.7 35.7 %experts_forward.3 = (bf16[3,512,1024]{2,1,0:T(8,128)(2,1)}, f32[3,512,512]{2,1,0:T(8,128)}, f32[3,512,512]{2,1,0:T(8,128)}, f32[3,512,128]{2,1,0:T(8,128)}, f32...) custom-call(bf16[4,512,1024]{2,1,0:T(8,128)(2,1)} %get-tuple-element, ...), custom_call_target="tpu_custom_call", output_to_operand_aliasing={{6}: (7, {})} | custom-call | flops 20999999488 | bytes 31457280 | tf_op jit(solution)/shard_map/experts_forward/pallas_call | solution.py:655
  210.4 52.2 %experts_reverse.3 = (bf16[8,3,128,1536]{3,2,1,0:T(8,128)(2,1)}, f32[2048,1024]{1,0:T(8,128)}, f32[2048,128]{1,0:T(8,128)}, bf16[8,2,128,1536]{3,2,1,0:T(8,128)(2,1)}) custom-call(bf16[512,1024]{1,0:T(8,128)(2,1)} %bitcast.52, bf16[2,256,1024]{2,1,0:T(8,128)(2,1)} %get-tuple-element.97.refs_6_.refs_1_.refs_9_, ...), custom_call_target="tpu_custom_call", output_to_operand_aliasing={{3}: (10, {})} | custom-call | flops 27000000512 | bytes 41943040 | tf_op jit(solution)/shard_map/experts_reverse/pallas_call | solution.py:1025
  262.8 30.1 %experts_forward.4 = (bf16[3,512,1024]{2,1,0:T(8,128)(2,1)}, f32[3,512,512]{2,1,0:T(8,128)}, f32[3,512,512]{2,1,0:T(8,128)}, f32[3,512,128]{2,1,0:T(8,128)}, f32...) custom-call(bf16[4,512,1024]{2,1,0:T(8,128)(2,1)} %get-tuple-element, ...), custom_call_target="tpu_custom_call", output_to_operand_aliasing={{4}: (5, {}), {6}: (7, {})} | custom-call | flops 20999999488 | bytes 31457280 | tf_op jit(solution)/shard_map/experts_forward/pallas_call | solution.py:655
  292.9 40.5 %experts_reverse.4 = (bf16[8,3,128,1536]{3,2,1,0:T(8,128)(2,1)}, f32[2048,1024]{1,0:T(8,128)}, f32[2048,128]{1,0:T(8,128)}, bf16[8,2,128,1536]{3,2,1,0:T(8,128)(2,1)}) custom-call(bf16[512,1024]{1,0:T(8,128)(2,1)} %bitcast.53, ...), custom_call_target="tpu_custom_call", output_to_operand_aliasing={{1}: (10, {}), {2}: (11, {}), {3}: (12, {})} | custom-call | flops 27000000512 | bytes 41943040 | tf_op jit(solution)/shard_map/experts_reverse/pallas_call | solution.py:1025
  333.5 22.6 %experts_forward.5 = (bf16[2,512,1024]{2,1,0:T(8,128)(2,1)}, f32[2,512,512]{2,1,0:T(8,128)}, f32[2,512,512]{2,1,0:T(8,128)}, f32[2,512,128]{2,1,0:T(8,128)}, bf1...) custom-call(bf16[4,512,1024]{2,1,0:T(8,128)(2,1)} %get-tuple-element.98.refs_0_, ...), custom_call_target="tpu_custom_call" | custom-call | flops 14000000000 | bytes 31457280 | tf_op jit(solution)/shard_map/experts_forward/pallas_call | solution.py:655
  356.1 4.7 reduce-scatter.4.cloned.1.call-done
  360.8 33.7 %experts_reverse.5 = (bf16[8,2,128,1536]{3,2,1,0:T(8,128)(2,1)}, bf16[4,512,1024]{2,1,0:T(8,128)(2,1)}, f32[8,2048]{1,0:T(8,128)}, bf16[2,256,1024]{2,1,0:T(8,12...) custom-call(bf16[512,1024]{1,0:T(8,128)(2,1)} %bitcast.54, ...), custom_call_target="tpu_custom_call" | custom-call | flops 17999998976 | bytes 41943040 | tf_op jit(solution)/shard_map/experts_reverse/pallas_call | solution.py:1025
  394.5 1.7 slice.29.refs_14_
  396.2 155.5 %attention_backward.1 = (bf16[512,1024]{1,0:T(8,128)(2,1)}, f32[512,1024]{1,0:T(8,128)}, f32[128,512]{1,0:T(8,128)}, f32[128,256]{1,0:T(8,128)}, f32[32,256]{1,0...) custom-call(bf16[4,512,1024]{2,1,0:T(8,128)(2,1)} %get-tuple-element.141.refs_0_, ...), custom_call_target="tpu_custom_call" | custom-call | flops 60000002048 | bytes 104857600 | tf_op jit(solution)/shard_map/attention_backward/pallas_call | solution.py:1457
  551.7 1.3 dynamic-slice_bitcast_fusion
  553.0 1.4 fusion.7
  554.5 2.4 reduce-scatter.8.cloned.1.call-done
  556.8 1.3 copy-done.1
  558.1 1.1 copy-done.2
  559.2 4.1 collect.1
  563.4 1.0 copy.85
  564.4 1.3 copy.86
  (56 shorter events, 7.8 us)
Async XLA Ops:
  7.2 10.1 %copy-start.6 = (bf16[128,8,512]{2,1,0:T(8,128)(2,1)S(1)}, bf16[128,8,512]{2,1,0:T(8,128)(2,1)}, u32[]{:S(2)}) copy-start(bf16[128,8,512]{2,1,0:T(8,128)(2,1)} %param.25) | copy-start | bytes 3145732
  7.2 10.4 %copy-start.7 = (bf16[128,8,512]{2,1,0:T(8,128)(2,1)S(1)}, bf16[128,8,512]{2,1,0:T(8,128)(2,1)}, u32[]{:S(2)}) copy-start(bf16[128,8,512]{2,1,0:T(8,128)(2,1)} %param.26) | copy-start | bytes 3145732
  7.2 167.5 %all-gather.5.cloned.1.call-start = ((), (), s32[]{:S(2)}) async-start(), calls=%async_computation.6 | async-start | bytes 10616832 | tf_op jit(solution)/shard_map/all_gather | solution.py:1608
  9.9 20.2 %collective-permute-start.2 = (bf16[128,896]{1,0:T(8,128)(2,1)}, bf16[128,896]{1,0:T(8,128)(2,1)}, u32[]{:S(2)}, u32[]{:S(2)}) collective-permute-start(bf16[128,896]{1,0:T(8,128)(2,1)} %fusion.1.refs_3_), channel_id=1, source_target_pairs={{0,6},{1,7},{2,4},{3,5},{4,2},{5,3},{6,0},{7,1},{8,14},{9,15},{10,... | collective-permute-start | bytes 688136 | tf_op jit(solution)/shard_map/ppermute | solution.py:1523
  11.2 19.3 %collective-permute-start.1 = (bf16[128,896]{1,0:T(8,128)(2,1)}, bf16[128,896]{1,0:T(8,128)(2,1)}, u32[]{:S(2)}, u32[]{:S(2)}) collective-permute-start(bf16[128,896]{1,0:T(8,128)(2,1)} %fusion.1.refs_3_), channel_id=1, source_target_pairs={{0,4},{1,5},{2,6},{3,7},{4,0},{5,1},{6,2},{7,3},{8,12},{9,13},{10,... | collective-permute-start | bytes 688136 | tf_op jit(solution)/shard_map/ppermute | solution.py:1523
  12.2 18.3 %collective-permute-start = (bf16[128,896]{1,0:T(8,128)(2,1)}, bf16[128,896]{1,0:T(8,128)(2,1)}, u32[]{:S(2)}, u32[]{:S(2)}) collective-permute-start(bf16[128,896]{1,0:T(8,128)(2,1)} %fusion.1.refs_3_), channel_id=1, source_target_pairs={{0,2},{1,3},{2,0},{3,1},{4,6},{5,7},{6,4},{7,5},{8,10},{9,11},{10,... | collective-permute-start | bytes 688136 | tf_op jit(solution)/shard_map/ppermute | solution.py:1523
  14.6 3.4 copy-start.8
  18.6 1.6 copy-start.3
  18.6 2.4 copy-start.4
  30.6 232.2 %all-gather.7.cloned.1.call-start = ((), (), s32[]{:S(2)}) async-start(), calls=%async_computation.7 | async-start | bytes 10616832 | tf_op jit(solution)/shard_map/all_gather | solution.py:1608
  31.3 329.5 %reduce-scatter.4.cloned.1.call-start = ((), (), s32[]{:S(2)}) async-start(), calls=%async_computation.3 | async-start | bytes 10616832 | tf_op jit(solution)/shard_map/reduce_scatter | solution.py:1678
  262.7 291.8 %reduce-scatter.6.cloned.1.call-start = ((), (), s32[]{:S(2)}) async-start(), calls=%async_computation.4 | async-start | bytes 10616832 | tf_op jit(solution)/shard_map/reduce_scatter | solution.py:1678
  333.4 223.4 %reduce-scatter.8.cloned.1.call-start = ((), (), s32[]{:S(2)}) async-start(), calls=%async_computation.5 | async-start | bytes 7077888 | tf_op jit(solution)/shard_map/reduce_scatter | solution.py:1678
  396.2 160.6 %copy-start = (bf16[1,3,128,1536]{3,2,1,0:T(8,128)(2,1)S(1)}, bf16[1,3,128,1536]{3,2,1,0:T(8,128)(2,1)}, u32[]{:S(2)}) copy-start(bf16[1,3,128,1536]{3,2,1,0:T(8,128)(2,1)} %reduce-scatter.4.cloned.1.call-done) | copy-start | bytes 3538948
  556.8 1.3 copy-start.1
  558.1 1.1 copy-start.2
  559.2 4.1 copy-start.9
  559.2 5.1 copy-start.5
  563.4 2.3 copy-start.10
  563.4 3.0 copy-start.11
Sparse Core Ops, SparseCore 0:
  30.7 91.1 all-gather.4
  124.2 99.8 all-gather.6
  262.8 97.9 reduce-scatter.3
  363.0 103.5 reduce-scatter.5
  468.7 88.1 reduce-scatter.7

commit v7 on v6

--- a/solution.py
+++ b/solution.py
@@ -1328,6 +1328,7 @@
         wo[j] = mm_tn(dattn, mixed[:, cols]).astype(BF).reshape(pairs, 2, shard, ow)
         wos.share(j)
     routers.over_row()
+    wos.join()
 
     quad = 4 * hw
     groups = nblk * qw // quad
@@ -1381,14 +1382,14 @@
         gain_a_part = gain_a_part + jnp.sum(dattn_in * x * rx, axis=0, keepdims=True)
         igs.start(b)
         if b == 1:
-            wos.join()
+            wos.middle()
             routers.over_line()
 
     refs[18][...] = jnp.concatenate(
         [gain_a_part, gain_m_part, jnp.zeros((6, width), F32)], axis=0
     )
     gains.share.start()
-    wos.middle()
+    wos.settle()
     for j in range(nblk):
         wq[j] = (
             mm_tn(attn[...], dproj[:, j * qw : (j + 1) * qw])
@@ -1419,7 +1420,6 @@
     summed = own[0].astype(F32) + (own[1].astype(F32) + rest)
     block_out[...] = (input_grad[...] + RESIDUAL_SCALE * summed).astype(BF)
 
-    wos.settle()
     wqs.middle()
     gains.over_line()
     igs.wait((1, 0), (2, 1))

time: 578 us -> 578 us (level)
  no operation moved by 1% of the time
where the time goes in v7:
time: 578 us; the launch traced here: 574 us
  Pallas kernels  514 us (89%)
  local copies, waits for them, and re-layouts  24.7 us (4%)
  between operations  14.2 us (2%)
  waiting for transfers between devices  9.89 us (2%)
  other arithmetic  6.82 us (1%)
    pallas_call x1, Pallas kernels, backward(): pl.pallas_call(functools.partial(back_kernel, nblk), out_shape=(shape((to...  154 us
    pallas_call x1, Pallas kernels, front(): pl.pallas_call(functools.partial(front_kernel, pairs), out_shape=(shape((...  141 us
    pallas_call x3, Pallas kernels, experts_reverse(): pl.pallas_call(functools.partial(reverse_kernel, base, first, last, stage...  126 us
    pallas_call x3, Pallas kernels, experts_forward(): pl.pallas_call(functools.partial(forward_kernel, base, first, last, gathe...  88.5 us
  transfers between devices with their start and end apart: 8, of which 3 were waited for; matrix products, arithmetic and copies ran while one was open for 4% of the time, Pallas kernels for 89%

profile of v7, /device:TPU:9, one launch (start us, length us, event | category | flops | bytes accessed | tf_op | source)
XLA Modules:
  0.0 573.8 jit_solution(12889003595721389992)
XLA Ops:
  7.3 0.9 constant_dynamic-slice_fusion.3
  8.3 1.7 fusion.1.refs_3_
  9.9 1.3 collective-permute-start.2
  11.2 1.0 collective-permute-start.1
  12.2 1.2 collective-permute-start
  14.6 1.3 copy.69
  15.9 1.3 copy.70
  18.6 1.6 fusion.6
  21.0 1.1 add_xor_fusion.refs_7_
  22.1 1.9 multiply_sine_fusion
  24.8 2.2 concatenate.25.refs_9_.refs_22_
  27.1 2.4 concatenate.27.refs_10_.refs_23_
  31.6 0.9 slice.32.refs_2_
  32.5 0.9 copy.72.refs_8_.refs_21_
  33.4 141.3 %attention_forward.1 = (bf16[512,1024]{1,0:T(8,128)(2,1)}, bf16[512,1024]{1,0:T(8,128)(2,1)}, bf16[512,2048]{1,0:T(8,128)(2,1)}, bf16[512,1024]{1,0:T(8,128)(2,1...) custom-call(bf16[512,1024]{1,0:T(8,128)(2,1)} %bitcast.49, ...), custom_call_target="tpu_custom_call" | custom-call | flops 20000000000 | bytes 62914560 | tf_op jit(solution)/shard_map/attention_forward/pallas_call | solution.py:349
  174.7 35.7 %experts_forward.3 = (bf16[3,512,1024]{2,1,0:T(8,128)(2,1)}, f32[3,512,512]{2,1,0:T(8,128)}, f32[3,512,512]{2,1,0:T(8,128)}, f32[3,512,128]{2,1,0:T(8,128)}, f32...) custom-call(bf16[4,512,1024]{2,1,0:T(8,128)(2,1)} %get-tuple-element, ...), custom_call_target="tpu_custom_call", output_to_operand_aliasing={{6}: (7, {})} | custom-call | flops 20999999488 | bytes 31457280 | tf_op jit(solution)/shard_map/experts_forward/pallas_call | solution.py:655
  210.4 52.2 %experts_reverse.3 = (bf16[8,3,128,1536]{3,2,1,0:T(8,128)(2,1)}, f32[2048,1024]{1,0:T(8,128)}, f32[2048,128]{1,0:T(8,128)}, bf16[8,2,128,1536]{3,2,1,0:T(8,128)(2,1)}) custom-call(bf16[512,1024]{1,0:T(8,128)(2,1)} %bitcast.52, bf16[2,256,1024]{2,1,0:T(8,128)(2,1)} %get-tuple-element.97.refs_6_.refs_1_.refs_9_, ...), custom_call_target="tpu_custom_call", output_to_operand_aliasing={{3}: (10, {})} | custom-call | flops 27000000512 | bytes 41943040 | tf_op jit(solution)/shard_map/experts_reverse/pallas_call | solution.py:1025
  262.8 30.1 %experts_forward.4 = (bf16[3,512,1024]{2,1,0:T(8,128)(2,1)}, f32[3,512,512]{2,1,0:T(8,128)}, f32[3,512,512]{2,1,0:T(8,128)}, f32[3,512,128]{2,1,0:T(8,128)}, f32...) custom-call(bf16[4,512,1024]{2,1,0:T(8,128)(2,1)} %get-tuple-element, ...), custom_call_target="tpu_custom_call", output_to_operand_aliasing={{4}: (5, {}), {6}: (7, {})} | custom-call | flops 20999999488 | bytes 31457280 | tf_op jit(solution)/shard_map/experts_forward/pallas_call | solution.py:655
  292.9 40.5 %experts_reverse.4 = (bf16[8,3,128,1536]{3,2,1,0:T(8,128)(2,1)}, f32[2048,1024]{1,0:T(8,128)}, f32[2048,128]{1,0:T(8,128)}, bf16[8,2,128,1536]{3,2,1,0:T(8,128)(2,1)}) custom-call(bf16[512,1024]{1,0:T(8,128)(2,1)} %bitcast.53, ...), custom_call_target="tpu_custom_call", output_to_operand_aliasing={{1}: (10, {}), {2}: (11, {}), {3}: (12, {})} | custom-call | flops 27000000512 | bytes 41943040 | tf_op jit(solution)/shard_map/experts_reverse/pallas_call | solution.py:1025
  333.5 22.6 %experts_forward.5 = (bf16[2,512,1024]{2,1,0:T(8,128)(2,1)}, f32[2,512,512]{2,1,0:T(8,128)}, f32[2,512,512]{2,1,0:T(8,128)}, f32[2,512,128]{2,1,0:T(8,128)}, bf1...) custom-call(bf16[4,512,1024]{2,1,0:T(8,128)(2,1)} %get-tuple-element.98.refs_0_, ...), custom_call_target="tpu_custom_call" | custom-call | flops 14000000000 | bytes 31457280 | tf_op jit(solution)/shard_map/experts_forward/pallas_call | solution.py:655
  356.1 4.7 reduce-scatter.4.cloned.1.call-done
  360.8 33.7 %experts_reverse.5 = (bf16[8,2,128,1536]{3,2,1,0:T(8,128)(2,1)}, bf16[4,512,1024]{2,1,0:T(8,128)(2,1)}, f32[8,2048]{1,0:T(8,128)}, bf16[2,256,1024]{2,1,0:T(8,12...) custom-call(bf16[512,1024]{1,0:T(8,128)(2,1)} %bitcast.54, ...), custom_call_target="tpu_custom_call" | custom-call | flops 17999998976 | bytes 41943040 | tf_op jit(solution)/shard_map/experts_reverse/pallas_call | solution.py:1025
  394.5 1.7 slice.29.refs_14_
  396.2 154.0 %attention_backward.1 = (bf16[512,1024]{1,0:T(8,128)(2,1)}, f32[512,1024]{1,0:T(8,128)}, f32[128,512]{1,0:T(8,128)}, f32[128,256]{1,0:T(8,128)}, f32[32,256]{1,0...) custom-call(bf16[4,512,1024]{2,1,0:T(8,128)(2,1)} %get-tuple-element.141.refs_0_, ...), custom_call_target="tpu_custom_call" | custom-call | flops 60000002048 | bytes 104857600 | tf_op jit(solution)/shard_map/attention_backward/pallas_call | solution.py:1457
  550.2 1.3 dynamic-slice_bitcast_fusion
  551.5 1.4 fusion.7
  553.0 3.9 reduce-scatter.8.cloned.1.call-done
  556.8 1.3 copy-done.1
  558.1 1.1 copy-done.2
  559.2 4.1 collect.1
  563.4 1.0 copy.85
  564.4 1.3 copy.86
  (56 shorter events, 7.8 us)
Async XLA Ops:
  7.2 10.1 %copy-start.6 = (bf16[128,8,512]{2,1,0:T(8,128)(2,1)S(1)}, bf16[128,8,512]{2,1,0:T(8,128)(2,1)}, u32[]{:S(2)}) copy-start(bf16[128,8,512]{2,1,0:T(8,128)(2,1)} %param.25) | copy-start | bytes 3145732
  7.2 10.4 %copy-start.7 = (bf16[128,8,512]{2,1,0:T(8,128)(2,1)S(1)}, bf16[128,8,512]{2,1,0:T(8,128)(2,1)}, u32[]{:S(2)}) copy-start(bf16[128,8,512]{2,1,0:T(8,128)(2,1)} %param.26) | copy-start | bytes 3145732
  7.2 167.5 %all-gather.5.cloned.1.call-start = ((), (), s32[]{:S(2)}) async-start(), calls=%async_computation.6 | async-start | bytes 10616832 | tf_op jit(solution)/shard_map/all_gather | solution.py:1608
  9.9 20.2 %collective-permute-start.2 = (bf16[128,896]{1,0:T(8,128)(2,1)}, bf16[128,896]{1,0:T(8,128)(2,1)}, u32[]{:S(2)}, u32[]{:S(2)}) collective-permute-start(bf16[128,896]{1,0:T(8,128)(2,1)} %fusion.1.refs_3_), channel_id=1, source_target_pairs={{0,6},{1,7},{2,4},{3,5},{4,2},{5,3},{6,0},{7,1},{8,14},{9,15},{10,... | collective-permute-start | bytes 688136 | tf_op jit(solution)/shard_map/ppermute | solution.py:1523
  11.2 19.3 %collective-permute-start.1 = (bf16[128,896]{1,0:T(8,128)(2,1)}, bf16[128,896]{1,0:T(8,128)(2,1)}, u32[]{:S(2)}, u32[]{:S(2)}) collective-permute-start(bf16[128,896]{1,0:T(8,128)(2,1)} %fusion.1.refs_3_), channel_id=1, source_target_pairs={{0,4},{1,5},{2,6},{3,7},{4,0},{5,1},{6,2},{7,3},{8,12},{9,13},{10,... | collective-permute-start | bytes 688136 | tf_op jit(solution)/shard_map/ppermute | solution.py:1523
  12.2 18.3 %collective-permute-start = (bf16[128,896]{1,0:T(8,128)(2,1)}, bf16[128,896]{1,0:T(8,128)(2,1)}, u32[]{:S(2)}, u32[]{:S(2)}) collective-permute-start(bf16[128,896]{1,0:T(8,128)(2,1)} %fusion.1.refs_3_), channel_id=1, source_target_pairs={{0,2},{1,3},{2,0},{3,1},{4,6},{5,7},{6,4},{7,5},{8,10},{9,11},{10,... | collective-permute-start | bytes 688136 | tf_op jit(solution)/shard_map/ppermute | solution.py:1523
  14.6 3.4 copy-start.8
  18.6 1.6 copy-start.3
  18.6 2.4 copy-start.4
  30.6 232.2 %all-gather.7.cloned.1.call-start = ((), (), s32[]{:S(2)}) async-start(), calls=%async_computation.7 | async-start | bytes 10616832 | tf_op jit(solution)/shard_map/all_gather | solution.py:1608
  31.3 329.5 %reduce-scatter.4.cloned.1.call-start = ((), (), s32[]{:S(2)}) async-start(), calls=%async_computation.3 | async-start | bytes 10616832 | tf_op jit(solution)/shard_map/reduce_scatter | solution.py:1678
  262.7 290.2 %reduce-scatter.6.cloned.1.call-start = ((), (), s32[]{:S(2)}) async-start(), calls=%async_computation.4 | async-start | bytes 10616832 | tf_op jit(solution)/shard_map/reduce_scatter | solution.py:1678
  333.4 223.4 %reduce-scatter.8.cloned.1.call-start = ((), (), s32[]{:S(2)}) async-start(), calls=%async_computation.5 | async-start | bytes 7077888 | tf_op jit(solution)/shard_map/reduce_scatter | solution.py:1678
  396.2 160.6 %copy-start = (bf16[1,3,128,1536]{3,2,1,0:T(8,128)(2,1)S(1)}, bf16[1,3,128,1536]{3,2,1,0:T(8,128)(2,1)}, u32[]{:S(2)}) copy-start(bf16[1,3,128,1536]{3,2,1,0:T(8,128)(2,1)} %reduce-scatter.4.cloned.1.call-done) | copy-start | bytes 3538948
  556.8 1.3 copy-start.1
  558.1 1.1 copy-start.2
  559.2 4.1 copy-start.9
  559.2 5.1 copy-start.5
  563.4 2.3 copy-start.10
  563.4 3.0 copy-start.11
Sparse Core Ops, SparseCore 0:
  30.7 91.1 all-gather.4
  124.2 99.8 all-gather.6
  262.8 97.9 reduce-scatter.3
  363.0 103.7 reduce-scatter.5
  468.9 87.9 reduce-scatter.7
